TPU v7x, 256 devices: a whole 4x4x8 slice. The times are simulated.
256 devices in a mesh: tp: 16 (over x_lo, y, core), grp: 16 (over z, x_hi).
Axes of the slice: x: 4 (x_hi: 2, x_lo: 2; x = x_hi * 2 + x_lo), y: 4, z: 8, core: 2. Of those that a mesh axis runs over, the one named last changes fastest.
Arguments:
- resid_in: bfloat16 [1024, 8192], P('grp', 'tp'), may hold values from -6 to 6
- queries: bfloat16 [1024, 4096], P('grp', 'tp')
- kv_cache: bfloat16 [2, 1024, 16, 128, 128], P(None, 'grp', 'tp'), as said below
- new_kv: bfloat16 [2, 1024, 4, 128], P(None, 'grp')
- lengths: int32 [1024], P('grp'), may hold values from 1 to 128, 65536 in all
- out_weight: bfloat16 [4096, 8192], P('tp'), may hold values from -0.09375 to 0.09375
- enc_weight: bfloat16 [8192, 32768], P('tp', 'grp'), may hold values from -0.0625 to 0.0625
- enc_bias: float32 [32768], P('grp'), may hold values from -1 to 0.5
- dec_weight: bfloat16 [32768, 8192], P('grp', 'tp'), may hold values from -0.75 to 0.75
- clamp_ids: int32 [1024, 4], P('grp'), may hold values from 0 to 32767, as said below
- clamp_values: float32 [1024, 4], P('grp'), may hold values from 2 to 8
Outputs:
- resid_out: bfloat16 [1024, 8192], P('grp', 'tp')
- features: bfloat16 [1024, 32768], P('tp', 'grp')
Inputs may be any that keep to these rules, and one draw needn't show every extreme that they name: Entries of kv_cache whose third index divided by 4 agrees are equal. `clamp_ids`: a row's 4 ids are (b + c * 8192) modulo 32768 for c = 0 .. 3.
All inputs are finite; a program needn't handle non-finite values. No bound on the sum of `lengths` on one device may be relied on, other than what follows from the above.
Results may differ from a plain program's by a relative error of at most 0.008.
Values may be sent and summed in bfloat16 or wider, within the bound.
No kernel may reach another device: no remote copies, remote signals or barrier semaphores. Data moves between devices by JAX's collectives and lax.ppermute only.
A program may use at most 128 MiB of HBM per device.

v0:
```python
import jax
import jax.numpy as jnp
from jax import lax
from jax.experimental import pallas as pl
from jax.experimental.pallas import tpu as pltpu
from jax.experimental import pallas as pl
from jax.experimental.pallas import tpu as pltpu
from jax.sharding import PartitionSpec as P

HEAD_DIM = 128
QUARTER = 8192


def tp_moves(move):
    return [(chip * 2 + core, move(chip, core)) for chip in range(8) for core in range(2)]


def grp_moves(move):
    return [(z * 2 + plane, move(z, plane)) for z in range(8) for plane in range(2)]


def swap_core(value):
    return lax.ppermute(value, "tp", tp_moves(lambda chip, core: chip * 2 + 1 - core))


def from_z(value, ahead):
    return lax.ppermute(
        value, "grp", grp_moves(lambda z, plane: (z - ahead) % 8 * 2 + plane)
    )


def chip_at(chip, dx, dy):
    return (chip // 4 + dx) % 2 * 4 + (chip + dy) % 4


def to_chip(value, dx, dy):
    return lax.ppermute(
        value, "tp", tp_moves(lambda chip, core: chip_at(chip, dx, dy) * 2 + core)
    )


def attend(queries, kv_cache, new_kv, lengths, kv_index):
    row_count = queries.shape[0]
    own_heads = queries.shape[1] // HEAD_DIM
    slot_count = kv_cache.shape[3]
    score_scale = HEAD_DIM ** (-0.5)
    query_heads = queries.reshape(row_count, own_heads, HEAD_DIM)
    cache_keys = kv_cache[0, :, 0]
    cache_values = kv_cache[1, :, 0]
    new_key = lax.dynamic_index_in_dim(new_kv[0], kv_index, 1, keepdims=False)
    new_value = lax.dynamic_index_in_dim(new_kv[1], kv_index, 1, keepdims=False)
    scores = (
        jnp.einsum("shd,spd->shp", query_heads, cache_keys, preferred_element_type=jnp.float32)
        * score_scale
    )
    new_score = (
        jnp.einsum("shd,sd->sh", query_heads, new_key, preferred_element_type=jnp.float32)
        * score_scale
    )
    slot_index = jnp.arange(slot_count, dtype=jnp.int32)
    is_valid = (slot_index[None, :] < lengths[:, None])[:, None, :]
    top_score = jnp.maximum(jnp.max(jnp.where(is_valid, scores, -jnp.inf), axis=-1), new_score)
    prob_cache = jnp.where(is_valid, jnp.exp(scores - top_score[..., None]), 0.0)
    new_prob = jnp.exp(new_score - top_score)
    total_weight = jnp.sum(prob_cache, axis=-1) + new_prob
    new_rounded = lax.optimization_barrier(new_prob.astype(jnp.bfloat16)).astype(jnp.float32)
    weighted = jnp.einsum(
        "shp,spd->shd",
        prob_cache.astype(jnp.bfloat16),
        cache_values,
        preferred_element_type=jnp.float32,
    )
    weighted = weighted + new_rounded[..., None] * new_value.astype(jnp.float32)[:, None, :]
    return (
        (weighted / total_weight[..., None])
        .astype(jnp.bfloat16)
        .reshape(row_count, own_heads * HEAD_DIM)
    )


def mm(a, b):
    return jnp.dot(a, b, preferred_element_type=jnp.float32)


def project_kernel(core_ref, mine_ref, other_ref, w_mine_ref, w_other_ref, out_ref):
    out_ref[0] = (mm(mine_ref[...], w_mine_ref[...]) + mm(other_ref[...], w_other_ref[...])).astype(
        out_ref.dtype
    )


def project(core, heads_mine, heads_other, w_mine, w_other, width):
    rows, depth = heads_mine.shape
    columns = lambda i, core_ref: (0, 2 * i + core_ref[0])
    whole = lambda i, core_ref: (0, 0)
    return pl.pallas_call(
        project_kernel,
        grid_spec=pltpu.PrefetchScalarGridSpec(
            num_scalar_prefetch=1,
            grid=(8,),
            in_specs=[
                pl.BlockSpec((rows, depth), whole),
                pl.BlockSpec((rows, depth), whole),
                pl.BlockSpec((depth, width), columns),
                pl.BlockSpec((depth, width), columns),
            ],
            out_specs=pl.BlockSpec((1, rows, width), lambda i, core_ref: (i, 0, 0)),
        ),
        out_shape=jax.ShapeDtypeStruct((8, rows, width), jnp.bfloat16),
        cost_estimate=pl.CostEstimate(
            flops=2 * rows * 2 * depth * 8 * width,
            bytes_accessed=2 * 2 * depth * 8 * width,
            transcendentals=0,
        ),
        name="project",
    )(core.reshape(1), heads_mine, heads_other, w_mine, w_other)


def encode_kernel(slot_ref, *refs):
    block_refs, (want_ref, bias_ref, w_mine_ref, w_other_ref) = refs[:8], refs[8:12]
    out_refs, x_ref = refs[12:21], refs[21]
    step = pl.program_id(0)
    half = w_mine_ref.shape[0]
    tile = w_mine_ref.shape[1]
    rows = out_refs[0].shape[0]

    @pl.when(step == 0)
    def _():
        for k in range(8):
            x_ref[pl.ds(pl.multiple_of(slot_ref[k] * rows, rows), rows), :] = block_refs[k][...]

    part = mm(x_ref[:, :half], w_mine_ref[...]) + mm(x_ref[:, half:], w_other_ref[...])
    part = part.astype(jnp.bfloat16)
    for slot in range(8):
        out_refs[slot][...] = part[slot * rows : (slot + 1) * rows]
    column = lax.broadcasted_iota(jnp.int32, part.shape, 1) + step * tile
    is_hit = column == want_ref[...]
    now = jnp.sum(
        jnp.where(is_hit, part.astype(jnp.float32) + bias_ref[...], 0.0), axis=1, keepdims=True
    )
    total_ref = out_refs[8]

    @pl.when(step == 0)
    def _():
        total_ref[...] = now

    @pl.when(step != 0)
    def _():
        total_ref[...] += now


def encode(block, slot, want, bias, w_mine, w_other):
    rows, depth = block[0].shape
    count = 8 * rows
    span = w_mine.shape[1]
    tile = 256
    return pl.pallas_call(
        encode_kernel,
        grid_spec=pltpu.PrefetchScalarGridSpec(
            num_scalar_prefetch=1,
            grid=(span // tile,),
            in_specs=[pl.BlockSpec((rows, depth), lambda i, slot: (0, 0))] * 8
            + [
                pl.BlockSpec((count, 1), lambda i, slot: (0, 0)),
                pl.BlockSpec((1, tile), lambda i, slot: (0, i)),
                pl.BlockSpec((depth // 2, tile), lambda i, slot: (0, i)),
                pl.BlockSpec((depth // 2, tile), lambda i, slot: (0, i)),
            ],
            out_specs=[pl.BlockSpec((rows, tile), lambda i, slot: (0, i))] * 8
            + [pl.BlockSpec((count, 1), lambda i, slot: (0, 0))],
            scratch_shapes=[pltpu.VMEM((count, depth), jnp.bfloat16)],
        ),
        out_shape=[jax.ShapeDtypeStruct((rows, span), jnp.bfloat16)] * 8
        + [jax.ShapeDtypeStruct((count, 1), jnp.float32)],
        cost_estimate=pl.CostEstimate(
            flops=2 * count * depth * span,
            bytes_accessed=2 * (depth * span + count * (depth + span)),
            transcendentals=0,
        ),
        name="encode",
    )(slot, *block, want, bias, w_mine, w_other)


def per_device(
    resid_in,
    queries,
    kv_cache,
    new_kv,
    lengths,
    out_weight,
    enc_weight,
    enc_bias,
    dec_weight,
    clamp_ids,
    clamp_values,
):
    f32, bf16 = jnp.float32, jnp.bfloat16
    tp_rank, grp_rank = lax.axis_index("tp"), lax.axis_index("grp")
    chip, core = tp_rank // 2, tp_rank % 2
    z, plane = grp_rank // 2, grp_rank % 2
    rows, width = resid_in.shape
    span = enc_weight.shape[1]
    my_quarter, parity = z // 2, z % 2

    ids = lax.all_to_all(
        jnp.broadcast_to(clamp_ids[:, 0].reshape(1, 1, rows), (16, 1, rows)), "grp", 0, 0, tiled=True
    ).reshape(16, rows)
    out_other = swap_core(out_weight)
    enc_other = swap_core(enc_weight)

    heads_mine = attend(queries, kv_cache, new_kv, lengths, tp_rank // 4)
    heads_other = swap_core(heads_mine)
    part = project(core, heads_mine, heads_other, out_weight, out_other, width)
    groups = [[c + 2 * i for i in range(8)] for c in range(2)]
    arrived = lax.all_to_all(part, "tp", 0, 0, axis_index_groups=groups, tiled=True)
    resid_mid = (resid_in.astype(f32) + jnp.sum(arrived.astype(f32), axis=0)).astype(bf16)

    want = ids % QUARTER + my_quarter * QUARTER - grp_rank * span
    ordered = want.reshape(4, 2, 2, rows).transpose(1, 2, 0, 3)
    ordered = jnp.where(parity == 1, ordered, ordered[::-1])
    ordered = jnp.where(plane == 1, ordered, ordered[:, ::-1]).reshape(16 * rows)
    hits = (ordered[:, None] == jnp.arange(span, dtype=jnp.int32)[None, :]).astype(bf16)
    found = mm(hits, dec_weight).astype(bf16)

    mid_other = swap_core(resid_mid)
    both = jnp.concatenate([resid_mid, mid_other], axis=1)
    cross = [
        (t * 16 + z_ * 2 + t % 2, t * 16 + z_ * 2 + 1 - t % 2) for t in range(16) for z_ in range(8)
    ]
    crossed = lax.ppermute(both, ("tp", "grp"), cross)
    near = lax.ppermute(found[: 8 * rows], "grp", grp_moves(lambda z_, s: (z_ ^ 1) * 2 + s))
    block = [None] * 8
    block[0] = jnp.where(core == plane, both, crossed)
    for k, source, step in (
        (1, 0, 1), (7, 0, 7), (2, 0, 2), (6, 0, 6),
        (3, 2, 1), (5, 6, 7), (4, 2, 2),
    ):
        block[k] = from_z(block[source], step)
    found = found[8 * rows :] + near
    near = lax.ppermute(found[: 4 * rows], "grp", grp_moves(lambda z_, s: z_ * 2 + 1 - s))
    found = (found[4 * rows :] + near).reshape(4, rows, width)
    dec_rows = [lax.dynamic_index_in_dim(found, my_quarter, 0, keepdims=False)]
    for k in (1, 2, 3):
        give = lax.dynamic_index_in_dim(found, (my_quarter + k) % 4, 0, keepdims=False)
        dec_rows.append(from_z(give, -2 * k))

    target = [chip_at(chip, s // 4, s % 4) for s in range(8)]
    ahead = (jnp.arange(8, dtype=jnp.int32) + z) % 8
    slot = (ahead // 4 + chip // 4) % 2 * 4 + (ahead - chip) % 4
    mine = lax.dynamic_index_in_dim(want.reshape(8, 2, rows), core, 1, keepdims=False)
    slots = jnp.concatenate([lax.dynamic_index_in_dim(mine, t, 0, keepdims=False) for t in target])
    bias = jnp.where(chip == 0, enc_bias, 0.0).reshape(1, span)
    outs = encode(block, slot, slots.reshape(8 * rows, 1), bias, enc_weight, enc_other)

    now = outs[8].reshape(8, rows)
    by_z = jnp.stack(
        [
            lax.dynamic_index_in_dim(now, chip_at(t, chip // 4, -chip % 4), 0, keepdims=False)
            for t in range(8)
        ]
    )
    sent = jnp.where(
        (jnp.arange(2) == core)[None, :, None], by_z[:, None, :], 0.0
    ).reshape(16, 1, rows)
    held = lax.all_to_all(sent, "grp", 0, 0, tiled=True)
    held = held.reshape(4, 4, rows).sum(axis=1)

    total = outs[0].astype(f32)
    moved = []
    for s in (6, 5, 7, 4, 2, 1, 3):
        moved.append(to_chip(outs[s], s // 4, s % 4))
    every = lax.all_to_all(
        jnp.broadcast_to(held[None], (16, 4, rows)), "tp", 0, 0, tiled=True
    )
    for value in moved:
        total = total + value.astype(f32)
    features = jnp.maximum(total + enc_bias, 0.0).astype(bf16)

    every = every.reshape(16, 4, rows).sum(axis=0)
    every = jnp.maximum(every, 0.0).astype(bf16).astype(f32)
    edit = jnp.zeros((rows, width), f32)
    own_quarter = clamp_ids // QUARTER
    for k in range(4):
        q = (my_quarter - k) % 4
        value = jnp.sum(jnp.where(own_quarter == q, clamp_values, 0.0), axis=1)
        delta = (value - lax.dynamic_index_in_dim(every, q, 0, keepdims=False)).astype(bf16)
        edit = edit + delta.astype(f32)[:, None] * dec_rows[k].astype(f32)
    resid_out = (resid_mid.astype(f32) + edit).astype(bf16)
    return (resid_out, features)


def solution(mesh):
    placed = (
        P("grp", "tp"),
        P("grp", "tp"),
        P(None, "grp", "tp", None, None),
        P(None, "grp", None, None),
        P("grp"),
        P("tp", None),
        P("tp", "grp"),
        P("grp"),
        P("grp", "tp"),
        P("grp", None),
        P("grp", None),
    )
    return jax.shard_map(
        per_device,
        mesh=mesh,
        in_specs=placed,
        out_specs=(P("grp", "tp"), P("tp", "grp")),
        check_vma=False,
    )
```

profile of v0, /device:TPU:8, one launch (start us, length us, event | category | flops | bytes accessed | tf_op | source)
XLA Modules:
  0.0 150.6 jit_solution(12126751590858987576)
XLA Ops:
  2.2 11.0 %all-to-all-start.1 = ((s32[16,1,64]{2,1,0:T(1,128)}), s32[16,1,64]{2,1,0:T(1,128)S(1)}, u32[]{:S(2)}, u32[]{:S(2)}) async-start(s32[16,1,64]{2,1,0:T(1,128)} %broadcast_in_dim.91), calls=%async_computation.1 | async-start | bytes 16384 | tf_op jit(solution)/shard_map/all_to_all | solution.py:204
  16.0 2.9 %select_reduce_fusion = (f32[64,2]{1,0:T(8,128)S(1)}, f32[64,2,128]{2,1,0:T(2,128)S(1)}) fusion(pred[64,128]{1,0:T(8,128)(4,1)S(1)} %iota_compare_fusion.4, bf16[64,2,128]{2,1,0:T(2,128)(2,1)S(1)} %reshape.169, bf16[2,64,1,128,128]{4,3,1,2,0:T(8,128)(2,1)} %bitcast.117), kind=kOutput, calls=%fused_computation.29 | convolution fusion | flops 4243328 | bytes 2204160 | tf_op jit(solution)/shard_map/shd,spd->shp/dot_general | solution.py:53
  19.2 2.3 %fusion.8 = bf16[64,2,128]{2,1,0:T(2,128)(2,1)S(1)} fusion(bf16[2,64,1,128,128]{4,3,1,2,0:T(8,128)(2,1)} %bitcast.118, f32[64,2]{1,0:T(8,128)S(1)} %get-tuple-element.30, f32[64,128]{1,0:T(8,128)S(1)} %bitcast.113, f32[64,2]{1,0:T(8,128)S(1)} %convert_element_type.148, f32[64,2,128]{2,1,0:T(2,128)S(1)} %get-tuple-element.52, ...), kind=kOutput, calls=%fused_computation.11 | convolution fusion | flops 4308992 | bytes 2237952 | tf_op jit(solution)/shard_map/shp,spd->shd/dot_general | solution.py:67
  23.9 6.4 %project.1 = bf16[8,64,512]{2,1,0:T(8,128)(2,1)} custom-call(s32[1]{0:T(128)} %bitcast.core_ref, bf16[64,256]{1,0:T(8,128)(2,1)} %bitcast.105, bf16[64,256]{1,0:T(8,128)(2,1)} %copy-done.5, bf16[256,8192]{1,0:T(8,128)(2,1)} %w_mine_ref.1, bf16[256,8192]{1,0:T(8,128)(2,1)} %collective-permute-done.1.w_other_ref), custom_call_target="tpu_custom_call" | custom-call | flops 268435456 | bytes 4194304 | tf_op jit(solution)/shard_map/project/pallas_call | solution.py:95
  30.3 5.1 %all-to-all-start = ((bf16[8,64,512]{2,1,0:T(8,128)(2,1)}), bf16[8,64,512]{2,1,0:T(8,128)(2,1)S(1)}, u32[]{:S(2)}, u32[]{:S(2)}) async-start(bf16[8,64,512]{2,1,0:T(8,128)(2,1)} %project.1), calls=%async_computation | async-start | bytes 1048576 | tf_op jit(solution)/shard_map/all_to_all | solution.py:214
  35.6 8.1 %all-to-all-done = bf16[8,64,512]{2,1,0:T(8,128)(2,1)S(1)} async-done(((bf16[8,64,512]{2,1,0:T(8,128)(2,1)}), bf16[8,64,512]{2,1,0:T(8,128)(2,1)S(1)}, u32[]{:S(2)}, u32[]{:S(2)}) %all-to-all-start) | async-done | bytes 524320 | tf_op jit(solution)/shard_map/all_to_all | solution.py:214
  45.1 5.9 %collective-permute-start.3 = (bf16[64,1024]{1,0:T(8,128)(2,1)S(1)}, bf16[64,1024]{1,0:T(8,128)(2,1)S(1)}, u32[]{:S(2)}, u32[]{:S(2)}) collective-permute-start(bf16[64,1024]{1,0:T(8,128)(2,1)S(1)} %pad_maximum_fusion), channel_id=1, source_target_pairs={{0,1},{2,3},{4,5},{6,7},{8,9},{10,11},{12,13},{14,15},{17,16},{19,... | collective-permute-start | bytes 393224 | tf_op jit(solution)/shard_map/ppermute | solution.py:229
  51.0 2.4 %fusion.4 = bf16[1024,512]{1,0:T(8,128)(2,1)S(1)} fusion(bf16[2048,512]{1,0:T(8,128)(2,1)S(1)} %copy-done, s32[1024]{0:T(1024)S(1)} %eq.126), kind=kOutput, calls=%fused_computation.7 | convolution fusion | flops 2150105088 | bytes 3149824 | tf_op jit(solution)/shard_map/dot_general | solution.py:82
  56.7 2.7 %collective-permute-start.5 = (bf16[64,1024]{1,0:T(8,128)(2,1)}, bf16[64,1024]{1,0:T(8,128)(2,1)}, u32[]{:S(2)}, u32[]{:S(2)}) collective-permute-start(bf16[64,1024]{1,0:T(8,128)(2,1)} %broadcast_select_fusion.refs_0_), channel_id=1, source_target_pairs={{0,12},{1,13},{2,14},{3,15},{4,0},{5,1},{6,2},{7,3},{8,4},{9,5},{1... | collective-permute-start | bytes 393224 | tf_op jit(solution)/shard_map/ppermute | solution.py:27
  61.8 8.9 %collective-permute-done.12 = bf16[512,512]{1,0:T(8,128)(2,1)S(1)} collective-permute-done((bf16[512,512]{1,0:T(8,128)(2,1)S(1)}, bf16[512,512]{1,0:T(8,128)(2,1)S(1)}, u32[]{:S(2)}, u32[]{:S(2)}) %collective-permute-start.12) | collective-permute-done | bytes 524320 | tf_op jit(solution)/shard_map/ppermute | solution.py:230
  70.7 3.5 %collective-permute-start.4 = (bf16[64,1024]{1,0:T(8,128)(2,1)}, bf16[64,1024]{1,0:T(8,128)(2,1)S(1)}, u32[]{:S(2)}, u32[]{:S(2)}) collective-permute-start(bf16[64,1024]{1,0:T(8,128)(2,1)} %broadcast_select_fusion.refs_0_), channel_id=1, source_target_pairs={{0,14},{1,15},{2,0},{3,1},{4,2},{5,3},{6,4},{7,5},{8,6},{9,7},{10,... | collective-permute-start | bytes 393224 | tf_op jit(solution)/shard_map/ppermute | solution.py:27
  74.3 3.5 %collective-permute-start.6 = (bf16[64,1024]{1,0:T(8,128)(2,1)}, bf16[64,1024]{1,0:T(8,128)(2,1)S(1)}, u32[]{:S(2)}, u32[]{:S(2)}) collective-permute-start(bf16[64,1024]{1,0:T(8,128)(2,1)} %collective-permute-done.5.refs_2_), channel_id=1, source_target_pairs={{0,14},{1,15},{2,0},{3,1},{4,2},{5,3},{6,4},{7,5},{8,6},{9,7},{10,... | collective-permute-start | bytes 393224 | tf_op jit(solution)/shard_map/ppermute | solution.py:27
  77.7 3.0 %collective-permute-start.7 = (bf16[64,1024]{1,0:T(8,128)(2,1)}, bf16[64,1024]{1,0:T(8,128)(2,1)}, u32[]{:S(2)}, u32[]{:S(2)}) collective-permute-start(bf16[64,1024]{1,0:T(8,128)(2,1)} %collective-permute-done.5.refs_2_), channel_id=1, source_target_pairs={{0,12},{1,13},{2,14},{3,15},{4,0},{5,1},{6,2},{7,3},{8,4},{9,5},{1... | collective-permute-start | bytes 393224 | tf_op jit(solution)/shard_map/ppermute | solution.py:27
  83.9 3.3 %collective-permute-done.9.refs_5_ = bf16[64,1024]{1,0:T(8,128)(2,1)} collective-permute-done((bf16[64,1024]{1,0:T(8,128)(2,1)}, bf16[64,1024]{1,0:T(8,128)(2,1)}, u32[]{:S(2)}, u32[]{:S(2)}) %collective-permute-start.9) | collective-permute-done | bytes 131104 | tf_op jit(solution)/shard_map/ppermute | solution.py:27
  87.2 9.5 %encode.1 = (bf16[64,2048]{1,0:T(8,128)(2,1)}, bf16[64,2048]{1,0:T(8,128)(2,1)}, bf16[64,2048]{1,0:T(8,128)(2,1)}, bf16[64,2048]{1,0:T(8,128)(2,1)}, bf16[64,204...) custom-call(s32[8]{0:T(128)} %fusion.29.slot_ref, ...), custom_call_target="tpu_custom_call" | custom-call | flops 2147483648 | bytes 7340032 | tf_op jit(solution)/shard_map/encode/pallas_call | solution.py:156
  98.7 5.1 %all-to-all-start.2 = ((f32[16,1,64]{2,1,0:T(1,128)}), f32[16,1,64]{2,1,0:T(1,128)S(1)}, u32[]{:S(2)}, u32[]{:S(2)}) async-start(f32[16,1,64]{2,1,0:T(1,128)} %broadcast_select_fusion.1), calls=%async_computation.2 | async-start | bytes 16384 | tf_op jit(solution)/shard_map/all_to_all | solution.py:264
  103.8 2.8 %collective-permute-start.17 = (bf16[64,2048]{1,0:T(8,128)(2,1)}, bf16[64,2048]{1,0:T(8,128)(2,1)S(1)}, u32[]{:S(2)}, u32[]{:S(2)}) collective-permute-start(bf16[64,2048]{1,0:T(8,128)(2,1)} %get-tuple-element.13), channel_id=1, source_target_pairs={{0,192},{16,208},{32,224},{48,240},{64,128},{80,144},{96,160},{112... | collective-permute-start | bytes 786440 | tf_op jit(solution)/shard_map/ppermute | solution.py:37
  107.6 6.0 %all-to-all-done.2 = f32[16,1,64]{2,1,0:T(1,128)S(1)} async-done(((f32[16,1,64]{2,1,0:T(1,128)}), f32[16,1,64]{2,1,0:T(1,128)S(1)}, u32[]{:S(2)}, u32[]{:S(2)}) %all-to-all-start.2) | async-done | bytes 4128 | tf_op jit(solution)/shard_map/all_to_all | solution.py:264
  114.4 5.2 %all-to-all-start.3 = ((f32[16,1,256]{2,1,0:T(1,128)}), f32[16,1,256]{2,1,0:T(1,128)S(1)}, u32[]{:S(2)}, u32[]{:S(2)}) async-start(f32[16,1,256]{2,1,0:T(1,128)} %reshape.183), calls=%async_computation.3 | async-start | bytes 32768 | tf_op jit(solution)/shard_map/all_to_all | solution.py:271
  120.9 2.3 %collective-permute-start.15 = (bf16[64,512]{1,0:T(8,128)(2,1)}, bf16[64,512]{1,0:T(8,128)(2,1)S(1)}, u32[]{:S(2)}, u32[]{:S(2)}) collective-permute-start(bf16[64,512]{1,0:T(8,128)(2,1)} %get-tuple-element.26), channel_id=1, source_target_pairs={{0,8},{1,9},{2,10},{3,11},{4,12},{5,13},{6,14},{7,15},{8,0},{9,1},... | collective-permute-start | bytes 196616 | tf_op jit(solution)/shard_map/ppermute | solution.py:27
  126.4 3.2 %collective-permute-done.14 = bf16[64,512]{1,0:T(8,128)(2,1)S(1)} collective-permute-done((bf16[64,512]{1,0:T(8,128)(2,1)}, bf16[64,512]{1,0:T(8,128)(2,1)S(1)}, u32[]{:S(2)}, u32[]{:S(2)}) %collective-permute-start.14) | collective-permute-done | bytes 65568 | tf_op jit(solution)/shard_map/ppermute | solution.py:27
  137.6 2.3 %collective-permute-done.19 = bf16[64,2048]{1,0:T(8,128)(2,1)S(1)} collective-permute-done((bf16[64,2048]{1,0:T(8,128)(2,1)}, bf16[64,2048]{1,0:T(8,128)(2,1)S(1)}, u32[]{:S(2)}, u32[]{:S(2)}) %collective-permute-start.19) | collective-permute-done | bytes 262176 | tf_op jit(solution)/shard_map/ppermute | solution.py:37
  142.0 3.1 %collective-permute-done.21 = bf16[64,2048]{1,0:T(8,128)(2,1)S(1)} collective-permute-done((bf16[64,2048]{1,0:T(8,128)(2,1)}, bf16[64,2048]{1,0:T(8,128)(2,1)S(1)}, u32[]{:S(2)}, u32[]{:S(2)}) %collective-permute-start.21) | collective-permute-done | bytes 262176 | tf_op jit(solution)/shard_map/ppermute | solution.py:37
  145.1 2.9 %collective-permute-done.22 = bf16[64,2048]{1,0:T(8,128)(2,1)S(1)} collective-permute-done((bf16[64,2048]{1,0:T(8,128)(2,1)}, bf16[64,2048]{1,0:T(8,128)(2,1)S(1)}, u32[]{:S(2)}, u32[]{:S(2)}) %collective-permute-start.22) | collective-permute-done | bytes 262176 | tf_op jit(solution)/shard_map/ppermute | solution.py:37
  (116 shorter events, 38.3 us)
Async XLA Ops:
  0.6 22.6 %collective-permute-start.1 = (bf16[256,8192]{1,0:T(8,128)(2,1)}, bf16[256,8192]{1,0:T(8,128)(2,1)}, u32[]{:S(2)}, u32[]{:S(2)}) collective-permute-start(bf16[256,8192]{1,0:T(8,128)(2,1)} %w_mine_ref.1), channel_id=1, source_target_pairs={{0,16},{16,0},{32,48},{48,32},{64,80},{80,64},{96,112},{112,96},{1... | collective-permute-start | bytes 12582920 | tf_op jit(solution)/shard_map/ppermute | solution.py:23
  2.2 28.1 %all-to-all-start.1 = ((s32[16,1,64]{2,1,0:T(1,128)}), s32[16,1,64]{2,1,0:T(1,128)S(1)}, u32[]{:S(2)}, u32[]{:S(2)}) async-start(s32[16,1,64]{2,1,0:T(1,128)} %broadcast_in_dim.91), calls=%async_computation.1 | async-start | bytes 16384 | tf_op jit(solution)/shard_map/all_to_all | solution.py:204
  21.7 56.1 %collective-permute-start.11 = (bf16[512,2048]{1,0:T(8,128)(2,1)}, bf16[512,2048]{1,0:T(8,128)(2,1)}, u32[]{:S(2)}, u32[]{:S(2)}) collective-permute-start(bf16[512,2048]{1,0:T(8,128)(2,1)} %refs_10_.1), channel_id=1, source_target_pairs={{0,16},{16,0},{32,48},{48,32},{64,80},{80,64},{96,112},{112,96},{1... | collective-permute-start | bytes 6291464 | tf_op jit(solution)/shard_map/ppermute | solution.py:23
  30.3 13.4 %all-to-all-start = ((bf16[8,64,512]{2,1,0:T(8,128)(2,1)}), bf16[8,64,512]{2,1,0:T(8,128)(2,1)S(1)}, u32[]{:S(2)}, u32[]{:S(2)}) async-start(bf16[8,64,512]{2,1,0:T(8,128)(2,1)} %project.1), calls=%async_computation | async-start | bytes 1048576 | tf_op jit(solution)/shard_map/all_to_all | solution.py:214
  45.1 10.9 %collective-permute-start.3 = (bf16[64,1024]{1,0:T(8,128)(2,1)S(1)}, bf16[64,1024]{1,0:T(8,128)(2,1)S(1)}, u32[]{:S(2)}, u32[]{:S(2)}) collective-permute-start(bf16[64,1024]{1,0:T(8,128)(2,1)S(1)} %pad_maximum_fusion), channel_id=1, source_target_pairs={{0,1},{2,3},{4,5},{6,7},{8,9},{10,11},{12,13},{14,15},{17,16},{19,... | collective-permute-start | bytes 393224 | tf_op jit(solution)/shard_map/ppermute | solution.py:229
  54.4 16.3 %collective-permute-start.12 = (bf16[512,512]{1,0:T(8,128)(2,1)S(1)}, bf16[512,512]{1,0:T(8,128)(2,1)S(1)}, u32[]{:S(2)}, u32[]{:S(2)}) collective-permute-start(bf16[512,512]{1,0:T(8,128)(2,1)S(1)} %slice.39), channel_id=1, source_target_pairs={{0,2},{1,3},{2,0},{3,1},{4,6},{5,7},{6,4},{7,5},{8,10},{9,11},{10,... | collective-permute-start | bytes 1572872 | tf_op jit(solution)/shard_map/ppermute | solution.py:230
  56.7 17.6 %collective-permute-start.5 = (bf16[64,1024]{1,0:T(8,128)(2,1)}, bf16[64,1024]{1,0:T(8,128)(2,1)}, u32[]{:S(2)}, u32[]{:S(2)}) collective-permute-start(bf16[64,1024]{1,0:T(8,128)(2,1)} %broadcast_select_fusion.refs_0_), channel_id=1, source_target_pairs={{0,12},{1,13},{2,14},{3,15},{4,0},{5,1},{6,2},{7,3},{8,4},{9,5},{1... | collective-permute-start | bytes 393224 | tf_op jit(solution)/shard_map/ppermute | solution.py:27
  59.3 21.4 %collective-permute-start.8 = (bf16[64,1024]{1,0:T(8,128)(2,1)}, bf16[64,1024]{1,0:T(8,128)(2,1)}, u32[]{:S(2)}, u32[]{:S(2)}) collective-permute-start(bf16[64,1024]{1,0:T(8,128)(2,1)} %broadcast_select_fusion.refs_0_), channel_id=1, source_target_pairs={{0,4},{1,5},{2,6},{3,7},{4,8},{5,9},{6,10},{7,11},{8,12},{9,13},{1... | collective-permute-start | bytes 393224 | tf_op jit(solution)/shard_map/ppermute | solution.py:27
  60.6 21.2 %collective-permute-start.10 = (bf16[64,1024]{1,0:T(8,128)(2,1)}, bf16[64,1024]{1,0:T(8,128)(2,1)S(1)}, u32[]{:S(2)}, u32[]{:S(2)}) collective-permute-start(bf16[64,1024]{1,0:T(8,128)(2,1)} %broadcast_select_fusion.refs_0_), channel_id=1, source_target_pairs={{0,2},{1,3},{2,4},{3,5},{4,6},{5,7},{6,8},{7,9},{8,10},{9,11},{10,... | collective-permute-start | bytes 393224 | tf_op jit(solution)/shard_map/ppermute | solution.py:27
  70.7 11.8 %collective-permute-start.4 = (bf16[64,1024]{1,0:T(8,128)(2,1)}, bf16[64,1024]{1,0:T(8,128)(2,1)S(1)}, u32[]{:S(2)}, u32[]{:S(2)}) collective-permute-start(bf16[64,1024]{1,0:T(8,128)(2,1)} %broadcast_select_fusion.refs_0_), channel_id=1, source_target_pairs={{0,14},{1,15},{2,0},{3,1},{4,2},{5,3},{6,4},{7,5},{8,6},{9,7},{10,... | collective-permute-start | bytes 393224 | tf_op jit(solution)/shard_map/ppermute | solution.py:27
  74.3 8.2 %collective-permute-start.6 = (bf16[64,1024]{1,0:T(8,128)(2,1)}, bf16[64,1024]{1,0:T(8,128)(2,1)S(1)}, u32[]{:S(2)}, u32[]{:S(2)}) collective-permute-start(bf16[64,1024]{1,0:T(8,128)(2,1)} %collective-permute-done.5.refs_2_), channel_id=1, source_target_pairs={{0,14},{1,15},{2,0},{3,1},{4,2},{5,3},{6,4},{7,5},{8,6},{9,7},{10,... | collective-permute-start | bytes 393224 | tf_op jit(solution)/shard_map/ppermute | solution.py:27
  81.9 21.9 %collective-permute-start.13 = (bf16[256,512]{1,0:T(8,128)(2,1)S(1)}, bf16[256,512]{1,0:T(8,128)(2,1)S(1)}, u32[]{:S(2)}, u32[]{:S(2)}) collective-permute-start(bf16[256,512]{1,0:T(8,128)(2,1)S(1)} %slice.41), channel_id=1, source_target_pairs={{0,1},{1,0},{2,3},{3,2},{4,5},{5,4},{6,7},{7,6},{8,9},{9,8},{10,11... | collective-permute-start | bytes 786440 | tf_op jit(solution)/shard_map/ppermute | solution.py:239
  98.7 15.0 %all-to-all-start.2 = ((f32[16,1,64]{2,1,0:T(1,128)}), f32[16,1,64]{2,1,0:T(1,128)S(1)}, u32[]{:S(2)}, u32[]{:S(2)}) async-start(f32[16,1,64]{2,1,0:T(1,128)} %broadcast_select_fusion.1), calls=%async_computation.2 | async-start | bytes 16384 | tf_op jit(solution)/shard_map/all_to_all | solution.py:264
  103.8 31.1 %collective-permute-start.17 = (bf16[64,2048]{1,0:T(8,128)(2,1)}, bf16[64,2048]{1,0:T(8,128)(2,1)S(1)}, u32[]{:S(2)}, u32[]{:S(2)}) collective-permute-start(bf16[64,2048]{1,0:T(8,128)(2,1)} %get-tuple-element.13), channel_id=1, source_target_pairs={{0,192},{16,208},{32,224},{48,240},{64,128},{80,144},{96,160},{112... | collective-permute-start | bytes 786440 | tf_op jit(solution)/shard_map/ppermute | solution.py:37
  106.5 29.3 %collective-permute-start.18 = (bf16[64,2048]{1,0:T(8,128)(2,1)}, bf16[64,2048]{1,0:T(8,128)(2,1)S(1)}, u32[]{:S(2)}, u32[]{:S(2)}) collective-permute-start(bf16[64,2048]{1,0:T(8,128)(2,1)} %get-tuple-element.14), channel_id=1, source_target_pairs={{0,160},{16,176},{32,192},{48,208},{64,224},{80,240},{96,128},{112... | collective-permute-start | bytes 786440 | tf_op jit(solution)/shard_map/ppermute | solution.py:37
  114.4 10.7 %all-to-all-start.3 = ((f32[16,1,256]{2,1,0:T(1,128)}), f32[16,1,256]{2,1,0:T(1,128)S(1)}, u32[]{:S(2)}, u32[]{:S(2)}) async-start(f32[16,1,256]{2,1,0:T(1,128)} %reshape.183), calls=%async_computation.3 | async-start | bytes 32768 | tf_op jit(solution)/shard_map/all_to_all | solution.py:271
  120.2 9.4 %collective-permute-start.14 = (bf16[64,512]{1,0:T(8,128)(2,1)}, bf16[64,512]{1,0:T(8,128)(2,1)S(1)}, u32[]{:S(2)}, u32[]{:S(2)}) collective-permute-start(bf16[64,512]{1,0:T(8,128)(2,1)} %get-tuple-element.24), channel_id=1, source_target_pairs={{0,4},{1,5},{2,6},{3,7},{4,8},{5,9},{6,10},{7,11},{8,12},{9,13},{1... | collective-permute-start | bytes 196616 | tf_op jit(solution)/shard_map/ppermute | solution.py:27
  120.9 10.2 %collective-permute-start.15 = (bf16[64,512]{1,0:T(8,128)(2,1)}, bf16[64,512]{1,0:T(8,128)(2,1)S(1)}, u32[]{:S(2)}, u32[]{:S(2)}) collective-permute-start(bf16[64,512]{1,0:T(8,128)(2,1)} %get-tuple-element.26), channel_id=1, source_target_pairs={{0,8},{1,9},{2,10},{3,11},{4,12},{5,13},{6,14},{7,15},{8,0},{9,1},... | collective-permute-start | bytes 196616 | tf_op jit(solution)/shard_map/ppermute | solution.py:27
  123.2 9.6 %collective-permute-start.16 = (bf16[64,512]{1,0:T(8,128)(2,1)S(1)}, bf16[64,512]{1,0:T(8,128)(2,1)S(1)}, u32[]{:S(2)}, u32[]{:S(2)}) collective-permute-start(bf16[64,512]{1,0:T(8,128)(2,1)S(1)} %get-tuple-element.25), channel_id=1, source_target_pairs={{0,12},{1,13},{2,14},{3,15},{4,0},{5,1},{6,2},{7,3},{8,4},{9,5},{1... | collective-permute-start | bytes 196616 | tf_op jit(solution)/shard_map/ppermute | solution.py:27
  129.7 10.3 %collective-permute-start.19 = (bf16[64,2048]{1,0:T(8,128)(2,1)}, bf16[64,2048]{1,0:T(8,128)(2,1)S(1)}, u32[]{:S(2)}, u32[]{:S(2)}) collective-permute-start(bf16[64,2048]{1,0:T(8,128)(2,1)} %get-tuple-element.15), channel_id=1, source_target_pairs={{0,224},{16,240},{32,128},{48,144},{64,160},{80,176},{96,192},{112... | collective-permute-start | bytes 786440 | tf_op jit(solution)/shard_map/ppermute | solution.py:37
  131.1 10.9 %collective-permute-start.20 = (bf16[64,2048]{1,0:T(8,128)(2,1)}, bf16[64,2048]{1,0:T(8,128)(2,1)S(1)}, u32[]{:S(2)}, u32[]{:S(2)}) collective-permute-start(bf16[64,2048]{1,0:T(8,128)(2,1)} %get-tuple-element.16), channel_id=1, source_target_pairs={{0,128},{16,144},{32,160},{48,176},{64,192},{80,208},{96,224},{112... | collective-permute-start | bytes 786440 | tf_op jit(solution)/shard_map/ppermute | solution.py:37
  132.7 12.3 %collective-permute-start.21 = (bf16[64,2048]{1,0:T(8,128)(2,1)}, bf16[64,2048]{1,0:T(8,128)(2,1)S(1)}, u32[]{:S(2)}, u32[]{:S(2)}) collective-permute-start(bf16[64,2048]{1,0:T(8,128)(2,1)} %get-tuple-element.17), channel_id=1, source_target_pairs={{0,64},{16,80},{32,96},{48,112},{64,0},{80,16},{96,32},{112,48},{1... | collective-permute-start | bytes 786440 | tf_op jit(solution)/shard_map/ppermute | solution.py:37
  134.8 13.1 %collective-permute-start.22 = (bf16[64,2048]{1,0:T(8,128)(2,1)}, bf16[64,2048]{1,0:T(8,128)(2,1)S(1)}, u32[]{:S(2)}, u32[]{:S(2)}) collective-permute-start(bf16[64,2048]{1,0:T(8,128)(2,1)} %get-tuple-element.18), channel_id=1, source_target_pairs={{0,32},{16,48},{32,64},{48,80},{64,96},{80,112},{96,0},{112,16},{1... | collective-permute-start | bytes 786440 | tf_op jit(solution)/shard_map/ppermute | solution.py:37
  135.8 13.7 %collective-permute-start.23 = (bf16[64,2048]{1,0:T(8,128)(2,1)}, bf16[64,2048]{1,0:T(8,128)(2,1)S(1)}, u32[]{:S(2)}, u32[]{:S(2)}) collective-permute-start(bf16[64,2048]{1,0:T(8,128)(2,1)} %get-tuple-element.19), channel_id=1, source_target_pairs={{0,96},{16,112},{32,0},{48,16},{64,32},{80,48},{96,64},{112,80},{1... | collective-permute-start | bytes 786440 | tf_op jit(solution)/shard_map/ppermute | solution.py:37
  (16 other events, 156.5 us)
where the time goes:
time: 153 us; the launch traced here: 151 us
  starting transfers between devices  63.4 us (41%)
  waiting for transfers between devices  45.3 us (30%)
  Pallas kernels  15.8 us (10%)
  local copies, waits for them, and re-layouts  8.68 us (6%)
  other arithmetic  8.54 us (6%)
  matrix products  7.75 us (5%)
    ppermute x10, starting transfers between devices, from_z(): lax.ppermute(value, 'grp', grp_moves(lambda z, plane: (z - ahead) % 8 * 2...  18.9 us
    ppermute x7, waiting for transfers between devices, to_chip(): lax.ppermute(value, 'tp', tp_moves(lambda chip, core: chip_at(chip, dx, d...  11.9 us
    all_to_all x1, starting transfers between devices, per_device(): lax.all_to_all(jnp.broadcast_to(clamp_ids[:, 0].reshape(1, 1, rows), (16,...  11 us
    ppermute x7, starting transfers between devices, to_chip(): lax.ppermute(value, 'tp', tp_moves(lambda chip, core: chip_at(chip, dx, d...  9.83 us
    pallas_call x1, Pallas kernels, encode(): pl.pallas_call(encode_kernel, grid_spec=pltpu.PrefetchScalarGridSpec(num_...  9.46 us
    ppermute x10, waiting for transfers between devices, from_z(): lax.ppermute(value, 'grp', grp_moves(lambda z, plane: (z - ahead) % 8 * 2...  9.17 us
    ppermute x1, waiting for transfers between devices, per_device(): lax.ppermute(found[:8 * rows], 'grp', grp_moves(lambda z_, s: (z_ ^ 1) *...  8.92 us
    all_to_all x1, waiting for transfers between devices, per_device(): lax.all_to_all(part, 'tp', 0, 0, axis_index_groups=groups, tiled=True)  8.07 us
  transfers between devices with their start and end apart: 28, of which 13 were waited for; matrix products, arithmetic and copies ran while one was open for 14% of the time, Pallas kernels for 11%

commit v1 on v0

v1 whole, which is shorter than its diff:
```python
import jax
import jax.numpy as jnp
from jax import lax
from jax.experimental import pallas as pl
from jax.experimental.pallas import tpu as pltpu
from jax.experimental import pallas as pl
from jax.experimental.pallas import tpu as pltpu
from jax.sharding import PartitionSpec as P

HEAD_DIM = 128
QUARTER = 8192


def tp_moves(move):
    return [(chip * 2 + core, move(chip, core)) for chip in range(8) for core in range(2)]


def grp_moves(move):
    return [(z * 2 + plane, move(z, plane)) for z in range(8) for plane in range(2)]


def swap_core(value):
    return lax.ppermute(value, "tp", tp_moves(lambda chip, core: chip * 2 + 1 - core))


def from_z(value, ahead):
    return lax.ppermute(
        value, "grp", grp_moves(lambda z, plane: (z - ahead) % 8 * 2 + plane)
    )


def flip_z(value, k):
    return lax.ppermute(value, "grp", grp_moves(lambda z, plane: (z ^ k) * 2 + plane))


def flip_plane(value):
    return lax.ppermute(value, "grp", grp_moves(lambda z, plane: z * 2 + 1 - plane))


def chip_at(chip, dx, dy):
    return (chip // 4 + dx) % 2 * 4 + (chip + dy) % 4


def to_chip(value, dx, dy):
    return lax.ppermute(
        value, "tp", tp_moves(lambda chip, core: chip_at(chip, dx, dy) * 2 + core)
    )


def attend(queries, kv_cache, new_kv, lengths, kv_index):
    row_count = queries.shape[0]
    own_heads = queries.shape[1] // HEAD_DIM
    slot_count = kv_cache.shape[3]
    score_scale = HEAD_DIM ** (-0.5)
    query_heads = queries.reshape(row_count, own_heads, HEAD_DIM)
    cache_keys = kv_cache[0, :, 0]
    cache_values = kv_cache[1, :, 0]
    new_key = lax.dynamic_index_in_dim(new_kv[0], kv_index, 1, keepdims=False)
    new_value = lax.dynamic_index_in_dim(new_kv[1], kv_index, 1, keepdims=False)
    scores = (
        jnp.einsum("shd,spd->shp", query_heads, cache_keys, preferred_element_type=jnp.float32)
        * score_scale
    )
    new_score = (
        jnp.einsum("shd,sd->sh", query_heads, new_key, preferred_element_type=jnp.float32)
        * score_scale
    )
    slot_index = jnp.arange(slot_count, dtype=jnp.int32)
    is_valid = (slot_index[None, :] < lengths[:, None])[:, None, :]
    top_score = jnp.maximum(jnp.max(jnp.where(is_valid, scores, -jnp.inf), axis=-1), new_score)
    prob_cache = jnp.where(is_valid, jnp.exp(scores - top_score[..., None]), 0.0)
    new_prob = jnp.exp(new_score - top_score)
    total_weight = jnp.sum(prob_cache, axis=-1) + new_prob
    new_rounded = lax.optimization_barrier(new_prob.astype(jnp.bfloat16)).astype(jnp.float32)
    weighted = jnp.einsum(
        "shp,spd->shd",
        prob_cache.astype(jnp.bfloat16),
        cache_values,
        preferred_element_type=jnp.float32,
    )
    weighted = weighted + new_rounded[..., None] * new_value.astype(jnp.float32)[:, None, :]
    return (
        (weighted / total_weight[..., None])
        .astype(jnp.bfloat16)
        .reshape(row_count, own_heads * HEAD_DIM)
    )


def mm(a, b):
    return jnp.dot(a, b, preferred_element_type=jnp.float32)


def project_kernel(core_ref, mine_ref, other_ref, *refs):
    weight_refs, out_ref = refs[:4], refs[4]
    for i in range(2):
        out_ref[i] = (
            mm(mine_ref[...], weight_refs[i][...]) + mm(other_ref[...], weight_refs[2 + i][...])
        ).astype(out_ref.dtype)


def project(core, heads_mine, heads_other, w_mine, w_other, width):
    rows, depth = heads_mine.shape
    columns = [pl.BlockSpec((depth, width), lambda i, core_ref, e=e: (0, 4 * i + 2 * e + core_ref[0])) for e in range(2)]
    whole = pl.BlockSpec((rows, depth), lambda i, core_ref: (0, 0))
    return pl.pallas_call(
        project_kernel,
        grid_spec=pltpu.PrefetchScalarGridSpec(
            num_scalar_prefetch=1,
            grid=(4,),
            in_specs=[whole, whole] + columns + columns,
            out_specs=pl.BlockSpec((2, rows, width), lambda i, core_ref: (i, 0, 0)),
        ),
        out_shape=jax.ShapeDtypeStruct((8, rows, width), jnp.bfloat16),
        cost_estimate=pl.CostEstimate(
            flops=2 * rows * 2 * depth * 8 * width,
            bytes_accessed=2 * 2 * depth * 8 * width,
            transcendentals=0,
        ),
        name="project",
    )(core.reshape(1), heads_mine, heads_other, w_mine, w_mine, w_other, w_other)


def select_kernel(dec_want_ref, enc_want_ref, dec_ref, enc_ref, bias_ref, dec_out_ref, enc_out_ref):
    width = dec_ref.shape[1]
    column = lax.broadcasted_iota(jnp.int32, (dec_want_ref.shape[0], dec_ref.shape[0]), 1)
    hits = (column == dec_want_ref[...]).astype(jnp.float32).astype(jnp.bfloat16)
    dec_out_ref[...] = mm(hits, dec_ref[...]).astype(jnp.bfloat16)
    hits = (column == enc_want_ref[...]).astype(jnp.float32).astype(jnp.bfloat16)
    across = lambda a, b: lax.dot_general(
        a, b, (((1,), (1,)), ((), ())), preferred_element_type=jnp.float32
    )
    enc_out_ref[:, :width] = across(hits, enc_ref[...]).astype(jnp.bfloat16)
    enc_out_ref[:, width:] = across(hits, bias_ref[...]).astype(jnp.bfloat16)


def select(dec_want, enc_want, dec_weight, enc_weight, bias_parts):
    count, tile = dec_want.shape[0], 256
    span, width = dec_weight.shape
    lanes = bias_parts.shape[0]
    fixed = lambda shape: pl.BlockSpec(shape, lambda i: (0, 0), pipeline_mode=pl.Buffered(1))
    return pl.pallas_call(
        select_kernel,
        grid=(count // tile,),
        in_specs=[
            pl.BlockSpec((tile, 1), lambda i: (i, 0)),
            pl.BlockSpec((tile, 1), lambda i: (i, 0)),
            fixed((span, width)),
            fixed((width, span)),
            fixed((lanes, span)),
        ],
        out_specs=[
            pl.BlockSpec((tile, width), lambda i: (i, 0)),
            pl.BlockSpec((tile, width + lanes), lambda i: (i, 0)),
        ],
        out_shape=[
            jax.ShapeDtypeStruct((count, width), jnp.bfloat16),
            jax.ShapeDtypeStruct((count, width + lanes), jnp.bfloat16),
        ],
        cost_estimate=pl.CostEstimate(
            flops=2 * count * span * (2 * width + lanes),
            bytes_accessed=2 * span * (2 * width + lanes) + 2 * count * (2 * width + lanes),
            transcendentals=0,
        ),
        name="select",
    )(dec_want, enc_want, dec_weight, enc_weight, bias_parts)


def encode_kernel(slot_ref, *refs):
    block_refs, (w_mine_ref, w_other_ref) = refs[:8], refs[8:10]
    out_refs, x_ref = refs[10:18], refs[18]
    half = w_mine_ref.shape[0]
    rows = out_refs[0].shape[0]

    @pl.when(pl.program_id(0) == 0)
    def _():
        for k in range(8):
            x_ref[pl.ds(pl.multiple_of(slot_ref[k] * rows, rows), rows), :] = block_refs[k][...]

    part = mm(x_ref[:, :half], w_mine_ref[...]) + mm(x_ref[:, half:], w_other_ref[...])
    part = part.astype(jnp.bfloat16)
    for slot in range(8):
        out_refs[slot][...] = part[slot * rows : (slot + 1) * rows]


def encode(block, slot, w_mine, w_other):
    rows, depth = block[0].shape
    count = 8 * rows
    span = w_mine.shape[1]
    tile = 512
    return pl.pallas_call(
        encode_kernel,
        grid_spec=pltpu.PrefetchScalarGridSpec(
            num_scalar_prefetch=1,
            grid=(span // tile,),
            in_specs=[pl.BlockSpec((rows, depth), lambda i, slot: (0, 0))] * 8
            + [pl.BlockSpec((depth // 2, tile), lambda i, slot: (0, i))] * 2,
            out_specs=[pl.BlockSpec((rows, tile), lambda i, slot: (0, i))] * 8,
            scratch_shapes=[pltpu.VMEM((count, depth), jnp.bfloat16)],
        ),
        out_shape=[jax.ShapeDtypeStruct((rows, span), jnp.bfloat16)] * 8,
        cost_estimate=pl.CostEstimate(
            flops=2 * count * depth * span,
            bytes_accessed=2 * (depth * span + count * (depth + span)),
            transcendentals=0,
        ),
        name="encode",
    )(slot, *block, w_mine, w_other)


def per_device(
    resid_in,
    queries,
    kv_cache,
    new_kv,
    lengths,
    out_weight,
    enc_weight,
    enc_bias,
    dec_weight,
    clamp_ids,
    clamp_values,
):
    f32, bf16 = jnp.float32, jnp.bfloat16
    tp_rank, grp_rank = lax.axis_index("tp"), lax.axis_index("grp")
    chip, core = tp_rank // 2, tp_rank % 2
    z, plane = grp_rank // 2, grp_rank % 2
    rows, width = resid_in.shape
    span = enc_weight.shape[1]
    my_quarter = z // 2

    ids = clamp_ids[:, :1].reshape(1, rows)
    ids = jnp.concatenate([ids, flip_plane(ids)])
    for k in (1, 2, 4):
        ids = jnp.concatenate([ids, flip_z(ids, k)])

    out_other = swap_core(out_weight)
    enc_other = swap_core(enc_weight)

    heads_mine = attend(queries, kv_cache, new_kv, lengths, tp_rank // 4)
    heads_other = swap_core(heads_mine)
    part = project(core, heads_mine, heads_other, out_weight, out_other, width)
    groups = [[c + 2 * i for i in range(8)] for c in range(2)]
    arrived = lax.all_to_all(part, "tp", 0, 0, axis_index_groups=groups, tiled=True)
    resid_mid = (resid_in.astype(f32) + jnp.sum(arrived.astype(f32), axis=0)).astype(bf16)

    want = (ids % QUARTER + my_quarter * QUARTER - grp_rank * span).reshape(4, 2, 2, rows)
    want = want[:, ::-1, ::-1]
    dec_want = want.transpose(1, 2, 0, 3).reshape(16 * rows, 1)
    enc_want = want.transpose(2, 1, 0, 3).reshape(16 * rows, 1)
    high = enc_bias.astype(bf16)
    middle = (enc_bias - high.astype(f32)).astype(bf16)
    low = (enc_bias - high.astype(f32) - middle.astype(f32)).astype(bf16)
    bias_parts = jnp.pad(jnp.stack([high, middle, low]), ((0, 125), (0, 0)))
    found_dec, found_enc = select(dec_want, enc_want, dec_weight, enc_weight, bias_parts)
    near_dec = flip_z(found_dec[: 8 * rows], 1)
    near_enc = flip_plane(found_enc[: 8 * rows])

    mid_other = swap_core(resid_mid)
    both = jnp.concatenate([resid_mid, mid_other], axis=1)
    cross = [
        (t * 16 + z_ * 2 + t % 2, t * 16 + z_ * 2 + 1 - t % 2) for t in range(16) for z_ in range(8)
    ]
    crossed = lax.ppermute(both, ("tp", "grp"), cross)
    block = [None] * 8
    block[0] = jnp.where(core == plane, both, crossed)
    for k, source, step in (
        (1, 0, 1), (7, 0, 7), (2, 0, 2), (6, 0, 6),
        (3, 2, 1), (5, 6, 7), (4, 2, 2),
    ):
        block[k] = from_z(block[source], step)
    found_dec = found_dec[8 * rows :] + near_dec
    found_enc = found_enc[8 * rows :] + near_enc
    near_dec = flip_plane(found_dec[: 4 * rows])
    near_enc = flip_z(found_enc[: 4 * rows], 1)
    found = jnp.concatenate([found_dec[4 * rows :] + near_dec, found_enc[4 * rows :] + near_enc], axis=1)
    held = [found[:rows]]
    for k in (1, 2, 3):
        held.append(flip_z(found[k * rows : (k + 1) * rows], 2 * k))

    ahead = (jnp.arange(8, dtype=jnp.int32) + z) % 8
    slot = (ahead // 4 + chip // 4) % 2 * 4 + (ahead - chip) % 4
    outs = encode(block, slot, enc_weight, enc_other)

    total = outs[0].astype(f32)
    moved = []
    for s in (6, 5, 7, 4, 2, 1, 3):
        moved.append(to_chip(outs[s], s // 4, s % 4))

    mid_again = lax.optimization_barrier(resid_mid).astype(f32)
    dots = jnp.stack(
        [
            jnp.sum(mid_again * h[:, width : 2 * width].astype(f32), axis=1)
            for h in held
        ]
    )
    every = lax.all_to_all(
        jnp.broadcast_to(dots[None], (16, 4, rows)), "tp", 0, 0, tiled=True
    )
    for value in moved:
        total = total + value.astype(f32)
    features = jnp.maximum(total + enc_bias, 0.0).astype(bf16)

    every = every.reshape(16, 4, rows).sum(axis=0)
    edit = jnp.zeros((rows, width), f32)
    own_quarter = clamp_ids // QUARTER
    for k in range(4):
        value = jnp.sum(jnp.where(own_quarter == my_quarter ^ k, clamp_values, 0.0), axis=1)
        bias = jnp.sum(held[k][:, 2 * width :].astype(f32), axis=1)
        now = jnp.maximum(every[k] + bias, 0.0).astype(bf16).astype(f32)
        delta = (value - now).astype(bf16).astype(f32)
        edit = edit + delta[:, None] * held[k][:, :width].astype(f32)
    resid_out = (resid_mid.astype(f32) + edit).astype(bf16)
    return (resid_out, features)


def solution(mesh):
    placed = (
        P("grp", "tp"),
        P("grp", "tp"),
        P(None, "grp", "tp", None, None),
        P(None, "grp", None, None),
        P("grp"),
        P("tp", None),
        P("tp", "grp"),
        P("grp"),
        P("grp", "tp"),
        P("grp", None),
        P("grp", None),
    )
    return jax.shard_map(
        per_device,
        mesh=mesh,
        in_specs=placed,
        out_specs=(P("grp", "tp"), P("tp", "grp")),
        check_vma=False,
    )
```

time: 153 us -> 169 us (1.10)
  the two profiles are of different devices: /device:TPU:8 before, /device:TPU:64 now
where the time goes in v1:
time: 169 us; the launch traced here: 168 us
  starting transfers between devices  61.1 us (36%)
  waiting for transfers between devices  58.7 us (35%)
  Pallas kernels  20.6 us (12%)
  local copies, waits for them, and re-layouts  11.4 us (7%)
  other arithmetic  9.69 us (6%)
  matrix products  5.36 us (3%)
    ppermute x8, starting transfers between devices, flip_z(): lax.ppermute(value, 'grp', grp_moves(lambda z, plane: (z ^ k) * 2 + plane))  19.7 us
    ppermute x7, waiting for transfers between devices, to_chip(): lax.ppermute(value, 'tp', tp_moves(lambda chip, core: chip_at(chip, dx, d...  19.4 us
    ppermute x8, waiting for transfers between devices, flip_z(): lax.ppermute(value, 'grp', grp_moves(lambda z, plane: (z ^ k) * 2 + plane))  17.4 us
    ppermute x7, starting transfers between devices, from_z(): lax.ppermute(value, 'grp', grp_moves(lambda z, plane: (z - ahead) % 8 * 2...  12.3 us
    ppermute x7, starting transfers between devices, to_chip(): lax.ppermute(value, 'tp', tp_moves(lambda chip, core: chip_at(chip, dx, d...  10.1 us
    pallas_call x1, Pallas kernels, select(): pl.pallas_call(select_kernel, grid=(count // tile,), in_specs=[pl.BlockSp...  9.58 us
    ppermute x7, waiting for transfers between devices, from_z(): lax.ppermute(value, 'grp', grp_moves(lambda z, plane: (z - ahead) % 8 * 2...  9.35 us
    pallas_call x1, Pallas kernels, encode(): pl.pallas_call(encode_kernel, grid_spec=pltpu.PrefetchScalarGridSpec(num_...  6.51 us
  transfers between devices with their start and end apart: 32, of which 15 were waited for; matrix products, arithmetic and copies ran while one was open for 13% of the time, Pallas kernels for 12%

profile of v1, /device:TPU:64, one launch (start us, length us, event | category | flops | bytes accessed | tf_op | source)
XLA Modules:
  0.0 168.0 jit_solution(102264976586892304)
XLA Ops:
  1.4 3.0 %collective-permute-start.2 = (s32[1,64]{1,0:T(1,128)S(1)}, s32[1,64]{1,0:T(1,128)S(1)}, u32[]{:S(2)}, u32[]{:S(2)}) collective-permute-start(s32[1,64]{1,0:T(1,128)S(1)} %slice_bitcast_fusion.12), channel_id=1, source_target_pairs={{0,1},{1,0},{2,3},{3,2},{4,5},{5,4},{6,7},{7,6},{8,9},{9,8},{10,11... | collective-permute-start | bytes 776 | tf_op jit(solution)/shard_map/ppermute | solution.py:37
  8.8 2.9 %select_reduce_fusion = (f32[64,2]{1,0:T(8,128)S(1)}, f32[64,2,128]{2,1,0:T(2,128)S(1)}) fusion(pred[64,128]{1,0:T(8,128)(4,1)S(1)} %iota_compare_fusion.1, bf16[64,2,128]{2,1,0:T(2,128)(2,1)S(1)} %reshape.118, bf16[2,64,1,128,128]{4,3,1,2,0:T(8,128)(2,1)} %bitcast.104), kind=kOutput, calls=%fused_computation.36 | convolution fusion | flops 4243328 | bytes 2204160 | tf_op jit(solution)/shard_map/shd,spd->shp/dot_general | solution.py:61
  15.6 4.5 %collective-permute-done.4 = s32[4,64]{1,0:T(4,128)S(1)} collective-permute-done((s32[4,64]{1,0:T(4,128)S(1)}, s32[4,64]{1,0:T(4,128)S(1)}, u32[]{:S(2)}, u32[]{:S(2)}) %collective-permute-start.4) | collective-permute-done | bytes 1056 | tf_op jit(solution)/shard_map/ppermute | solution.py:33
  20.0 5.5 %collective-permute-start.5 = (s32[8,64]{1,0:T(8,128)S(1)}, s32[8,64]{1,0:T(8,128)S(1)}, u32[]{:S(2)}, u32[]{:S(2)}) collective-permute-start(s32[8,64]{1,0:T(8,128)S(1)} %pad_add_fusion), channel_id=1, source_target_pairs={{0,8},{1,9},{2,10},{3,11},{4,12},{5,13},{6,14},{7,15},{8,0},{9,1},... | collective-permute-start | bytes 6152 | tf_op jit(solution)/shard_map/ppermute | solution.py:33
  30.3 9.6 %select.56 = (bf16[1024,512]{1,0:T(8,128)(2,1)}, bf16[1024,640]{1,0:T(8,128)(2,1)}) custom-call(s32[1024,1]{1,0:T(8,128)} %reshape.126.dec_want_ref, s32[1024,1]{1,0:T(8,128)} %reshape.127.enc_want_ref, bf16[2048,512]{1,0:T(8,128)(2,1)} %dec_ref.1, bf16[512,2048]{1,0:T(8,128)(2,1)} %refs_8_.1, bf16[128,2048]{1,0:T(8,128)(2,1)} %fusion.10.bias_ref), custom_call_target="tpu_custom_call" | custom-call | flops 4831838208 | bytes 7077888 | tf_op jit(solution)/shard_map/select/pallas_call | solution.py:141
  48.0 3.9 %collective-permute-done.8 = bf16[512,512]{1,0:T(8,128)(2,1)S(1)} collective-permute-done((bf16[512,512]{1,0:T(8,128)(2,1)S(1)}, bf16[512,512]{1,0:T(8,128)(2,1)S(1)}, u32[]{:S(2)}, u32[]{:S(2)}) %collective-permute-start.8) | collective-permute-done | bytes 524320 | tf_op jit(solution)/shard_map/ppermute | solution.py:33
  53.2 4.5 %project.1 = bf16[8,64,512]{2,1,0:T(8,128)(2,1)} custom-call(s32[1]{0:T(128)} %bitcast.core_ref, bf16[64,256]{1,0:T(8,128)(2,1)} %bitcast.93, bf16[64,256]{1,0:T(8,128)(2,1)} %copy-done.4, bf16[256,8192]{1,0:T(8,128)(2,1)} %refs_1_.1, bf16[256,8192]{1,0:T(8,128)(2,1)} %refs_1_.1, bf16[256,8192]{1,0:T(8,128)(2,1)} %collective-permute-done.1.refs_2_.refs_3_, ...), custom_call_target="tpu_custom_call" | custom-call | flops 268435456 | bytes 4194304 | tf_op jit(solution)/shard_map/project/pallas_call | solution.py:105
  57.7 5.4 %all-to-all-start = ((bf16[8,64,512]{2,1,0:T(8,128)(2,1)}), bf16[8,64,512]{2,1,0:T(8,128)(2,1)S(1)}, u32[]{:S(2)}, u32[]{:S(2)}) async-start(bf16[8,64,512]{2,1,0:T(8,128)(2,1)} %project.1), calls=%async_computation | async-start | bytes 1048576 | tf_op jit(solution)/shard_map/all_to_all | solution.py:243
  67.3 4.2 %all-to-all-done = bf16[8,64,512]{2,1,0:T(8,128)(2,1)S(1)} async-done(((bf16[8,64,512]{2,1,0:T(8,128)(2,1)}), bf16[8,64,512]{2,1,0:T(8,128)(2,1)S(1)}, u32[]{:S(2)}, u32[]{:S(2)}) %all-to-all-start) | async-done | bytes 524320 | tf_op jit(solution)/shard_map/all_to_all | solution.py:243
  73.8 4.6 %collective-permute-start.14 = (bf16[64,1024]{1,0:T(8,128)(2,1)S(1)}, bf16[64,1024]{1,0:T(8,128)(2,1)S(1)}, u32[]{:S(2)}, u32[]{:S(2)}) collective-permute-start(bf16[64,1024]{1,0:T(8,128)(2,1)S(1)} %pad_maximum_fusion.3), channel_id=1, source_target_pairs={{0,1},{2,3},{4,5},{6,7},{8,9},{10,11},{12,13},{14,15},{17,16},{19,... | collective-permute-start | bytes 393224 | tf_op jit(solution)/shard_map/ppermute | solution.py:263
  78.5 5.3 %collective-permute-start.11 = (bf16[64,1152]{1,0:T(8,128)(2,1)S(1)}, bf16[64,1152]{1,0:T(8,128)(2,1)S(1)}, u32[]{:S(2)}, u32[]{:S(2)}) collective-permute-start(bf16[64,1152]{1,0:T(8,128)(2,1)S(1)} %get-tuple-element.31), channel_id=1, source_target_pairs={{0,8},{1,9},{2,10},{3,11},{4,12},{5,13},{6,14},{7,15},{8,0},{9,1},... | collective-permute-start | bytes 442376 | tf_op jit(solution)/shard_map/ppermute | solution.py:33
  86.9 2.7 %collective-permute-start.19 = (bf16[64,1024]{1,0:T(8,128)(2,1)S(1)}, bf16[64,1024]{1,0:T(8,128)(2,1)S(1)}, u32[]{:S(2)}, u32[]{:S(2)}) collective-permute-start(bf16[64,1024]{1,0:T(8,128)(2,1)S(1)} %broadcast_select_fusion.refs_0_), channel_id=1, source_target_pairs={{0,4},{1,5},{2,6},{3,7},{4,8},{5,9},{6,10},{7,11},{8,12},{9,13},{1... | collective-permute-start | bytes 393224 | tf_op jit(solution)/shard_map/ppermute | solution.py:27
  90.3 5.8 %collective-permute-done.10 = bf16[64,1152]{1,0:T(8,128)(2,1)S(1)} collective-permute-done((bf16[64,1152]{1,0:T(8,128)(2,1)S(1)}, bf16[64,1152]{1,0:T(8,128)(2,1)S(1)}, u32[]{:S(2)}, u32[]{:S(2)}) %collective-permute-start.10) | collective-permute-done | bytes 147488 | tf_op jit(solution)/shard_map/ppermute | solution.py:33
  96.1 3.3 %collective-permute-start.21 = (bf16[64,1024]{1,0:T(8,128)(2,1)S(1)}, bf16[64,1024]{1,0:T(8,128)(2,1)S(1)}, u32[]{:S(2)}, u32[]{:S(2)}) collective-permute-start(bf16[64,1024]{1,0:T(8,128)(2,1)S(1)} %broadcast_select_fusion.refs_0_), channel_id=1, source_target_pairs={{0,2},{1,3},{2,4},{3,5},{4,6},{5,7},{6,8},{7,9},{8,10},{9,11},{10,... | collective-permute-start | bytes 393224 | tf_op jit(solution)/shard_map/ppermute | solution.py:27
  99.4 2.8 %collective-permute-start.18 = (bf16[64,1024]{1,0:T(8,128)(2,1)S(1)}, bf16[64,1024]{1,0:T(8,128)(2,1)S(1)}, u32[]{:S(2)}, u32[]{:S(2)}) collective-permute-start(bf16[64,1024]{1,0:T(8,128)(2,1)S(1)} %collective-permute-done.16.refs_2_), channel_id=1, source_target_pairs={{0,12},{1,13},{2,14},{3,15},{4,0},{5,1},{6,2},{7,3},{8,4},{9,5},{1... | collective-permute-start | bytes 393224 | tf_op jit(solution)/shard_map/ppermute | solution.py:27
  105.9 9.3 %collective-permute-done.18.refs_4_ = bf16[64,1024]{1,0:T(8,128)(2,1)S(1)} collective-permute-done((bf16[64,1024]{1,0:T(8,128)(2,1)S(1)}, bf16[64,1024]{1,0:T(8,128)(2,1)S(1)}, u32[]{:S(2)}, u32[]{:S(2)}) %collective-permute-start.18) | collective-permute-done | bytes 131104 | tf_op jit(solution)/shard_map/ppermute | solution.py:27
  116.5 6.5 %encode.1 = (bf16[64,2048]{1,0:T(8,128)(2,1)}, bf16[64,2048]{1,0:T(8,128)(2,1)}, bf16[64,2048]{1,0:T(8,128)(2,1)}, bf16[64,2048]{1,0:T(8,128)(2,1)}, bf16[64,204...) custom-call(s32[8]{0:T(128)} %fusion.26.slot_ref, ...), custom_call_target="tpu_custom_call" | custom-call | flops 2147483648 | bytes 7340032 | tf_op jit(solution)/shard_map/encode/pallas_call | solution.py:190
  126.0 4.4 %all-to-all-start.1 = ((f32[16,1,256]{2,1,0:T(1,128)}), f32[16,1,256]{2,1,0:T(1,128)S(1)}, u32[]{:S(2)}, u32[]{:S(2)}) async-start(f32[16,1,256]{2,1,0:T(1,128)} %reshape.128), calls=%async_computation.1 | async-start | bytes 32768 | tf_op jit(solution)/shard_map/all_to_all | solution.py:296
  130.6 6.0 %all-to-all-done.1 = f32[16,1,256]{2,1,0:T(1,128)S(1)} async-done(((f32[16,1,256]{2,1,0:T(1,128)}), f32[16,1,256]{2,1,0:T(1,128)S(1)}, u32[]{:S(2)}, u32[]{:S(2)}) %all-to-all-start.1) | async-done | bytes 16416 | tf_op jit(solution)/shard_map/all_to_all | solution.py:296
  139.7 2.9 %collective-permute-start.25 = (bf16[64,2048]{1,0:T(8,128)(2,1)}, bf16[64,2048]{1,0:T(8,128)(2,1)S(1)}, u32[]{:S(2)}, u32[]{:S(2)}) collective-permute-start(bf16[64,2048]{1,0:T(8,128)(2,1)} %get-tuple-element.17), channel_id=1, source_target_pairs={{0,224},{16,240},{32,128},{48,144},{64,160},{80,176},{96,192},{112... | collective-permute-start | bytes 786440 | tf_op jit(solution)/shard_map/ppermute | solution.py:45
  142.7 3.2 %collective-permute-start.23 = (bf16[64,2048]{1,0:T(8,128)(2,1)}, bf16[64,2048]{1,0:T(8,128)(2,1)S(1)}, u32[]{:S(2)}, u32[]{:S(2)}) collective-permute-start(bf16[64,2048]{1,0:T(8,128)(2,1)} %get-tuple-element.15), channel_id=1, source_target_pairs={{0,192},{16,208},{32,224},{48,240},{64,128},{80,144},{96,160},{112... | collective-permute-start | bytes 786440 | tf_op jit(solution)/shard_map/ppermute | solution.py:45
  148.5 5.9 %collective-permute-done.25 = bf16[64,2048]{1,0:T(8,128)(2,1)S(1)} collective-permute-done((bf16[64,2048]{1,0:T(8,128)(2,1)}, bf16[64,2048]{1,0:T(8,128)(2,1)S(1)}, u32[]{:S(2)}, u32[]{:S(2)}) %collective-permute-start.25) | collective-permute-done | bytes 262176 | tf_op jit(solution)/shard_map/ppermute | solution.py:45
  154.5 6.8 %collective-permute-done.24 = bf16[64,2048]{1,0:T(8,128)(2,1)S(1)} collective-permute-done((bf16[64,2048]{1,0:T(8,128)(2,1)}, bf16[64,2048]{1,0:T(8,128)(2,1)S(1)}, u32[]{:S(2)}, u32[]{:S(2)}) %collective-permute-start.24) | collective-permute-done | bytes 262176 | tf_op jit(solution)/shard_map/ppermute | solution.py:45
  161.3 4.8 %collective-permute-done.23 = bf16[64,2048]{1,0:T(8,128)(2,1)S(1)} collective-permute-done((bf16[64,2048]{1,0:T(8,128)(2,1)}, bf16[64,2048]{1,0:T(8,128)(2,1)S(1)}, u32[]{:S(2)}, u32[]{:S(2)}) %collective-permute-start.23) | collective-permute-done | bytes 262176 | tf_op jit(solution)/shard_map/ppermute | solution.py:45
  (131 shorter events, 49.1 us)
Async XLA Ops:
  0.6 52.0 %collective-permute-start.1 = (bf16[256,8192]{1,0:T(8,128)(2,1)}, bf16[256,8192]{1,0:T(8,128)(2,1)}, u32[]{:S(2)}, u32[]{:S(2)}) collective-permute-start(bf16[256,8192]{1,0:T(8,128)(2,1)} %refs_1_.1), channel_id=1, source_target_pairs={{0,16},{16,0},{32,48},{48,32},{64,80},{80,64},{96,112},{112,96},{1... | collective-permute-start | bytes 12582920 | tf_op jit(solution)/shard_map/ppermute | solution.py:23
  1.4 10.3 %collective-permute-start.2 = (s32[1,64]{1,0:T(1,128)S(1)}, s32[1,64]{1,0:T(1,128)S(1)}, u32[]{:S(2)}, u32[]{:S(2)}) collective-permute-start(s32[1,64]{1,0:T(1,128)S(1)} %slice_bitcast_fusion.12), channel_id=1, source_target_pairs={{0,1},{1,0},{2,3},{3,2},{4,5},{5,4},{6,7},{7,6},{8,9},{9,8},{10,11... | collective-permute-start | bytes 776 | tf_op jit(solution)/shard_map/ppermute | solution.py:37
  4.4 94.9 %collective-permute-start.22 = (bf16[512,2048]{1,0:T(8,128)(2,1)}, bf16[512,2048]{1,0:T(8,128)(2,1)}, u32[]{:S(2)}, u32[]{:S(2)}) collective-permute-start(bf16[512,2048]{1,0:T(8,128)(2,1)} %refs_8_.1), channel_id=1, source_target_pairs={{0,16},{16,0},{32,48},{48,32},{64,80},{80,64},{96,112},{112,96},{1... | collective-permute-start | bytes 6291464 | tf_op jit(solution)/shard_map/ppermute | solution.py:23
  41.0 10.9 %collective-permute-start.8 = (bf16[512,512]{1,0:T(8,128)(2,1)S(1)}, bf16[512,512]{1,0:T(8,128)(2,1)S(1)}, u32[]{:S(2)}, u32[]{:S(2)}) collective-permute-start(bf16[512,512]{1,0:T(8,128)(2,1)S(1)} %slice.114), channel_id=1, source_target_pairs={{0,2},{1,3},{2,0},{3,1},{4,6},{5,7},{6,4},{7,5},{8,10},{9,11},{10,... | collective-permute-start | bytes 1572872 | tf_op jit(solution)/shard_map/ppermute | solution.py:33
  45.0 18.1 %collective-permute-start.6 = (bf16[512,640]{1,0:T(8,128)(2,1)}, bf16[512,640]{1,0:T(8,128)(2,1)}, u32[]{:S(2)}, u32[]{:S(2)}) collective-permute-start(bf16[512,640]{1,0:T(8,128)(2,1)} %slice.109), channel_id=1, source_target_pairs={{0,1},{1,0},{2,3},{3,2},{4,5},{5,4},{6,7},{7,6},{8,9},{9,8},{10,11... | collective-permute-start | bytes 1966088 | tf_op jit(solution)/shard_map/ppermute | solution.py:37
  52.0 15.3 %collective-permute-start.9 = (bf16[256,512]{1,0:T(8,128)(2,1)S(1)}, bf16[256,512]{1,0:T(8,128)(2,1)S(1)}, u32[]{:S(2)}, u32[]{:S(2)}) collective-permute-start(bf16[256,512]{1,0:T(8,128)(2,1)S(1)} %slice.141), channel_id=1, source_target_pairs={{0,1},{1,0},{2,3},{3,2},{4,5},{5,4},{6,7},{7,6},{8,9},{9,8},{10,11... | collective-permute-start | bytes 786440 | tf_op jit(solution)/shard_map/ppermute | solution.py:37
  57.7 13.9 %all-to-all-start = ((bf16[8,64,512]{2,1,0:T(8,128)(2,1)}), bf16[8,64,512]{2,1,0:T(8,128)(2,1)S(1)}, u32[]{:S(2)}, u32[]{:S(2)}) async-start(bf16[8,64,512]{2,1,0:T(8,128)(2,1)} %project.1), calls=%async_computation | async-start | bytes 1048576 | tf_op jit(solution)/shard_map/all_to_all | solution.py:243
  73.8 11.4 %collective-permute-start.14 = (bf16[64,1024]{1,0:T(8,128)(2,1)S(1)}, bf16[64,1024]{1,0:T(8,128)(2,1)S(1)}, u32[]{:S(2)}, u32[]{:S(2)}) collective-permute-start(bf16[64,1024]{1,0:T(8,128)(2,1)S(1)} %pad_maximum_fusion.3), channel_id=1, source_target_pairs={{0,1},{2,3},{4,5},{6,7},{8,9},{10,11},{12,13},{14,15},{17,16},{19,... | collective-permute-start | bytes 393224 | tf_op jit(solution)/shard_map/ppermute | solution.py:263
  78.5 11.7 %collective-permute-start.11 = (bf16[64,1152]{1,0:T(8,128)(2,1)S(1)}, bf16[64,1152]{1,0:T(8,128)(2,1)S(1)}, u32[]{:S(2)}, u32[]{:S(2)}) collective-permute-start(bf16[64,1152]{1,0:T(8,128)(2,1)S(1)} %get-tuple-element.31), channel_id=1, source_target_pairs={{0,8},{1,9},{2,10},{3,11},{4,12},{5,13},{6,14},{7,15},{8,0},{9,1},... | collective-permute-start | bytes 442376 | tf_op jit(solution)/shard_map/ppermute | solution.py:33
  83.8 12.2 %collective-permute-start.10 = (bf16[64,1152]{1,0:T(8,128)(2,1)S(1)}, bf16[64,1152]{1,0:T(8,128)(2,1)S(1)}, u32[]{:S(2)}, u32[]{:S(2)}) collective-permute-start(bf16[64,1152]{1,0:T(8,128)(2,1)S(1)} %get-tuple-element.30), channel_id=1, source_target_pairs={{0,4},{1,5},{2,6},{3,7},{4,0},{5,1},{6,2},{7,3},{8,12},{9,13},{10,... | collective-permute-start | bytes 442376 | tf_op jit(solution)/shard_map/ppermute | solution.py:33
  85.3 14.0 %collective-permute-start.16 = (bf16[64,1024]{1,0:T(8,128)(2,1)S(1)}, bf16[64,1024]{1,0:T(8,128)(2,1)S(1)}, u32[]{:S(2)}, u32[]{:S(2)}) collective-permute-start(bf16[64,1024]{1,0:T(8,128)(2,1)S(1)} %broadcast_select_fusion.refs_0_), channel_id=1, source_target_pairs={{0,12},{1,13},{2,14},{3,15},{4,0},{5,1},{6,2},{7,3},{8,4},{9,5},{1... | collective-permute-start | bytes 393224 | tf_op jit(solution)/shard_map/ppermute | solution.py:27
  86.9 15.3 %collective-permute-start.19 = (bf16[64,1024]{1,0:T(8,128)(2,1)S(1)}, bf16[64,1024]{1,0:T(8,128)(2,1)S(1)}, u32[]{:S(2)}, u32[]{:S(2)}) collective-permute-start(bf16[64,1024]{1,0:T(8,128)(2,1)S(1)} %broadcast_select_fusion.refs_0_), channel_id=1, source_target_pairs={{0,4},{1,5},{2,6},{3,7},{4,8},{5,9},{6,10},{7,11},{8,12},{9,13},{1... | collective-permute-start | bytes 393224 | tf_op jit(solution)/shard_map/ppermute | solution.py:27
  90.2 14.1 %collective-permute-start.15 = (bf16[64,1024]{1,0:T(8,128)(2,1)S(1)}, bf16[64,1024]{1,0:T(8,128)(2,1)S(1)}, u32[]{:S(2)}, u32[]{:S(2)}) collective-permute-start(bf16[64,1024]{1,0:T(8,128)(2,1)S(1)} %broadcast_select_fusion.refs_0_), channel_id=1, source_target_pairs={{0,14},{1,15},{2,0},{3,1},{4,2},{5,3},{6,4},{7,5},{8,6},{9,7},{10,... | collective-permute-start | bytes 393224 | tf_op jit(solution)/shard_map/ppermute | solution.py:27
  96.1 9.8 %collective-permute-start.21 = (bf16[64,1024]{1,0:T(8,128)(2,1)S(1)}, bf16[64,1024]{1,0:T(8,128)(2,1)S(1)}, u32[]{:S(2)}, u32[]{:S(2)}) collective-permute-start(bf16[64,1024]{1,0:T(8,128)(2,1)S(1)} %broadcast_select_fusion.refs_0_), channel_id=1, source_target_pairs={{0,2},{1,3},{2,4},{3,5},{4,6},{5,7},{6,8},{7,9},{8,10},{9,11},{10,... | collective-permute-start | bytes 393224 | tf_op jit(solution)/shard_map/ppermute | solution.py:27
  99.4 15.9 %collective-permute-start.18 = (bf16[64,1024]{1,0:T(8,128)(2,1)S(1)}, bf16[64,1024]{1,0:T(8,128)(2,1)S(1)}, u32[]{:S(2)}, u32[]{:S(2)}) collective-permute-start(bf16[64,1024]{1,0:T(8,128)(2,1)S(1)} %collective-permute-done.16.refs_2_), channel_id=1, source_target_pairs={{0,12},{1,13},{2,14},{3,15},{4,0},{5,1},{6,2},{7,3},{8,4},{9,5},{1... | collective-permute-start | bytes 393224 | tf_op jit(solution)/shard_map/ppermute | solution.py:27
  102.1 13.1 %collective-permute-start.20 = (bf16[64,1024]{1,0:T(8,128)(2,1)S(1)}, bf16[64,1024]{1,0:T(8,128)(2,1)S(1)}, u32[]{:S(2)}, u32[]{:S(2)}) collective-permute-start(bf16[64,1024]{1,0:T(8,128)(2,1)S(1)} %collective-permute-done.19.refs_6_), channel_id=1, source_target_pairs={{0,2},{1,3},{2,4},{3,5},{4,6},{5,7},{6,8},{7,9},{8,10},{9,11},{10,... | collective-permute-start | bytes 393224 | tf_op jit(solution)/shard_map/ppermute | solution.py:27
  104.3 20.8 %collective-permute-start.12 = (bf16[64,1152]{1,0:T(8,128)(2,1)S(1)}, bf16[64,1152]{1,0:T(8,128)(2,1)S(1)}, u32[]{:S(2)}, u32[]{:S(2)}) collective-permute-start(bf16[64,1152]{1,0:T(8,128)(2,1)S(1)} %get-tuple-element.32), channel_id=1, source_target_pairs={{0,12},{1,13},{2,14},{3,15},{4,8},{5,9},{6,10},{7,11},{8,4},{9,5},... | collective-permute-start | bytes 442376 | tf_op jit(solution)/shard_map/ppermute | solution.py:33
  123.0 19.6 %collective-permute-start.29 = (bf16[64,2048]{1,0:T(8,128)(2,1)}, bf16[64,2048]{1,0:T(8,128)(2,1)S(1)}, u32[]{:S(2)}, u32[]{:S(2)}) collective-permute-start(bf16[64,2048]{1,0:T(8,128)(2,1)} %get-tuple-element.21), channel_id=1, source_target_pairs={{0,96},{16,112},{32,0},{48,16},{64,32},{80,48},{96,64},{112,80},{1... | collective-permute-start | bytes 786440 | tf_op jit(solution)/shard_map/ppermute | solution.py:45
  124.2 18.4 %collective-permute-start.28 = (bf16[64,2048]{1,0:T(8,128)(2,1)}, bf16[64,2048]{1,0:T(8,128)(2,1)S(1)}, u32[]{:S(2)}, u32[]{:S(2)}) collective-permute-start(bf16[64,2048]{1,0:T(8,128)(2,1)} %get-tuple-element.20), channel_id=1, source_target_pairs={{0,32},{16,48},{32,64},{48,80},{64,96},{80,112},{96,0},{112,16},{1... | collective-permute-start | bytes 786440 | tf_op jit(solution)/shard_map/ppermute | solution.py:45
  126.0 10.5 %all-to-all-start.1 = ((f32[16,1,256]{2,1,0:T(1,128)}), f32[16,1,256]{2,1,0:T(1,128)S(1)}, u32[]{:S(2)}, u32[]{:S(2)}) async-start(f32[16,1,256]{2,1,0:T(1,128)} %reshape.128), calls=%async_computation.1 | async-start | bytes 32768 | tf_op jit(solution)/shard_map/all_to_all | solution.py:296
  137.9 10.1 %collective-permute-start.27 = (bf16[64,2048]{1,0:T(8,128)(2,1)}, bf16[64,2048]{1,0:T(8,128)(2,1)S(1)}, u32[]{:S(2)}, u32[]{:S(2)}) collective-permute-start(bf16[64,2048]{1,0:T(8,128)(2,1)} %get-tuple-element.19), channel_id=1, source_target_pairs={{0,64},{16,80},{32,96},{48,112},{64,0},{80,16},{96,32},{112,48},{1... | collective-permute-start | bytes 786440 | tf_op jit(solution)/shard_map/ppermute | solution.py:45
  139.7 14.7 %collective-permute-start.25 = (bf16[64,2048]{1,0:T(8,128)(2,1)}, bf16[64,2048]{1,0:T(8,128)(2,1)S(1)}, u32[]{:S(2)}, u32[]{:S(2)}) collective-permute-start(bf16[64,2048]{1,0:T(8,128)(2,1)} %get-tuple-element.17), channel_id=1, source_target_pairs={{0,224},{16,240},{32,128},{48,144},{64,160},{80,176},{96,192},{112... | collective-permute-start | bytes 786440 | tf_op jit(solution)/shard_map/ppermute | solution.py:45
  142.7 18.6 %collective-permute-start.24 = (bf16[64,2048]{1,0:T(8,128)(2,1)}, bf16[64,2048]{1,0:T(8,128)(2,1)S(1)}, u32[]{:S(2)}, u32[]{:S(2)}) collective-permute-start(bf16[64,2048]{1,0:T(8,128)(2,1)} %get-tuple-element.16), channel_id=1, source_target_pairs={{0,160},{16,176},{32,192},{48,208},{64,224},{80,240},{96,128},{112... | collective-permute-start | bytes 786440 | tf_op jit(solution)/shard_map/ppermute | solution.py:45
  142.7 23.4 %collective-permute-start.23 = (bf16[64,2048]{1,0:T(8,128)(2,1)}, bf16[64,2048]{1,0:T(8,128)(2,1)S(1)}, u32[]{:S(2)}, u32[]{:S(2)}) collective-permute-start(bf16[64,2048]{1,0:T(8,128)(2,1)} %get-tuple-element.15), channel_id=1, source_target_pairs={{0,192},{16,208},{32,224},{48,240},{64,128},{80,144},{96,160},{112... | collective-permute-start | bytes 786440 | tf_op jit(solution)/shard_map/ppermute | solution.py:45
  (23 other events, 226.0 us)

commit v2 on v1

--- a/solution.py
+++ b/solution.py
@@ -120,61 +120,88 @@
     )(core.reshape(1), heads_mine, heads_other, w_mine, w_mine, w_other, w_other)
 
 
-def select_kernel(dec_want_ref, enc_want_ref, dec_ref, enc_ref, bias_ref, dec_out_ref, enc_out_ref):
-    width = dec_ref.shape[1]
-    column = lax.broadcasted_iota(jnp.int32, (dec_want_ref.shape[0], dec_ref.shape[0]), 1)
-    hits = (column == dec_want_ref[...]).astype(jnp.float32).astype(jnp.bfloat16)
-    dec_out_ref[...] = mm(hits, dec_ref[...]).astype(jnp.bfloat16)
-    hits = (column == enc_want_ref[...]).astype(jnp.float32).astype(jnp.bfloat16)
+def select_kernel(grp_ref, *refs):
+    want_refs, (dec_ref, enc_ref, bias_ref) = refs[:4], refs[4:7]
+    dec_give_ref, dec_keep_ref, enc_give_ref, enc_keep_ref = refs[7:]
+    want = jnp.concatenate([ref[0] for ref in want_refs])
+    column = lax.broadcasted_iota(jnp.int32, (want.shape[0], dec_ref.shape[0]), 1)
+    hits = (column == want).astype(jnp.float32).astype(jnp.bfloat16)
     across = lambda a, b: lax.dot_general(
         a, b, (((1,), (1,)), ((), ())), preferred_element_type=jnp.float32
     )
-    enc_out_ref[:, :width] = across(hits, enc_ref[...]).astype(jnp.bfloat16)
-    enc_out_ref[:, width:] = across(hits, bias_ref[...]).astype(jnp.bfloat16)
-
-
-def select(dec_want, enc_want, dec_weight, enc_weight, bias_parts):
-    count, tile = dec_want.shape[0], 256
+    dec = mm(hits, dec_ref[...]).astype(jnp.bfloat16)
+    enc = across(hits, enc_ref[...]).astype(jnp.bfloat16)
+    bias = across(hits, bias_ref[...]).astype(jnp.bfloat16)
+    step = pl.program_id(0)
+
+    def put(wanted, ref, values):
+        @pl.when(wanted)
+        def _():
+            at = 0
+            for value in values:
+                ref[:, at : at + value.shape[1]] = value
+                at += value.shape[1]
+
+    put(step < 2, dec_give_ref, [dec])
+    put(step >= 2, dec_keep_ref, [dec])
+    put(step % 2 == 0, enc_give_ref, [enc, bias])
+    put(step % 2 == 1, enc_keep_ref, [enc, bias])
+
+
+def select(grp_rank, want, dec_weight, enc_weight, bias_parts):
+    rows = want.shape[1]
+    tile = 4 * rows
     span, width = dec_weight.shape
     lanes = bias_parts.shape[0]
-    fixed = lambda shape: pl.BlockSpec(shape, lambda i: (0, 0), pipeline_mode=pl.Buffered(1))
+    fixed = lambda shape: pl.BlockSpec(shape, lambda i, g: (0, 0), pipeline_mode=pl.Buffered(1))
+    wanted = lambda k: pl.BlockSpec(
+        (1, rows, 1), lambda i, g: (g[0] ^ (4 * k + 2 * (1 - i // 2) + 1 - i % 2), 0, 0)
+    )
+    half = lambda cols: jax.ShapeDtypeStruct((2 * tile, cols), jnp.bfloat16)
     return pl.pallas_call(
         select_kernel,
-        grid=(count // tile,),
-        in_specs=[
-            pl.BlockSpec((tile, 1), lambda i: (i, 0)),
-            pl.BlockSpec((tile, 1), lambda i: (i, 0)),
-            fixed((span, width)),
-            fixed((width, span)),
-            fixed((lanes, span)),
-        ],
-        out_specs=[
-            pl.BlockSpec((tile, width), lambda i: (i, 0)),
-            pl.BlockSpec((tile, width + lanes), lambda i: (i, 0)),
-        ],
-        out_shape=[
-            jax.ShapeDtypeStruct((count, width), jnp.bfloat16),
-            jax.ShapeDtypeStruct((count, width + lanes), jnp.bfloat16),
-        ],
+        grid_spec=pltpu.PrefetchScalarGridSpec(
+            num_scalar_prefetch=1,
+            grid=(4,),
+            in_specs=[wanted(k) for k in range(4)]
+            + [fixed((span, width)), fixed((width, span)), fixed((lanes, span))],
+            out_specs=[
+                pl.BlockSpec((tile, width), lambda i, g: (jnp.minimum(i, 1), 0)),
+                pl.BlockSpec((tile, width), lambda i, g: (jnp.maximum(i - 2, 0), 0)),
+                pl.BlockSpec((tile, width + lanes), lambda i, g: (i // 2, 0)),
+                pl.BlockSpec((tile, width + lanes), lambda i, g: (i // 3, 0)),
+            ],
+        ),
+        out_shape=[half(width), half(width), half(width + lanes), half(width + lanes)],
         cost_estimate=pl.CostEstimate(
-            flops=2 * count * span * (2 * width + lanes),
-            bytes_accessed=2 * span * (2 * width + lanes) + 2 * count * (2 * width + lanes),
+            flops=8 * tile * span * (2 * width + lanes),
+            bytes_accessed=2 * (span + 4 * tile) * (2 * width + lanes),
             transcendentals=0,
         ),
         name="select",
-    )(dec_want, enc_want, dec_weight, enc_weight, bias_parts)
+    )(grp_rank.reshape(1), want, want, want, want, dec_weight, enc_weight, bias_parts)
 
 
 def encode_kernel(slot_ref, *refs):
     block_refs, (w_mine_ref, w_other_ref) = refs[:8], refs[8:10]
-    out_refs, x_ref = refs[10:18], refs[18]
+    out_refs, x_ref, sems = refs[10:18], refs[18], refs[19]
     half = w_mine_ref.shape[0]
     rows = out_refs[0].shape[0]
 
     @pl.when(pl.program_id(0) == 0)
     def _():
-        for k in range(8):
-            x_ref[pl.ds(pl.multiple_of(slot_ref[k] * rows, rows), rows), :] = block_refs[k][...]
+        copies = [
+            pltpu.make_async_copy(
+                block_refs[k],
+                x_ref.at[pl.ds(pl.multiple_of(slot_ref[k] * rows, rows), rows), :],
+                sems.at[k],
+            )
+            for k in range(8)
+        ]
+        for copy in copies:
+            copy.start()
+        for copy in copies:
+            copy.wait()
 
     part = mm(x_ref[:, :half], w_mine_ref[...]) + mm(x_ref[:, half:], w_other_ref[...])
     part = part.astype(jnp.bfloat16)
@@ -192,10 +219,13 @@
         grid_spec=pltpu.PrefetchScalarGridSpec(
             num_scalar_prefetch=1,
             grid=(span // tile,),
-            in_specs=[pl.BlockSpec((rows, depth), lambda i, slot: (0, 0))] * 8
+            in_specs=[pl.BlockSpec(memory_space=pl.ANY)] * 8
             + [pl.BlockSpec((depth // 2, tile), lambda i, slot: (0, i))] * 2,
             out_specs=[pl.BlockSpec((rows, tile), lambda i, slot: (0, i))] * 8,
-            scratch_shapes=[pltpu.VMEM((count, depth), jnp.bfloat16)],
+            scratch_shapes=[
+                pltpu.VMEM((count, depth), jnp.bfloat16),
+                pltpu.SemaphoreType.DMA((8,)),
+            ],
         ),
         out_shape=[jax.ShapeDtypeStruct((rows, span), jnp.bfloat16)] * 8,
         cost_estimate=pl.CostEstimate(
@@ -228,10 +258,9 @@
     span = enc_weight.shape[1]
     my_quarter = z // 2
 
-    ids = clamp_ids[:, :1].reshape(1, rows)
-    ids = jnp.concatenate([ids, flip_plane(ids)])
-    for k in (1, 2, 4):
-        ids = jnp.concatenate([ids, flip_z(ids, k)])
+    ids = lax.all_to_all(
+        jnp.broadcast_to(clamp_ids[:, 0].reshape(1, 1, rows), (16, 1, rows)), "grp", 0, 0, tiled=True
+    ).reshape(16, rows, 1)
 
     out_other = swap_core(out_weight)
     enc_other = swap_core(enc_weight)
@@ -243,17 +272,16 @@
     arrived = lax.all_to_all(part, "tp", 0, 0, axis_index_groups=groups, tiled=True)
     resid_mid = (resid_in.astype(f32) + jnp.sum(arrived.astype(f32), axis=0)).astype(bf16)
 
-    want = (ids % QUARTER + my_quarter * QUARTER - grp_rank * span).reshape(4, 2, 2, rows)
-    want = want[:, ::-1, ::-1]
-    dec_want = want.transpose(1, 2, 0, 3).reshape(16 * rows, 1)
-    enc_want = want.transpose(2, 1, 0, 3).reshape(16 * rows, 1)
+    want = ids % QUARTER + (my_quarter * QUARTER - grp_rank * span)
     high = enc_bias.astype(bf16)
     middle = (enc_bias - high.astype(f32)).astype(bf16)
     low = (enc_bias - high.astype(f32) - middle.astype(f32)).astype(bf16)
     bias_parts = jnp.pad(jnp.stack([high, middle, low]), ((0, 125), (0, 0)))
-    found_dec, found_enc = select(dec_want, enc_want, dec_weight, enc_weight, bias_parts)
-    near_dec = flip_z(found_dec[: 8 * rows], 1)
-    near_enc = flip_plane(found_enc[: 8 * rows])
+    dec_give, dec_keep, enc_give, enc_keep = select(
+        grp_rank, want, dec_weight, enc_weight, bias_parts
+    )
+    dec_near = flip_z(dec_give, 1)
+    enc_near = flip_plane(enc_give)
 
     mid_other = swap_core(resid_mid)
     both = jnp.concatenate([resid_mid, mid_other], axis=1)
@@ -268,23 +296,22 @@
         (3, 2, 1), (5, 6, 7), (4, 2, 2),
     ):
         block[k] = from_z(block[source], step)
-    found_dec = found_dec[8 * rows :] + near_dec
-    found_enc = found_enc[8 * rows :] + near_enc
-    near_dec = flip_plane(found_dec[: 4 * rows])
-    near_enc = flip_z(found_enc[: 4 * rows], 1)
-    found = jnp.concatenate([found_dec[4 * rows :] + near_dec, found_enc[4 * rows :] + near_enc], axis=1)
-    held = [found[:rows]]
-    for k in (1, 2, 3):
-        held.append(flip_z(found[k * rows : (k + 1) * rows], 2 * k))
+    first, last = slice(0, 4 * rows), slice(4 * rows, 8 * rows)
+    dec_near_2 = flip_plane(dec_keep[first] + dec_near[first])
+    enc_near_2 = flip_z(enc_keep[first] + enc_near[first], 1)
+    dec_sum = dec_keep[last] + dec_near[last] + dec_near_2
+    enc_sum = enc_keep[last] + enc_near[last] + enc_near_2
+    held = []
+    for k in range(4):
+        piece = slice(k * rows, (k + 1) * rows)
+        piece = jnp.concatenate([dec_sum[piece], enc_sum[piece]], axis=1)
+        if k:
+            piece = flip_z(piece, 2 * k)
+        held.append(piece)
 
     ahead = (jnp.arange(8, dtype=jnp.int32) + z) % 8
     slot = (ahead // 4 + chip // 4) % 2 * 4 + (ahead - chip) % 4
     outs = encode(block, slot, enc_weight, enc_other)
-
-    total = outs[0].astype(f32)
-    moved = []
-    for s in (6, 5, 7, 4, 2, 1, 3):
-        moved.append(to_chip(outs[s], s // 4, s % 4))
 
     mid_again = lax.optimization_barrier(resid_mid).astype(f32)
     dots = jnp.stack(
@@ -296,6 +323,11 @@
     every = lax.all_to_all(
         jnp.broadcast_to(dots[None], (16, 4, rows)), "tp", 0, 0, tiled=True
     )
+    total = outs[0].astype(f32)
+    moved = []
+    for s in (6, 5, 7, 4, 2, 1, 3):
+        moved.append(to_chip(outs[s], s // 4, s % 4))
+
     for value in moved:
         total = total + value.astype(f32)
     features = jnp.maximum(total + enc_bias, 0.0).astype(bf16)

time: 169 us -> 172 us (1.018)
  the two profiles are of different devices: /device:TPU:64 before, /device:TPU:68 now
where the time goes in v2:
time: 172 us; the launch traced here: 171 us
  waiting for transfers between devices  67.2 us (39%)
  starting transfers between devices  60 us (35%)
  Pallas kernels  22.4 us (13%)
  other arithmetic  8.83 us (5%)
  local copies, waits for them, and re-layouts  6.5 us (4%)
  matrix products  5.37 us (3%)
    ppermute x7, waiting for transfers between devices, to_chip(): lax.ppermute(value, 'tp', tp_moves(lambda chip, core: chip_at(chip, dx, d...  19.4 us
    ppermute x7, starting transfers between devices, from_z(): lax.ppermute(value, 'grp', grp_moves(lambda z, plane: (z - ahead) % 8 * 2...  14.1 us
    ppermute x5, waiting for transfers between devices, flip_z(): lax.ppermute(value, 'grp', grp_moves(lambda z, plane: (z ^ k) * 2 + plane))  12 us
    all_to_all x1, starting transfers between devices, per_device(): lax.all_to_all(jnp.broadcast_to(clamp_ids[:, 0].reshape(1, 1, rows), (16,...  10.5 us
    pallas_call x1, Pallas kernels, select(): pl.pallas_call(select_kernel, grid_spec=pltpu.PrefetchScalarGridSpec(num_...  10.5 us
    ppermute x7, starting transfers between devices, to_chip(): lax.ppermute(value, 'tp', tp_moves(lambda chip, core: chip_at(chip, dx, d...  10.1 us
    ppermute x2, waiting for transfers between devices, flip_plane(): lax.ppermute(value, 'grp', grp_moves(lambda z, plane: z * 2 + 1 - plane))  9.24 us
    all_to_all x1, waiting for transfers between devices, per_device(): lax.all_to_all(part, 'tp', 0, 0, axis_index_groups=groups, tiled=True)  9.09 us
  transfers between devices with their start and end apart: 29, of which 13 were waited for; matrix products, arithmetic and copies ran while one was open for 10% of the time, Pallas kernels for 13%

profile of v2, /device:TPU:68, one launch (start us, length us, event | category | flops | bytes accessed | tf_op | source)
XLA Modules:
  0.0 171.4 jit_solution(13499030946419464168)
XLA Ops:
  2.0 10.5 %all-to-all-start.1 = ((s32[16,1,64]{2,1,0:T(1,128)}), s32[16,1,64]{2,1,0:T(1,128)S(1)}, u32[]{:S(2)}, u32[]{:S(2)}) async-start(s32[16,1,64]{2,1,0:T(1,128)} %broadcast_in_dim.55), calls=%async_computation.1 | async-start | bytes 16384 | tf_op jit(solution)/shard_map/all_to_all | solution.py:261
  16.1 2.9 %select_reduce_fusion = (f32[64,2]{1,0:T(8,128)S(1)}, f32[64,2,128]{2,1,0:T(2,128)S(1)}) fusion(pred[64,128]{1,0:T(8,128)(4,1)S(1)} %iota_compare_fusion.1, bf16[64,2,128]{2,1,0:T(2,128)(2,1)S(1)} %reshape.179, bf16[2,64,1,128,128]{4,3,1,2,0:T(8,128)(2,1)} %bitcast.99), kind=kOutput, calls=%fused_computation.43 | convolution fusion | flops 4243328 | bytes 2204160 | tf_op jit(solution)/shard_map/shd,spd->shp/dot_general | solution.py:61
  21.5 10.5 %select.68 = (bf16[512,512]{1,0:T(8,128)(2,1)}, bf16[512,512]{1,0:T(8,128)(2,1)}, bf16[512,640]{1,0:T(8,128)(2,1)}, bf16[512,640]{1,0:T(8,128)(2,1)}) custom-call(s32[1]{0:T(128)} %bitcast.10.grp_ref, s32[16,64,1]{2,1,0:T(8,128)} %fusion.10.refs_0_.refs_1_.refs_2_.refs_3_, s32[16,64,1]{2,1,0:T(8,128)} %fusion.10.refs_0_.refs_1_.refs_2_.refs_3_, ...), custom_call_target="tpu_custom_call" | custom-call | flops 4831838208 | bytes 7077888 | tf_op jit(solution)/shard_map/select/pallas_call | solution.py:161
  37.2 9.4 %collective-permute-done.4 = bf16[512,512]{1,0:T(8,128)(2,1)S(1)} collective-permute-done((bf16[512,512]{1,0:T(8,128)(2,1)}, bf16[512,512]{1,0:T(8,128)(2,1)S(1)}, u32[]{:S(2)}, u32[]{:S(2)}) %collective-permute-start.4) | collective-permute-done | bytes 524320 | tf_op jit(solution)/shard_map/ppermute | solution.py:33
  47.9 5.1 %collective-permute-done.2 = bf16[512,640]{1,0:T(8,128)(2,1)S(1)} collective-permute-done((bf16[512,640]{1,0:T(8,128)(2,1)}, bf16[512,640]{1,0:T(8,128)(2,1)S(1)}, u32[]{:S(2)}, u32[]{:S(2)}) %collective-permute-start.2) | collective-permute-done | bytes 655392 | tf_op jit(solution)/shard_map/ppermute | solution.py:37
  53.7 4.2 %collective-permute-done.5 = bf16[256,512]{1,0:T(8,128)(2,1)S(1)} collective-permute-done((bf16[256,512]{1,0:T(8,128)(2,1)S(1)}, bf16[256,512]{1,0:T(8,128)(2,1)S(1)}, u32[]{:S(2)}, u32[]{:S(2)}) %collective-permute-start.5) | collective-permute-done | bytes 262176 | tf_op jit(solution)/shard_map/ppermute | solution.py:37
  58.0 4.4 %project.1 = bf16[8,64,512]{2,1,0:T(8,128)(2,1)} custom-call(s32[1]{0:T(128)} %bitcast.core_ref, bf16[64,256]{1,0:T(8,128)(2,1)} %bitcast.87.mine_ref, bf16[64,256]{1,0:T(8,128)(2,1)} %collective-permute-done.other_ref, bf16[256,8192]{1,0:T(8,128)(2,1)} %refs_1_.1, bf16[256,8192]{1,0:T(8,128)(2,1)} %refs_1_.1, ...), custom_call_target="tpu_custom_call" | custom-call | flops 268435456 | bytes 4194304 | tf_op jit(solution)/shard_map/project/pallas_call | solution.py:105
  62.4 5.1 %all-to-all-start = ((bf16[8,64,512]{2,1,0:T(8,128)(2,1)}), bf16[8,64,512]{2,1,0:T(8,128)(2,1)S(1)}, u32[]{:S(2)}, u32[]{:S(2)}) async-start(bf16[8,64,512]{2,1,0:T(8,128)(2,1)} %project.1), calls=%async_computation | async-start | bytes 1048576 | tf_op jit(solution)/shard_map/all_to_all | solution.py:272
  67.6 9.1 %all-to-all-done = bf16[8,64,512]{2,1,0:T(8,128)(2,1)S(1)} async-done(((bf16[8,64,512]{2,1,0:T(8,128)(2,1)}), bf16[8,64,512]{2,1,0:T(8,128)(2,1)S(1)}, u32[]{:S(2)}, u32[]{:S(2)}) %all-to-all-start) | async-done | bytes 524320 | tf_op jit(solution)/shard_map/all_to_all | solution.py:272
  76.9 2.7 %collective-permute-start.7 = (bf16[64,1152]{1,0:T(8,128)(2,1)S(1)}, bf16[64,1152]{1,0:T(8,128)(2,1)S(1)}, u32[]{:S(2)}, u32[]{:S(2)}) collective-permute-start(bf16[64,1152]{1,0:T(8,128)(2,1)S(1)} %pad_maximum_fusion.1), channel_id=1, source_target_pairs={{0,8},{1,9},{2,10},{3,11},{4,12},{5,13},{6,14},{7,15},{8,0},{9,1},... | collective-permute-start | bytes 442376 | tf_op jit(solution)/shard_map/ppermute | solution.py:33
  81.0 2.5 %collective-permute-start.6 = (bf16[64,1152]{1,0:T(8,128)(2,1)S(1)}, bf16[64,1152]{1,0:T(8,128)(2,1)S(1)}, u32[]{:S(2)}, u32[]{:S(2)}) collective-permute-start(bf16[64,1152]{1,0:T(8,128)(2,1)S(1)} %pad_maximum_fusion), channel_id=1, source_target_pairs={{0,4},{1,5},{2,6},{3,7},{4,0},{5,1},{6,2},{7,3},{8,12},{9,13},{10,... | collective-permute-start | bytes 442376 | tf_op jit(solution)/shard_map/ppermute | solution.py:33
  83.4 4.6 %collective-permute-done.10 = bf16[64,1024]{1,0:T(8,128)(2,1)S(1)} collective-permute-done((bf16[64,1024]{1,0:T(8,128)(2,1)S(1)}, bf16[64,1024]{1,0:T(8,128)(2,1)S(1)}, u32[]{:S(2)}, u32[]{:S(2)}) %collective-permute-start.10) | collective-permute-done | bytes 131104 | tf_op jit(solution)/shard_map/ppermute | solution.py:291
  93.8 2.5 %collective-permute-done.6 = bf16[64,1152]{1,0:T(8,128)(2,1)S(1)} collective-permute-done((bf16[64,1152]{1,0:T(8,128)(2,1)S(1)}, bf16[64,1152]{1,0:T(8,128)(2,1)S(1)}, u32[]{:S(2)}, u32[]{:S(2)}) %collective-permute-start.6) | collective-permute-done | bytes 147488 | tf_op jit(solution)/shard_map/ppermute | solution.py:33
  96.4 3.7 %collective-permute-start.17 = (bf16[64,1024]{1,0:T(8,128)(2,1)S(1)}, bf16[64,1024]{1,0:T(8,128)(2,1)S(1)}, u32[]{:S(2)}, u32[]{:S(2)}) collective-permute-start(bf16[64,1024]{1,0:T(8,128)(2,1)S(1)} %broadcast_select_fusion.refs_0_), channel_id=1, source_target_pairs={{0,2},{1,3},{2,4},{3,5},{4,6},{5,7},{6,8},{7,9},{8,10},{9,11},{10,... | collective-permute-start | bytes 393224 | tf_op jit(solution)/shard_map/ppermute | solution.py:27
  100.1 3.1 %collective-permute-start.14 = (bf16[64,1024]{1,0:T(8,128)(2,1)S(1)}, bf16[64,1024]{1,0:T(8,128)(2,1)S(1)}, u32[]{:S(2)}, u32[]{:S(2)}) collective-permute-start(bf16[64,1024]{1,0:T(8,128)(2,1)S(1)} %collective-permute-done.12.refs_2_), channel_id=1, source_target_pairs={{0,12},{1,13},{2,14},{3,15},{4,0},{5,1},{6,2},{7,3},{8,4},{9,5},{1... | collective-permute-start | bytes 393224 | tf_op jit(solution)/shard_map/ppermute | solution.py:27
  106.6 6.9 %collective-permute-done.14.refs_4_ = bf16[64,1024]{1,0:T(8,128)(2,1)S(1)} collective-permute-done((bf16[64,1024]{1,0:T(8,128)(2,1)S(1)}, bf16[64,1024]{1,0:T(8,128)(2,1)S(1)}, u32[]{:S(2)}, u32[]{:S(2)}) %collective-permute-start.14) | collective-permute-done | bytes 131104 | tf_op jit(solution)/shard_map/ppermute | solution.py:27
  114.8 7.5 %encode.1 = (bf16[64,2048]{1,0:T(8,128)(2,1)}, bf16[64,2048]{1,0:T(8,128)(2,1)}, bf16[64,2048]{1,0:T(8,128)(2,1)}, bf16[64,2048]{1,0:T(8,128)(2,1)}, bf16[64,204...) custom-call(s32[8]{0:T(128)} %fusion.27.slot_ref, ...), custom_call_target="tpu_custom_call" | custom-call | flops 2147483648 | bytes 7340032 | tf_op jit(solution)/shard_map/encode/pallas_call | solution.py:217
  125.3 8.6 %all-to-all-start.2 = ((f32[16,1,256]{2,1,0:T(1,128)}), f32[16,1,256]{2,1,0:T(1,128)S(1)}, u32[]{:S(2)}, u32[]{:S(2)}) async-start(f32[16,1,256]{2,1,0:T(1,128)} %reshape.186), calls=%async_computation.2 | async-start | bytes 32768 | tf_op jit(solution)/shard_map/all_to_all | solution.py:323
  134.0 6.0 %all-to-all-done.2 = f32[16,1,256]{2,1,0:T(1,128)S(1)} async-done(((f32[16,1,256]{2,1,0:T(1,128)}), f32[16,1,256]{2,1,0:T(1,128)S(1)}, u32[]{:S(2)}, u32[]{:S(2)}) %all-to-all-start.2) | async-done | bytes 16416 | tf_op jit(solution)/shard_map/all_to_all | solution.py:323
  143.1 2.9 %collective-permute-start.21 = (bf16[64,2048]{1,0:T(8,128)(2,1)}, bf16[64,2048]{1,0:T(8,128)(2,1)S(1)}, u32[]{:S(2)}, u32[]{:S(2)}) collective-permute-start(bf16[64,2048]{1,0:T(8,128)(2,1)} %get-tuple-element.21), channel_id=1, source_target_pairs={{0,224},{16,240},{32,128},{48,144},{64,160},{80,176},{96,192},{112... | collective-permute-start | bytes 786440 | tf_op jit(solution)/shard_map/ppermute | solution.py:45
  146.0 3.2 %collective-permute-start.19 = (bf16[64,2048]{1,0:T(8,128)(2,1)}, bf16[64,2048]{1,0:T(8,128)(2,1)S(1)}, u32[]{:S(2)}, u32[]{:S(2)}) collective-permute-start(bf16[64,2048]{1,0:T(8,128)(2,1)} %get-tuple-element.19), channel_id=1, source_target_pairs={{0,192},{16,208},{32,224},{48,240},{64,128},{80,144},{96,160},{112... | collective-permute-start | bytes 786440 | tf_op jit(solution)/shard_map/ppermute | solution.py:45
  151.9 5.9 %collective-permute-done.21 = bf16[64,2048]{1,0:T(8,128)(2,1)S(1)} collective-permute-done((bf16[64,2048]{1,0:T(8,128)(2,1)}, bf16[64,2048]{1,0:T(8,128)(2,1)S(1)}, u32[]{:S(2)}, u32[]{:S(2)}) %collective-permute-start.21) | collective-permute-done | bytes 262176 | tf_op jit(solution)/shard_map/ppermute | solution.py:45
  157.8 6.8 %collective-permute-done.20 = bf16[64,2048]{1,0:T(8,128)(2,1)S(1)} collective-permute-done((bf16[64,2048]{1,0:T(8,128)(2,1)}, bf16[64,2048]{1,0:T(8,128)(2,1)S(1)}, u32[]{:S(2)}, u32[]{:S(2)}) %collective-permute-start.20) | collective-permute-done | bytes 262176 | tf_op jit(solution)/shard_map/ppermute | solution.py:45
  164.6 4.8 %collective-permute-done.19 = bf16[64,2048]{1,0:T(8,128)(2,1)S(1)} collective-permute-done((bf16[64,2048]{1,0:T(8,128)(2,1)}, bf16[64,2048]{1,0:T(8,128)(2,1)S(1)}, u32[]{:S(2)}, u32[]{:S(2)}) %collective-permute-start.19) | collective-permute-done | bytes 262176 | tf_op jit(solution)/shard_map/ppermute | solution.py:45
  (117 shorter events, 37.4 us)
Async XLA Ops:
  0.6 57.3 %collective-permute-start.1 = (bf16[256,8192]{1,0:T(8,128)(2,1)}, bf16[256,8192]{1,0:T(8,128)(2,1)}, u32[]{:S(2)}, u32[]{:S(2)}) collective-permute-start(bf16[256,8192]{1,0:T(8,128)(2,1)} %refs_1_.1), channel_id=1, source_target_pairs={{0,16},{16,0},{32,48},{48,32},{64,80},{80,64},{96,112},{112,96},{1... | collective-permute-start | bytes 12582920 | tf_op jit(solution)/shard_map/ppermute | solution.py:23
  2.0 18.2 %all-to-all-start.1 = ((s32[16,1,64]{2,1,0:T(1,128)}), s32[16,1,64]{2,1,0:T(1,128)S(1)}, u32[]{:S(2)}, u32[]{:S(2)}) async-start(s32[16,1,64]{2,1,0:T(1,128)} %broadcast_in_dim.55), calls=%async_computation.1 | async-start | bytes 16384 | tf_op jit(solution)/shard_map/all_to_all | solution.py:261
  12.6 87.5 %collective-permute-start.18 = (bf16[512,2048]{1,0:T(8,128)(2,1)}, bf16[512,2048]{1,0:T(8,128)(2,1)}, u32[]{:S(2)}, u32[]{:S(2)}) collective-permute-start(bf16[512,2048]{1,0:T(8,128)(2,1)} %refs_8_.1), channel_id=1, source_target_pairs={{0,16},{16,0},{32,48},{48,32},{64,80},{80,64},{96,112},{112,96},{1... | collective-permute-start | bytes 6291464 | tf_op jit(solution)/shard_map/ppermute | solution.py:23
  32.0 14.6 %collective-permute-start.4 = (bf16[512,512]{1,0:T(8,128)(2,1)}, bf16[512,512]{1,0:T(8,128)(2,1)S(1)}, u32[]{:S(2)}, u32[]{:S(2)}) collective-permute-start(bf16[512,512]{1,0:T(8,128)(2,1)} %get-tuple-element.17), channel_id=1, source_target_pairs={{0,2},{1,3},{2,0},{3,1},{4,6},{5,7},{6,4},{7,5},{8,10},{9,11},{10,... | collective-permute-start | bytes 1572872 | tf_op jit(solution)/shard_map/ppermute | solution.py:33
  33.6 19.4 %collective-permute-start.2 = (bf16[512,640]{1,0:T(8,128)(2,1)}, bf16[512,640]{1,0:T(8,128)(2,1)S(1)}, u32[]{:S(2)}, u32[]{:S(2)}) collective-permute-start(bf16[512,640]{1,0:T(8,128)(2,1)} %get-tuple-element.15), channel_id=1, source_target_pairs={{0,1},{1,0},{2,3},{3,2},{4,5},{5,4},{6,7},{7,6},{8,9},{9,8},{10,11... | collective-permute-start | bytes 1966088 | tf_op jit(solution)/shard_map/ppermute | solution.py:37
  37.2 20.8 %collective-permute-start = (bf16[64,256]{1,0:T(8,128)(2,1)}, bf16[64,256]{1,0:T(8,128)(2,1)}, u32[]{:S(2)}, u32[]{:S(2)}) collective-permute-start(bf16[64,256]{1,0:T(8,128)(2,1)} %bitcast.87.mine_ref), channel_id=1, source_target_pairs={{0,16},{16,0},{32,48},{48,32},{64,80},{80,64},{96,112},{112,96},{1... | collective-permute-start | bytes 98312 | tf_op jit(solution)/shard_map/ppermute | solution.py:23
  46.7 11.2 %collective-permute-start.5 = (bf16[256,512]{1,0:T(8,128)(2,1)S(1)}, bf16[256,512]{1,0:T(8,128)(2,1)S(1)}, u32[]{:S(2)}, u32[]{:S(2)}) collective-permute-start(bf16[256,512]{1,0:T(8,128)(2,1)S(1)} %slice_add_fusion.2), channel_id=1, source_target_pairs={{0,1},{1,0},{2,3},{3,2},{4,5},{5,4},{6,7},{7,6},{8,9},{9,8},{10,11... | collective-permute-start | bytes 786440 | tf_op jit(solution)/shard_map/ppermute | solution.py:37
  53.1 14.4 %collective-permute-start.3 = (bf16[256,640]{1,0:T(8,128)(2,1)S(1)}, bf16[256,640]{1,0:T(8,128)(2,1)S(1)}, u32[]{:S(2)}, u32[]{:S(2)}) collective-permute-start(bf16[256,640]{1,0:T(8,128)(2,1)S(1)} %slice_add_fusion), channel_id=1, source_target_pairs={{0,2},{1,3},{2,0},{3,1},{4,6},{5,7},{6,4},{7,5},{8,10},{9,11},{10,... | collective-permute-start | bytes 983048 | tf_op jit(solution)/shard_map/ppermute | solution.py:33
  62.4 14.3 %all-to-all-start = ((bf16[8,64,512]{2,1,0:T(8,128)(2,1)}), bf16[8,64,512]{2,1,0:T(8,128)(2,1)S(1)}, u32[]{:S(2)}, u32[]{:S(2)}) async-start(bf16[8,64,512]{2,1,0:T(8,128)(2,1)} %project.1), calls=%async_computation | async-start | bytes 1048576 | tf_op jit(solution)/shard_map/all_to_all | solution.py:272
  76.9 15.5 %collective-permute-start.7 = (bf16[64,1152]{1,0:T(8,128)(2,1)S(1)}, bf16[64,1152]{1,0:T(8,128)(2,1)S(1)}, u32[]{:S(2)}, u32[]{:S(2)}) collective-permute-start(bf16[64,1152]{1,0:T(8,128)(2,1)S(1)} %pad_maximum_fusion.1), channel_id=1, source_target_pairs={{0,8},{1,9},{2,10},{3,11},{4,12},{5,13},{6,14},{7,15},{8,0},{9,1},... | collective-permute-start | bytes 442376 | tf_op jit(solution)/shard_map/ppermute | solution.py:33
  81.0 15.4 %collective-permute-start.6 = (bf16[64,1152]{1,0:T(8,128)(2,1)S(1)}, bf16[64,1152]{1,0:T(8,128)(2,1)S(1)}, u32[]{:S(2)}, u32[]{:S(2)}) collective-permute-start(bf16[64,1152]{1,0:T(8,128)(2,1)S(1)} %pad_maximum_fusion), channel_id=1, source_target_pairs={{0,4},{1,5},{2,6},{3,7},{4,0},{5,1},{6,2},{7,3},{8,12},{9,13},{10,... | collective-permute-start | bytes 442376 | tf_op jit(solution)/shard_map/ppermute | solution.py:33
  88.1 12.0 %collective-permute-start.12 = (bf16[64,1024]{1,0:T(8,128)(2,1)S(1)}, bf16[64,1024]{1,0:T(8,128)(2,1)S(1)}, u32[]{:S(2)}, u32[]{:S(2)}) collective-permute-start(bf16[64,1024]{1,0:T(8,128)(2,1)S(1)} %broadcast_select_fusion.refs_0_), channel_id=1, source_target_pairs={{0,12},{1,13},{2,14},{3,15},{4,0},{5,1},{6,2},{7,3},{8,4},{9,5},{1... | collective-permute-start | bytes 393224 | tf_op jit(solution)/shard_map/ppermute | solution.py:27
  90.5 12.7 %collective-permute-start.15 = (bf16[64,1024]{1,0:T(8,128)(2,1)S(1)}, bf16[64,1024]{1,0:T(8,128)(2,1)S(1)}, u32[]{:S(2)}, u32[]{:S(2)}) collective-permute-start(bf16[64,1024]{1,0:T(8,128)(2,1)S(1)} %broadcast_select_fusion.refs_0_), channel_id=1, source_target_pairs={{0,4},{1,5},{2,6},{3,7},{4,8},{5,9},{6,10},{7,11},{8,12},{9,13},{1... | collective-permute-start | bytes 393224 | tf_op jit(solution)/shard_map/ppermute | solution.py:27
  92.4 12.7 %collective-permute-start.11 = (bf16[64,1024]{1,0:T(8,128)(2,1)S(1)}, bf16[64,1024]{1,0:T(8,128)(2,1)S(1)}, u32[]{:S(2)}, u32[]{:S(2)}) collective-permute-start(bf16[64,1024]{1,0:T(8,128)(2,1)S(1)} %broadcast_select_fusion.refs_0_), channel_id=1, source_target_pairs={{0,14},{1,15},{2,0},{3,1},{4,2},{5,3},{6,4},{7,5},{8,6},{9,7},{10,... | collective-permute-start | bytes 393224 | tf_op jit(solution)/shard_map/ppermute | solution.py:27
  96.4 10.2 %collective-permute-start.17 = (bf16[64,1024]{1,0:T(8,128)(2,1)S(1)}, bf16[64,1024]{1,0:T(8,128)(2,1)S(1)}, u32[]{:S(2)}, u32[]{:S(2)}) collective-permute-start(bf16[64,1024]{1,0:T(8,128)(2,1)S(1)} %broadcast_select_fusion.refs_0_), channel_id=1, source_target_pairs={{0,2},{1,3},{2,4},{3,5},{4,6},{5,7},{6,8},{7,9},{8,10},{9,11},{10,... | collective-permute-start | bytes 393224 | tf_op jit(solution)/shard_map/ppermute | solution.py:27
  100.1 13.4 %collective-permute-start.14 = (bf16[64,1024]{1,0:T(8,128)(2,1)S(1)}, bf16[64,1024]{1,0:T(8,128)(2,1)S(1)}, u32[]{:S(2)}, u32[]{:S(2)}) collective-permute-start(bf16[64,1024]{1,0:T(8,128)(2,1)S(1)} %collective-permute-done.12.refs_2_), channel_id=1, source_target_pairs={{0,12},{1,13},{2,14},{3,15},{4,0},{5,1},{6,2},{7,3},{8,4},{9,5},{1... | collective-permute-start | bytes 393224 | tf_op jit(solution)/shard_map/ppermute | solution.py:27
  103.2 10.3 %collective-permute-start.16 = (bf16[64,1024]{1,0:T(8,128)(2,1)S(1)}, bf16[64,1024]{1,0:T(8,128)(2,1)S(1)}, u32[]{:S(2)}, u32[]{:S(2)}) collective-permute-start(bf16[64,1024]{1,0:T(8,128)(2,1)S(1)} %collective-permute-done.15.refs_6_), channel_id=1, source_target_pairs={{0,2},{1,3},{2,4},{3,5},{4,6},{5,7},{6,8},{7,9},{8,10},{9,11},{10,... | collective-permute-start | bytes 393224 | tf_op jit(solution)/shard_map/ppermute | solution.py:27
  105.1 19.2 %collective-permute-start.8 = (bf16[64,1152]{1,0:T(8,128)(2,1)S(1)}, bf16[64,1152]{1,0:T(8,128)(2,1)S(1)}, u32[]{:S(2)}, u32[]{:S(2)}) collective-permute-start(bf16[64,1152]{1,0:T(8,128)(2,1)S(1)} %pad_maximum_fusion.2), channel_id=1, source_target_pairs={{0,12},{1,13},{2,14},{3,15},{4,8},{5,9},{6,10},{7,11},{8,4},{9,5},... | collective-permute-start | bytes 442376 | tf_op jit(solution)/shard_map/ppermute | solution.py:33
  122.3 23.8 %collective-permute-start.25 = (bf16[64,2048]{1,0:T(8,128)(2,1)}, bf16[64,2048]{1,0:T(8,128)(2,1)S(1)}, u32[]{:S(2)}, u32[]{:S(2)}) collective-permute-start(bf16[64,2048]{1,0:T(8,128)(2,1)} %get-tuple-element.25), channel_id=1, source_target_pairs={{0,96},{16,112},{32,0},{48,16},{64,32},{80,48},{96,64},{112,80},{1... | collective-permute-start | bytes 786440 | tf_op jit(solution)/shard_map/ppermute | solution.py:45
  123.4 22.7 %collective-permute-start.24 = (bf16[64,2048]{1,0:T(8,128)(2,1)}, bf16[64,2048]{1,0:T(8,128)(2,1)S(1)}, u32[]{:S(2)}, u32[]{:S(2)}) collective-permute-start(bf16[64,2048]{1,0:T(8,128)(2,1)} %get-tuple-element.24), channel_id=1, source_target_pairs={{0,32},{16,48},{32,64},{48,80},{64,96},{80,112},{96,0},{112,16},{1... | collective-permute-start | bytes 786440 | tf_op jit(solution)/shard_map/ppermute | solution.py:45
  125.3 14.7 %all-to-all-start.2 = ((f32[16,1,256]{2,1,0:T(1,128)}), f32[16,1,256]{2,1,0:T(1,128)S(1)}, u32[]{:S(2)}, u32[]{:S(2)}) async-start(f32[16,1,256]{2,1,0:T(1,128)} %reshape.186), calls=%async_computation.2 | async-start | bytes 32768 | tf_op jit(solution)/shard_map/all_to_all | solution.py:323
  143.1 14.7 %collective-permute-start.21 = (bf16[64,2048]{1,0:T(8,128)(2,1)}, bf16[64,2048]{1,0:T(8,128)(2,1)S(1)}, u32[]{:S(2)}, u32[]{:S(2)}) collective-permute-start(bf16[64,2048]{1,0:T(8,128)(2,1)} %get-tuple-element.21), channel_id=1, source_target_pairs={{0,224},{16,240},{32,128},{48,144},{64,160},{80,176},{96,192},{112... | collective-permute-start | bytes 786440 | tf_op jit(solution)/shard_map/ppermute | solution.py:45
  146.0 18.6 %collective-permute-start.20 = (bf16[64,2048]{1,0:T(8,128)(2,1)}, bf16[64,2048]{1,0:T(8,128)(2,1)S(1)}, u32[]{:S(2)}, u32[]{:S(2)}) collective-permute-start(bf16[64,2048]{1,0:T(8,128)(2,1)} %get-tuple-element.20), channel_id=1, source_target_pairs={{0,160},{16,176},{32,192},{48,208},{64,224},{80,240},{96,128},{112... | collective-permute-start | bytes 786440 | tf_op jit(solution)/shard_map/ppermute | solution.py:45
  146.0 23.4 %collective-permute-start.19 = (bf16[64,2048]{1,0:T(8,128)(2,1)}, bf16[64,2048]{1,0:T(8,128)(2,1)S(1)}, u32[]{:S(2)}, u32[]{:S(2)}) collective-permute-start(bf16[64,2048]{1,0:T(8,128)(2,1)} %get-tuple-element.19), channel_id=1, source_target_pairs={{0,192},{16,208},{32,224},{48,240},{64,128},{80,144},{96,160},{112... | collective-permute-start | bytes 786440 | tf_op jit(solution)/shard_map/ppermute | solution.py:45
  (19 other events, 260.2 us)

commit v3 on v0

--- a/solution.py
+++ b/solution.py
@@ -82,28 +82,25 @@
     return jnp.dot(a, b, preferred_element_type=jnp.float32)
 
 
-def project_kernel(core_ref, mine_ref, other_ref, w_mine_ref, w_other_ref, out_ref):
-    out_ref[0] = (mm(mine_ref[...], w_mine_ref[...]) + mm(other_ref[...], w_other_ref[...])).astype(
-        out_ref.dtype
-    )
+def project_kernel(core_ref, mine_ref, other_ref, *refs):
+    weight_refs, out_ref = refs[:4], refs[4]
+    for i in range(2):
+        out_ref[i] = (
+            mm(mine_ref[...], weight_refs[i][...]) + mm(other_ref[...], weight_refs[2 + i][...])
+        ).astype(out_ref.dtype)
 
 
 def project(core, heads_mine, heads_other, w_mine, w_other, width):
     rows, depth = heads_mine.shape
-    columns = lambda i, core_ref: (0, 2 * i + core_ref[0])
-    whole = lambda i, core_ref: (0, 0)
+    columns = [pl.BlockSpec((depth, width), lambda i, core_ref, e=e: (0, 4 * i + 2 * e + core_ref[0])) for e in range(2)]
+    whole = pl.BlockSpec((rows, depth), lambda i, core_ref: (0, 0))
     return pl.pallas_call(
         project_kernel,
         grid_spec=pltpu.PrefetchScalarGridSpec(
             num_scalar_prefetch=1,
-            grid=(8,),
-            in_specs=[
-                pl.BlockSpec((rows, depth), whole),
-                pl.BlockSpec((rows, depth), whole),
-                pl.BlockSpec((depth, width), columns),
-                pl.BlockSpec((depth, width), columns),
-            ],
-            out_specs=pl.BlockSpec((1, rows, width), lambda i, core_ref: (i, 0, 0)),
+            grid=(4,),
+            in_specs=[whole, whole] + columns + columns,
+            out_specs=pl.BlockSpec((2, rows, width), lambda i, core_ref: (i, 0, 0)),
         ),
         out_shape=jax.ShapeDtypeStruct((8, rows, width), jnp.bfloat16),
         cost_estimate=pl.CostEstimate(
@@ -112,72 +109,92 @@
             transcendentals=0,
         ),
         name="project",
-    )(core.reshape(1), heads_mine, heads_other, w_mine, w_other)
-
-
-def encode_kernel(slot_ref, *refs):
+    )(core.reshape(1), heads_mine, heads_other, w_mine, w_mine, w_other, w_other)
+
+
+def encode_kernel(place_ref, *refs):
     block_refs, (want_ref, bias_ref, w_mine_ref, w_other_ref) = refs[:8], refs[8:12]
-    out_refs, x_ref = refs[12:21], refs[21]
+    out_refs, now_ref = refs[12:20], refs[20]
+    x_ref, held_ref, sems = refs[21:]
     step = pl.program_id(0)
-    half = w_mine_ref.shape[0]
-    tile = w_mine_ref.shape[1]
+    half, tile = w_mine_ref.shape
     rows = out_refs[0].shape[0]
 
     @pl.when(step == 0)
     def _():
-        for k in range(8):
-            x_ref[pl.ds(pl.multiple_of(slot_ref[k] * rows, rows), rows), :] = block_refs[k][...]
+        copies = [
+            pltpu.make_async_copy(
+                block_refs[k],
+                x_ref.at[pl.ds(pl.multiple_of(place_ref[k] * rows, rows), rows), :],
+                sems.at[k],
+            )
+            for k in range(8)
+        ]
+        for copy in copies:
+            copy.start()
+        held_ref[...] = jnp.zeros_like(held_ref)
+        for copy in copies:
+            copy.wait()
 
     part = mm(x_ref[:, :half], w_mine_ref[...]) + mm(x_ref[:, half:], w_other_ref[...])
     part = part.astype(jnp.bfloat16)
     for slot in range(8):
         out_refs[slot][...] = part[slot * rows : (slot + 1) * rows]
-    column = lax.broadcasted_iota(jnp.int32, part.shape, 1) + step * tile
-    is_hit = column == want_ref[...]
-    now = jnp.sum(
-        jnp.where(is_hit, part.astype(jnp.float32) + bias_ref[...], 0.0), axis=1, keepdims=True
-    )
-    total_ref = out_refs[8]
-
-    @pl.when(step == 0)
+    lanes = held_ref.shape[1]
+    want = want_ref[...] - step * tile
+    for at in range(0, tile, lanes):
+        piece = part[:, at : at + lanes].astype(jnp.float32) + bias_ref[:, at : at + lanes]
+        column = lax.broadcasted_iota(jnp.int32, piece.shape, 1) + at
+        held_ref[...] += jnp.where(column == want, piece, 0.0)
+
+    @pl.when(step == pl.num_programs(0) - 1)
     def _():
-        total_ref[...] = now
-
-    @pl.when(step != 0)
-    def _():
-        total_ref[...] += now
-
-
-def encode(block, slot, want, bias, w_mine, w_other):
+        total = lax.dot_general(
+            jnp.ones((8, lanes), jnp.float32),
+            held_ref[...],
+            (((1,), (1,)), ((), ())),
+            precision=lax.Precision.HIGHEST,
+            preferred_element_type=jnp.float32,
+        )
+        now_ref[...] = jnp.zeros_like(now_ref)
+        for slot in range(8):
+            now_ref[pl.ds(place_ref[8 + slot], 1), :] = total[:1, slot * rows : (slot + 1) * rows]
+
+
+def encode(block, place, want, bias, w_mine, w_other):
     rows, depth = block[0].shape
     count = 8 * rows
     span = w_mine.shape[1]
-    tile = 256
+    tile = 512
     return pl.pallas_call(
         encode_kernel,
         grid_spec=pltpu.PrefetchScalarGridSpec(
             num_scalar_prefetch=1,
             grid=(span // tile,),
-            in_specs=[pl.BlockSpec((rows, depth), lambda i, slot: (0, 0))] * 8
+            in_specs=[pl.BlockSpec(memory_space=pl.ANY)] * 8
             + [
-                pl.BlockSpec((count, 1), lambda i, slot: (0, 0)),
-                pl.BlockSpec((1, tile), lambda i, slot: (0, i)),
-                pl.BlockSpec((depth // 2, tile), lambda i, slot: (0, i)),
-                pl.BlockSpec((depth // 2, tile), lambda i, slot: (0, i)),
+                pl.BlockSpec((count, 1), lambda i, place: (0, 0)),
+                pl.BlockSpec((1, tile), lambda i, place: (0, i)),
+                pl.BlockSpec((depth // 2, tile), lambda i, place: (0, i)),
+                pl.BlockSpec((depth // 2, tile), lambda i, place: (0, i)),
             ],
-            out_specs=[pl.BlockSpec((rows, tile), lambda i, slot: (0, i))] * 8
-            + [pl.BlockSpec((count, 1), lambda i, slot: (0, 0))],
-            scratch_shapes=[pltpu.VMEM((count, depth), jnp.bfloat16)],
+            out_specs=[pl.BlockSpec((rows, tile), lambda i, place: (0, i))] * 8
+            + [pl.BlockSpec((16, rows), lambda i, place: (0, 0))],
+            scratch_shapes=[
+                pltpu.VMEM((count, depth), jnp.bfloat16),
+                pltpu.VMEM((count, 128), jnp.float32),
+                pltpu.SemaphoreType.DMA((8,)),
+            ],
         ),
         out_shape=[jax.ShapeDtypeStruct((rows, span), jnp.bfloat16)] * 8
-        + [jax.ShapeDtypeStruct((count, 1), jnp.float32)],
+        + [jax.ShapeDtypeStruct((16, rows), jnp.float32)],
         cost_estimate=pl.CostEstimate(
             flops=2 * count * depth * span,
             bytes_accessed=2 * (depth * span + count * (depth + span)),
             transcendentals=0,
         ),
         name="encode",
-    )(slot, *block, want, bias, w_mine, w_other)
+    )(place, *block, want, bias, w_mine, w_other)
 
 
 def per_device(
@@ -249,28 +266,26 @@
     mine = lax.dynamic_index_in_dim(want.reshape(8, 2, rows), core, 1, keepdims=False)
     slots = jnp.concatenate([lax.dynamic_index_in_dim(mine, t, 0, keepdims=False) for t in target])
     bias = jnp.where(chip == 0, enc_bias, 0.0).reshape(1, span)
-    outs = encode(block, slot, slots.reshape(8 * rows, 1), bias, enc_weight, enc_other)
-
-    now = outs[8].reshape(8, rows)
-    by_z = jnp.stack(
-        [
-            lax.dynamic_index_in_dim(now, chip_at(t, chip // 4, -chip % 4), 0, keepdims=False)
-            for t in range(8)
-        ]
-    )
-    sent = jnp.where(
-        (jnp.arange(2) == core)[None, :, None], by_z[:, None, :], 0.0
-    ).reshape(16, 1, rows)
-    held = lax.all_to_all(sent, "grp", 0, 0, tiled=True)
+    each = jnp.arange(8, dtype=jnp.int32)
+    goal = ((chip // 4 + each // 4) % 2 * 4 + (chip + each) % 4) * 2 + core
+    outs = encode(
+        block, jnp.concatenate([slot, goal]), slots.reshape(8 * rows, 1), bias, enc_weight, enc_other
+    )
+
+    relayed = to_chip(outs[6], 0, 3)
+    seven = outs[7] + relayed
+    relayed = to_chip(outs[2], 0, 1)
+    one = outs[1] + relayed
+    moved = []
+    for value, s in ((outs[4], 4), (outs[5], 5), (outs[3], 3), (seven, 7), (one, 1)):
+        moved.append(to_chip(value, s // 4, s % 4))
+
+    held = lax.all_to_all(outs[8].reshape(16, 1, rows), "grp", 0, 0, tiled=True)
     held = held.reshape(4, 4, rows).sum(axis=1)
-
-    total = outs[0].astype(f32)
-    moved = []
-    for s in (6, 5, 7, 4, 2, 1, 3):
-        moved.append(to_chip(outs[s], s // 4, s % 4))
     every = lax.all_to_all(
         jnp.broadcast_to(held[None], (16, 4, rows)), "tp", 0, 0, tiled=True
     )
+    total = outs[0].astype(f32)
     for value in moved:
         total = total + value.astype(f32)
     features = jnp.maximum(total + enc_bias, 0.0).astype(bf16)

time: 153 us -> 144 us (0.941)
  waiting for transfers between devices: 45.3 us -> 40.5 us
  Pallas kernels: 15.8 us -> 13.2 us
    ppermute x10, waiting for transfers between devices: 9.17 us -> 4.81 us  [from_z(): lax.ppermute(value, 'grp', grp_moves(lambda z, plane: (z - ahead) % 8 * 2...]
    pallas_call x1, Pallas kernels: 6.39 us -> 4.36 us  [project(): pl.pallas_call(project_kernel, grid_spec=pltpu.PrefetchScalarGridSpec(num...]
    ppermute x7, waiting for transfers between devices: 11.9 us -> 10 us  [to_chip(): lax.ppermute(value, 'tp', tp_moves(lambda chip, core: chip_at(chip, dx, d...]
  transfers between devices with their start and end apart: 28 -> 28, of which waited for: 13 -> 8; matrix products, arithmetic and copies ran while one was open for 14% -> 15% of each run, Pallas kernels for 11% -> 9%
where the time goes in v3:
time: 144 us; the launch traced here: 142 us
  starting transfers between devices  63 us (44%)
  waiting for transfers between devices  40.5 us (28%)
  Pallas kernels  13.2 us (9%)
  other arithmetic  8.63 us (6%)
  matrix products  7.75 us (5%)
  local copies, waits for them, and re-layouts  7.44 us (5%)
    ppermute x10, starting transfers between devices, from_z(): lax.ppermute(value, 'grp', grp_moves(lambda z, plane: (z - ahead) % 8 * 2...  19 us
    all_to_all x1, starting transfers between devices, per_device(): lax.all_to_all(jnp.broadcast_to(clamp_ids[:, 0].reshape(1, 1, rows), (16,...  11 us
    ppermute x7, waiting for transfers between devices, to_chip(): lax.ppermute(value, 'tp', tp_moves(lambda chip, core: chip_at(chip, dx, d...  10 us
    ppermute x1, waiting for transfers between devices, per_device(): lax.ppermute(found[:8 * rows], 'grp', grp_moves(lambda z_, s: (z_ ^ 1) *...  9.73 us
    ppermute x7, starting transfers between devices, to_chip(): lax.ppermute(value, 'tp', tp_moves(lambda chip, core: chip_at(chip, dx, d...  9.2 us
    pallas_call x1, Pallas kernels, encode(): pl.pallas_call(encode_kernel, grid_spec=pltpu.PrefetchScalarGridSpec(num_...  8.82 us
    all_to_all x1, waiting for transfers between devices, per_device(): lax.all_to_all(part, 'tp', 0, 0, axis_index_groups=groups, tiled=True)  7.89 us
    all_to_all x1, waiting for transfers between devices, per_device(): held = lax.all_to_all(outs[8].reshape(16, 1, rows), 'grp', 0, 0, tiled=True)  6.86 us
  transfers between devices with their start and end apart: 28, of which 8 were waited for; matrix products, arithmetic and copies ran while one was open for 15% of the time, Pallas kernels for 9%

profile of v3, /device:TPU:8, one launch (start us, length us, event | category | flops | bytes accessed | tf_op | source)
XLA Modules:
  0.0 141.9 jit_solution(17369913000873242090)
XLA Ops:
  2.2 11.0 %all-to-all-start.1 = ((s32[16,1,64]{2,1,0:T(1,128)}), s32[16,1,64]{2,1,0:T(1,128)S(1)}, u32[]{:S(2)}, u32[]{:S(2)}) async-start(s32[16,1,64]{2,1,0:T(1,128)} %broadcast_in_dim.60), calls=%async_computation.1 | async-start | bytes 16384 | tf_op jit(solution)/shard_map/all_to_all | solution.py:221
  15.9 2.9 %select_reduce_fusion = (f32[64,2]{1,0:T(8,128)S(1)}, f32[64,2,128]{2,1,0:T(2,128)S(1)}) fusion(pred[64,128]{1,0:T(8,128)(4,1)S(1)} %iota_compare_fusion.4, bf16[64,2,128]{2,1,0:T(2,128)(2,1)S(1)} %reshape.129, bf16[2,64,1,128,128]{4,3,1,2,0:T(8,128)(2,1)} %bitcast.119), kind=kOutput, calls=%fused_computation.29 | convolution fusion | flops 4243328 | bytes 2204160 | tf_op jit(solution)/shard_map/shd,spd->shp/dot_general | solution.py:53
  19.1 2.3 %fusion.8 = bf16[64,2,128]{2,1,0:T(2,128)(2,1)S(1)} fusion(bf16[2,64,1,128,128]{4,3,1,2,0:T(8,128)(2,1)} %bitcast.120, f32[64,2]{1,0:T(8,128)S(1)} %get-tuple-element.30, f32[64,128]{1,0:T(8,128)S(1)} %bitcast.114, f32[64,2]{1,0:T(8,128)S(1)} %convert_element_type.142, f32[64,2,128]{2,1,0:T(2,128)S(1)} %get-tuple-element.44, ...), kind=kOutput, calls=%fused_computation.11 | convolution fusion | flops 4308992 | bytes 2237952 | tf_op jit(solution)/shard_map/shp,spd->shd/dot_general | solution.py:67
  23.9 4.4 %project.1 = bf16[8,64,512]{2,1,0:T(8,128)(2,1)} custom-call(s32[1]{0:T(128)} %bitcast.core_ref, bf16[64,256]{1,0:T(8,128)(2,1)} %bitcast.107, bf16[64,256]{1,0:T(8,128)(2,1)} %copy-done.6, bf16[256,8192]{1,0:T(8,128)(2,1)} %refs_1_.1, bf16[256,8192]{1,0:T(8,128)(2,1)} %refs_1_.1, bf16[256,8192]{1,0:T(8,128)(2,1)} %collective-permute-done.1.refs_2_.refs_3_, ...), custom_call_target="tpu_custom_call" | custom-call | flops 268435456 | bytes 4194304 | tf_op jit(solution)/shard_map/project/pallas_call | solution.py:97
  28.3 5.1 %all-to-all-start = ((bf16[8,64,512]{2,1,0:T(8,128)(2,1)}), bf16[8,64,512]{2,1,0:T(8,128)(2,1)S(1)}, u32[]{:S(2)}, u32[]{:S(2)}) async-start(bf16[8,64,512]{2,1,0:T(8,128)(2,1)} %project.1), calls=%async_computation | async-start | bytes 1048576 | tf_op jit(solution)/shard_map/all_to_all | solution.py:231
  33.8 7.9 %all-to-all-done = bf16[8,64,512]{2,1,0:T(8,128)(2,1)S(1)} async-done(((bf16[8,64,512]{2,1,0:T(8,128)(2,1)}), bf16[8,64,512]{2,1,0:T(8,128)(2,1)S(1)}, u32[]{:S(2)}, u32[]{:S(2)}) %all-to-all-start) | async-done | bytes 524320 | tf_op jit(solution)/shard_map/all_to_all | solution.py:231
  43.1 5.9 %collective-permute-start.3 = (bf16[64,1024]{1,0:T(8,128)(2,1)S(1)}, bf16[64,1024]{1,0:T(8,128)(2,1)S(1)}, u32[]{:S(2)}, u32[]{:S(2)}) collective-permute-start(bf16[64,1024]{1,0:T(8,128)(2,1)S(1)} %pad_maximum_fusion), channel_id=1, source_target_pairs={{0,1},{2,3},{4,5},{6,7},{8,9},{10,11},{12,13},{14,15},{17,16},{19,... | collective-permute-start | bytes 393224 | tf_op jit(solution)/shard_map/ppermute | solution.py:246
  49.1 2.4 %fusion.4 = bf16[1024,512]{1,0:T(8,128)(2,1)S(1)} fusion(bf16[2048,512]{1,0:T(8,128)(2,1)S(1)} %copy-done, s32[1024]{0:T(1024)S(1)} %eq.92), kind=kOutput, calls=%fused_computation.7 | convolution fusion | flops 2150105088 | bytes 3149824 | tf_op jit(solution)/shard_map/dot_general | solution.py:82
  53.8 2.8 %collective-permute-start.5 = (bf16[64,1024]{1,0:T(8,128)(2,1)S(1)}, bf16[64,1024]{1,0:T(8,128)(2,1)}, u32[]{:S(2)}, u32[]{:S(2)}) collective-permute-start(bf16[64,1024]{1,0:T(8,128)(2,1)S(1)} %broadcast_select_fusion.refs_0_), channel_id=1, source_target_pairs={{0,12},{1,13},{2,14},{3,15},{4,0},{5,1},{6,2},{7,3},{8,4},{9,5},{1... | collective-permute-start | bytes 393224 | tf_op jit(solution)/shard_map/ppermute | solution.py:27
  58.1 9.7 %collective-permute-done.12 = bf16[512,512]{1,0:T(8,128)(2,1)S(1)} collective-permute-done((bf16[512,512]{1,0:T(8,128)(2,1)S(1)}, bf16[512,512]{1,0:T(8,128)(2,1)S(1)}, u32[]{:S(2)}, u32[]{:S(2)}) %collective-permute-start.12) | collective-permute-done | bytes 524320 | tf_op jit(solution)/shard_map/ppermute | solution.py:247
  67.8 4.1 %collective-permute-start.4 = (bf16[64,1024]{1,0:T(8,128)(2,1)S(1)}, bf16[64,1024]{1,0:T(8,128)(2,1)}, u32[]{:S(2)}, u32[]{:S(2)}) collective-permute-start(bf16[64,1024]{1,0:T(8,128)(2,1)S(1)} %broadcast_select_fusion.refs_0_), channel_id=1, source_target_pairs={{0,14},{1,15},{2,0},{3,1},{4,2},{5,3},{6,4},{7,5},{8,6},{9,7},{10,... | collective-permute-start | bytes 393224 | tf_op jit(solution)/shard_map/ppermute | solution.py:27
  72.0 2.8 %collective-permute-start.6 = (bf16[64,1024]{1,0:T(8,128)(2,1)}, bf16[64,1024]{1,0:T(8,128)(2,1)}, u32[]{:S(2)}, u32[]{:S(2)}) collective-permute-start(bf16[64,1024]{1,0:T(8,128)(2,1)} %collective-permute-done.5.refs_2_), channel_id=1, source_target_pairs={{0,14},{1,15},{2,0},{3,1},{4,2},{5,3},{6,4},{7,5},{8,6},{9,7},{10,... | collective-permute-start | bytes 393224 | tf_op jit(solution)/shard_map/ppermute | solution.py:27
  74.8 3.0 %collective-permute-start.7 = (bf16[64,1024]{1,0:T(8,128)(2,1)}, bf16[64,1024]{1,0:T(8,128)(2,1)}, u32[]{:S(2)}, u32[]{:S(2)}) collective-permute-start(bf16[64,1024]{1,0:T(8,128)(2,1)} %collective-permute-done.5.refs_2_), channel_id=1, source_target_pairs={{0,12},{1,13},{2,14},{3,15},{4,0},{5,1},{6,2},{7,3},{8,4},{9,5},{1... | collective-permute-start | bytes 393224 | tf_op jit(solution)/shard_map/ppermute | solution.py:27
  81.0 3.2 %collective-permute-done.9.refs_5_ = bf16[64,1024]{1,0:T(8,128)(2,1)} collective-permute-done((bf16[64,1024]{1,0:T(8,128)(2,1)}, bf16[64,1024]{1,0:T(8,128)(2,1)}, u32[]{:S(2)}, u32[]{:S(2)}) %collective-permute-start.9) | collective-permute-done | bytes 131104 | tf_op jit(solution)/shard_map/ppermute | solution.py:27
  84.3 8.8 %encode.1 = (bf16[64,2048]{1,0:T(8,128)(2,1)}, bf16[64,2048]{1,0:T(8,128)(2,1)}, bf16[64,2048]{1,0:T(8,128)(2,1)}, bf16[64,2048]{1,0:T(8,128)(2,1)}, bf16[64,204...) custom-call(s32[16]{0:T(128)} %pad_add_fusion.place_ref, ...), custom_call_target="tpu_custom_call" | custom-call | flops 2147483648 | bytes 7340032 | tf_op jit(solution)/shard_map/encode/pallas_call | solution.py:169
  93.2 5.2 %all-to-all-start.2 = ((f32[16,1,64]{2,1,0:T(1,128)}), f32[16,1,64]{2,1,0:T(1,128)S(1)}, u32[]{:S(2)}, u32[]{:S(2)}) async-start(f32[16,1,64]{2,1,0:T(1,128)} %bitcast.118), calls=%async_computation.2 | async-start | bytes 16384 | tf_op jit(solution)/shard_map/all_to_all | solution.py:283
  101.5 6.9 %all-to-all-done.2 = f32[16,1,64]{2,1,0:T(1,128)S(1)} async-done(((f32[16,1,64]{2,1,0:T(1,128)}), f32[16,1,64]{2,1,0:T(1,128)S(1)}, u32[]{:S(2)}, u32[]{:S(2)}) %all-to-all-start.2) | async-done | bytes 4128 | tf_op jit(solution)/shard_map/all_to_all | solution.py:283
  109.0 5.2 %all-to-all-start.3 = ((f32[16,1,256]{2,1,0:T(1,128)}), f32[16,1,256]{2,1,0:T(1,128)S(1)}, u32[]{:S(2)}, u32[]{:S(2)}) async-start(f32[16,1,256]{2,1,0:T(1,128)} %reshape.142), calls=%async_computation.3 | async-start | bytes 32768 | tf_op jit(solution)/shard_map/all_to_all | solution.py:285
  115.4 2.4 %collective-permute-start.15 = (bf16[64,512]{1,0:T(8,128)(2,1)}, bf16[64,512]{1,0:T(8,128)(2,1)}, u32[]{:S(2)}, u32[]{:S(2)}) collective-permute-start(bf16[64,512]{1,0:T(8,128)(2,1)} %get-tuple-element.26), channel_id=1, source_target_pairs={{0,8},{1,9},{2,10},{3,11},{4,12},{5,13},{6,14},{7,15},{8,0},{9,1},... | collective-permute-start | bytes 196616 | tf_op jit(solution)/shard_map/ppermute | solution.py:27
  117.8 1.8 %collective-permute-start.16 = (bf16[64,512]{1,0:T(8,128)(2,1)}, bf16[64,512]{1,0:T(8,128)(2,1)}, u32[]{:S(2)}, u32[]{:S(2)}) collective-permute-start(bf16[64,512]{1,0:T(8,128)(2,1)} %get-tuple-element.25), channel_id=1, source_target_pairs={{0,12},{1,13},{2,14},{3,15},{4,0},{5,1},{6,2},{7,3},{8,4},{9,5},{1... | collective-permute-start | bytes 196616 | tf_op jit(solution)/shard_map/ppermute | solution.py:27
  125.8 2.7 %collective-permute-start.21 = (bf16[64,2048]{1,0:T(8,128)(2,1)S(1)}, bf16[64,2048]{1,0:T(8,128)(2,1)S(1)}, u32[]{:S(2)}, u32[]{:S(2)}) collective-permute-start(bf16[64,2048]{1,0:T(8,128)(2,1)S(1)} %add.419), channel_id=1, source_target_pairs={{0,224},{16,240},{32,128},{48,144},{64,160},{80,176},{96,192},{112... | collective-permute-start | bytes 786440 | tf_op jit(solution)/shard_map/ppermute | solution.py:37
  129.2 1.7 %fusion.13 = bf16[64,512]{1,0:T(8,128)(2,1)} fusion(bf16[64,512]{1,0:T(8,128)(2,1)} %collective-permute-done.16, bf16[64,512]{1,0:T(8,128)(2,1)} %collective-permute-done.15, bf16[64,512]{1,0:T(8,128)(2,1)} %collective-permute-done.14, bf16[64,512]{1,0:T(8,128)(2,1)S(1)} %add_convert_fusion, f32[64]{0:T(128)S(1)} %get-tuple-element.40, ...), kind=kLoop, calls=%fused_computation.22 | loop fusion | flops 458752 | bytes 394244 | tf_op jit(solution)/shard_map/convert_element_type | solution.py:302
  130.9 5.3 %collective-permute-done.18 = bf16[64,2048]{1,0:T(8,128)(2,1)S(1)} collective-permute-done((bf16[64,2048]{1,0:T(8,128)(2,1)}, bf16[64,2048]{1,0:T(8,128)(2,1)S(1)}, u32[]{:S(2)}, u32[]{:S(2)}) %collective-permute-start.18) | collective-permute-done | bytes 262176 | tf_op jit(solution)/shard_map/ppermute | solution.py:37
  136.2 4.8 %collective-permute-done.21 = bf16[64,2048]{1,0:T(8,128)(2,1)S(1)} collective-permute-done((bf16[64,2048]{1,0:T(8,128)(2,1)S(1)}, bf16[64,2048]{1,0:T(8,128)(2,1)S(1)}, u32[]{:S(2)}, u32[]{:S(2)}) %collective-permute-start.21) | collective-permute-done | bytes 262176 | tf_op jit(solution)/shard_map/ppermute | solution.py:37
  (116 shorter events, 28.3 us)
Async XLA Ops:
  0.6 22.7 %collective-permute-start.1 = (bf16[256,8192]{1,0:T(8,128)(2,1)}, bf16[256,8192]{1,0:T(8,128)(2,1)}, u32[]{:S(2)}, u32[]{:S(2)}) collective-permute-start(bf16[256,8192]{1,0:T(8,128)(2,1)} %refs_1_.1), channel_id=1, source_target_pairs={{0,16},{16,0},{32,48},{48,32},{64,80},{80,64},{96,112},{112,96},{1... | collective-permute-start | bytes 12582920 | tf_op jit(solution)/shard_map/ppermute | solution.py:23
  2.2 26.1 %all-to-all-start.1 = ((s32[16,1,64]{2,1,0:T(1,128)}), s32[16,1,64]{2,1,0:T(1,128)S(1)}, u32[]{:S(2)}, u32[]{:S(2)}) async-start(s32[16,1,64]{2,1,0:T(1,128)} %broadcast_in_dim.60), calls=%async_computation.1 | async-start | bytes 16384 | tf_op jit(solution)/shard_map/all_to_all | solution.py:221
  21.7 53.2 %collective-permute-start.11 = (bf16[512,2048]{1,0:T(8,128)(2,1)}, bf16[512,2048]{1,0:T(8,128)(2,1)}, u32[]{:S(2)}, u32[]{:S(2)}) collective-permute-start(bf16[512,2048]{1,0:T(8,128)(2,1)} %refs_10_.1), channel_id=1, source_target_pairs={{0,16},{16,0},{32,48},{48,32},{64,80},{80,64},{96,112},{112,96},{1... | collective-permute-start | bytes 6291464 | tf_op jit(solution)/shard_map/ppermute | solution.py:23
  28.3 13.4 %all-to-all-start = ((bf16[8,64,512]{2,1,0:T(8,128)(2,1)}), bf16[8,64,512]{2,1,0:T(8,128)(2,1)S(1)}, u32[]{:S(2)}, u32[]{:S(2)}) async-start(bf16[8,64,512]{2,1,0:T(8,128)(2,1)} %project.1), calls=%async_computation | async-start | bytes 1048576 | tf_op jit(solution)/shard_map/all_to_all | solution.py:231
  43.1 10.6 %collective-permute-start.3 = (bf16[64,1024]{1,0:T(8,128)(2,1)S(1)}, bf16[64,1024]{1,0:T(8,128)(2,1)S(1)}, u32[]{:S(2)}, u32[]{:S(2)}) collective-permute-start(bf16[64,1024]{1,0:T(8,128)(2,1)S(1)} %pad_maximum_fusion), channel_id=1, source_target_pairs={{0,1},{2,3},{4,5},{6,7},{8,9},{10,11},{12,13},{14,15},{17,16},{19,... | collective-permute-start | bytes 393224 | tf_op jit(solution)/shard_map/ppermute | solution.py:246
  51.5 16.3 %collective-permute-start.12 = (bf16[512,512]{1,0:T(8,128)(2,1)S(1)}, bf16[512,512]{1,0:T(8,128)(2,1)S(1)}, u32[]{:S(2)}, u32[]{:S(2)}) collective-permute-start(bf16[512,512]{1,0:T(8,128)(2,1)S(1)} %slice.39), channel_id=1, source_target_pairs={{0,2},{1,3},{2,0},{3,1},{4,6},{5,7},{6,4},{7,5},{8,10},{9,11},{10,... | collective-permute-start | bytes 1572872 | tf_op jit(solution)/shard_map/ppermute | solution.py:247
  53.8 18.2 %collective-permute-start.5 = (bf16[64,1024]{1,0:T(8,128)(2,1)S(1)}, bf16[64,1024]{1,0:T(8,128)(2,1)}, u32[]{:S(2)}, u32[]{:S(2)}) collective-permute-start(bf16[64,1024]{1,0:T(8,128)(2,1)S(1)} %broadcast_select_fusion.refs_0_), channel_id=1, source_target_pairs={{0,12},{1,13},{2,14},{3,15},{4,0},{5,1},{6,2},{7,3},{8,4},{9,5},{1... | collective-permute-start | bytes 393224 | tf_op jit(solution)/shard_map/ppermute | solution.py:27
  56.5 21.3 %collective-permute-start.8 = (bf16[64,1024]{1,0:T(8,128)(2,1)S(1)}, bf16[64,1024]{1,0:T(8,128)(2,1)}, u32[]{:S(2)}, u32[]{:S(2)}) collective-permute-start(bf16[64,1024]{1,0:T(8,128)(2,1)S(1)} %broadcast_select_fusion.refs_0_), channel_id=1, source_target_pairs={{0,4},{1,5},{2,6},{3,7},{4,8},{5,9},{6,10},{7,11},{8,12},{9,13},{1... | collective-permute-start | bytes 393224 | tf_op jit(solution)/shard_map/ppermute | solution.py:27
  56.8 21.1 %collective-permute-start.10 = (bf16[64,1024]{1,0:T(8,128)(2,1)S(1)}, bf16[64,1024]{1,0:T(8,128)(2,1)S(1)}, u32[]{:S(2)}, u32[]{:S(2)}) collective-permute-start(bf16[64,1024]{1,0:T(8,128)(2,1)S(1)} %broadcast_select_fusion.refs_0_), channel_id=1, source_target_pairs={{0,2},{1,3},{2,4},{3,5},{4,6},{5,7},{6,8},{7,9},{8,10},{9,11},{10,... | collective-permute-start | bytes 393224 | tf_op jit(solution)/shard_map/ppermute | solution.py:27
  67.8 11.7 %collective-permute-start.4 = (bf16[64,1024]{1,0:T(8,128)(2,1)S(1)}, bf16[64,1024]{1,0:T(8,128)(2,1)}, u32[]{:S(2)}, u32[]{:S(2)}) collective-permute-start(bf16[64,1024]{1,0:T(8,128)(2,1)S(1)} %broadcast_select_fusion.refs_0_), channel_id=1, source_target_pairs={{0,14},{1,15},{2,0},{3,1},{4,2},{5,3},{6,4},{7,5},{8,6},{9,7},{10,... | collective-permute-start | bytes 393224 | tf_op jit(solution)/shard_map/ppermute | solution.py:27
  72.0 7.5 %collective-permute-start.6 = (bf16[64,1024]{1,0:T(8,128)(2,1)}, bf16[64,1024]{1,0:T(8,128)(2,1)}, u32[]{:S(2)}, u32[]{:S(2)}) collective-permute-start(bf16[64,1024]{1,0:T(8,128)(2,1)} %collective-permute-done.5.refs_2_), channel_id=1, source_target_pairs={{0,14},{1,15},{2,0},{3,1},{4,2},{5,3},{6,4},{7,5},{8,6},{9,7},{10,... | collective-permute-start | bytes 393224 | tf_op jit(solution)/shard_map/ppermute | solution.py:27
  77.9 20.5 %collective-permute-start.13 = (bf16[256,512]{1,0:T(8,128)(2,1)S(1)}, bf16[256,512]{1,0:T(8,128)(2,1)}, u32[]{:S(2)}, u32[]{:S(2)}) collective-permute-start(bf16[256,512]{1,0:T(8,128)(2,1)S(1)} %slice.41), channel_id=1, source_target_pairs={{0,1},{1,0},{2,3},{3,2},{4,5},{5,4},{6,7},{7,6},{8,9},{9,8},{10,11... | collective-permute-start | bytes 786440 | tf_op jit(solution)/shard_map/ppermute | solution.py:256
  93.2 15.2 %all-to-all-start.2 = ((f32[16,1,64]{2,1,0:T(1,128)}), f32[16,1,64]{2,1,0:T(1,128)S(1)}, u32[]{:S(2)}, u32[]{:S(2)}) async-start(f32[16,1,64]{2,1,0:T(1,128)} %bitcast.118), calls=%async_computation.2 | async-start | bytes 16384 | tf_op jit(solution)/shard_map/all_to_all | solution.py:283
  99.3 21.6 %collective-permute-start.20 = (bf16[64,2048]{1,0:T(8,128)(2,1)}, bf16[64,2048]{1,0:T(8,128)(2,1)S(1)}, u32[]{:S(2)}, u32[]{:S(2)}) collective-permute-start(bf16[64,2048]{1,0:T(8,128)(2,1)} %get-tuple-element.17), channel_id=1, source_target_pairs={{0,96},{16,112},{32,0},{48,16},{64,32},{80,48},{96,64},{112,80},{1... | collective-permute-start | bytes 786440 | tf_op jit(solution)/shard_map/ppermute | solution.py:37
  100.8 22.7 %collective-permute-start.22 = (bf16[64,2048]{1,0:T(8,128)(2,1)}, bf16[64,2048]{1,0:T(8,128)(2,1)S(1)}, u32[]{:S(2)}, u32[]{:S(2)}) collective-permute-start(bf16[64,2048]{1,0:T(8,128)(2,1)} %get-tuple-element.19), channel_id=1, source_target_pairs={{0,32},{16,48},{32,64},{48,80},{64,96},{80,112},{96,0},{112,16},{1... | collective-permute-start | bytes 786440 | tf_op jit(solution)/shard_map/ppermute | solution.py:37
  109.0 10.6 %all-to-all-start.3 = ((f32[16,1,256]{2,1,0:T(1,128)}), f32[16,1,256]{2,1,0:T(1,128)S(1)}, u32[]{:S(2)}, u32[]{:S(2)}) async-start(f32[16,1,256]{2,1,0:T(1,128)} %reshape.142), calls=%async_computation.3 | async-start | bytes 32768 | tf_op jit(solution)/shard_map/all_to_all | solution.py:285
  114.9 10.3 %collective-permute-start.14 = (bf16[64,512]{1,0:T(8,128)(2,1)}, bf16[64,512]{1,0:T(8,128)(2,1)}, u32[]{:S(2)}, u32[]{:S(2)}) collective-permute-start(bf16[64,512]{1,0:T(8,128)(2,1)} %get-tuple-element.24), channel_id=1, source_target_pairs={{0,4},{1,5},{2,6},{3,7},{4,8},{5,9},{6,10},{7,11},{8,12},{9,13},{1... | collective-permute-start | bytes 196616 | tf_op jit(solution)/shard_map/ppermute | solution.py:27
  115.4 10.3 %collective-permute-start.15 = (bf16[64,512]{1,0:T(8,128)(2,1)}, bf16[64,512]{1,0:T(8,128)(2,1)}, u32[]{:S(2)}, u32[]{:S(2)}) collective-permute-start(bf16[64,512]{1,0:T(8,128)(2,1)} %get-tuple-element.26), channel_id=1, source_target_pairs={{0,8},{1,9},{2,10},{3,11},{4,12},{5,13},{6,14},{7,15},{8,0},{9,1},... | collective-permute-start | bytes 196616 | tf_op jit(solution)/shard_map/ppermute | solution.py:27
  117.8 10.7 %collective-permute-start.16 = (bf16[64,512]{1,0:T(8,128)(2,1)}, bf16[64,512]{1,0:T(8,128)(2,1)}, u32[]{:S(2)}, u32[]{:S(2)}) collective-permute-start(bf16[64,512]{1,0:T(8,128)(2,1)} %get-tuple-element.25), channel_id=1, source_target_pairs={{0,12},{1,13},{2,14},{3,15},{4,0},{5,1},{6,2},{7,3},{8,4},{9,5},{1... | collective-permute-start | bytes 196616 | tf_op jit(solution)/shard_map/ppermute | solution.py:27
  121.0 9.9 %collective-permute-start.17 = (bf16[64,2048]{1,0:T(8,128)(2,1)}, bf16[64,2048]{1,0:T(8,128)(2,1)S(1)}, u32[]{:S(2)}, u32[]{:S(2)}) collective-permute-start(bf16[64,2048]{1,0:T(8,128)(2,1)} %get-tuple-element.13), channel_id=1, source_target_pairs={{0,128},{16,144},{32,160},{48,176},{64,192},{80,208},{96,224},{112... | collective-permute-start | bytes 786440 | tf_op jit(solution)/shard_map/ppermute | solution.py:37
  123.5 12.6 %collective-permute-start.18 = (bf16[64,2048]{1,0:T(8,128)(2,1)}, bf16[64,2048]{1,0:T(8,128)(2,1)S(1)}, u32[]{:S(2)}, u32[]{:S(2)}) collective-permute-start(bf16[64,2048]{1,0:T(8,128)(2,1)} %get-tuple-element.14), channel_id=1, source_target_pairs={{0,160},{16,176},{32,192},{48,208},{64,224},{80,240},{96,128},{112... | collective-permute-start | bytes 786440 | tf_op jit(solution)/shard_map/ppermute | solution.py:37
  125.2 11.0 %collective-permute-start.19 = (bf16[64,2048]{1,0:T(8,128)(2,1)}, bf16[64,2048]{1,0:T(8,128)(2,1)S(1)}, u32[]{:S(2)}, u32[]{:S(2)}) collective-permute-start(bf16[64,2048]{1,0:T(8,128)(2,1)} %get-tuple-element.15), channel_id=1, source_target_pairs={{0,96},{16,112},{32,0},{48,16},{64,32},{80,48},{96,64},{112,80},{1... | collective-permute-start | bytes 786440 | tf_op jit(solution)/shard_map/ppermute | solution.py:37
  125.8 15.1 %collective-permute-start.21 = (bf16[64,2048]{1,0:T(8,128)(2,1)S(1)}, bf16[64,2048]{1,0:T(8,128)(2,1)S(1)}, u32[]{:S(2)}, u32[]{:S(2)}) collective-permute-start(bf16[64,2048]{1,0:T(8,128)(2,1)S(1)} %add.419), channel_id=1, source_target_pairs={{0,224},{16,240},{32,128},{48,144},{64,160},{80,176},{96,192},{112... | collective-permute-start | bytes 786440 | tf_op jit(solution)/shard_map/ppermute | solution.py:37
  128.5 12.4 %collective-permute-start.23 = (bf16[64,2048]{1,0:T(8,128)(2,1)S(1)}, bf16[64,2048]{1,0:T(8,128)(2,1)S(1)}, u32[]{:S(2)}, u32[]{:S(2)}) collective-permute-start(bf16[64,2048]{1,0:T(8,128)(2,1)S(1)} %add.421), channel_id=1, source_target_pairs={{0,32},{16,48},{32,64},{48,80},{64,96},{80,112},{96,0},{112,16},{1... | collective-permute-start | bytes 786440 | tf_op jit(solution)/shard_map/ppermute | solution.py:37
  (19 other events, 345.6 us)

commit v4 on v3

--- a/solution.py
+++ b/solution.py
@@ -27,6 +27,14 @@
     return lax.ppermute(
         value, "grp", grp_moves(lambda z, plane: (z - ahead) % 8 * 2 + plane)
     )
+
+
+def flip_z(value, k):
+    return lax.ppermute(value, "grp", grp_moves(lambda z, plane: (z ^ k) * 2 + plane))
+
+
+def flip_plane(value):
+    return lax.ppermute(value, "grp", grp_moves(lambda z, plane: z * 2 + 1 - plane))
 
 
 def chip_at(chip, dx, dy):
@@ -113,12 +121,14 @@
 
 
 def encode_kernel(place_ref, *refs):
-    block_refs, (want_ref, bias_ref, w_mine_ref, w_other_ref) = refs[:8], refs[8:12]
-    out_refs, now_ref = refs[12:20], refs[20]
-    x_ref, held_ref, sems = refs[21:]
+    block_refs, (bias_ref, w_mine_ref, w_other_ref) = refs[:8], refs[8:11]
+    out_refs, table_ref = refs[11:19], refs[19]
+    x_ref, held_ref, sems = refs[20:]
+    f32 = jnp.float32
     step = pl.program_id(0)
     half, tile = w_mine_ref.shape
     rows = out_refs[0].shape[0]
+    lanes = held_ref.shape[1]
 
     @pl.when(step == 0)
     def _():
@@ -136,35 +146,48 @@
         for copy in copies:
             copy.wait()
 
-    part = mm(x_ref[:, :half], w_mine_ref[...]) + mm(x_ref[:, half:], w_other_ref[...])
+    part = mm(x_ref[:, :half], w_mine_ref[...]) + mm(x_ref[:, half : 2 * half], w_other_ref[...])
     part = part.astype(jnp.bfloat16)
     for slot in range(8):
         out_refs[slot][...] = part[slot * rows : (slot + 1) * rows]
-    lanes = held_ref.shape[1]
-    want = want_ref[...] - step * tile
+    first_id = (
+        x_ref[:, 2 * half : 2 * half + 1].astype(f32) * 256.0
+        + x_ref[:, 2 * half + 1 : 2 * half + 2].astype(f32)
+    ).astype(jnp.int32)
+    want = (first_id & (QUARTER - 1)) - place_ref[16] - step * tile
     for at in range(0, tile, lanes):
-        piece = part[:, at : at + lanes].astype(jnp.float32) + bias_ref[:, at : at + lanes]
+        piece = part[:, at : at + lanes].astype(f32) + bias_ref[:, at : at + lanes]
         column = lax.broadcasted_iota(jnp.int32, piece.shape, 1) + at
         held_ref[...] += jnp.where(column == want, piece, 0.0)
 
     @pl.when(step == pl.num_programs(0) - 1)
     def _():
-        total = lax.dot_general(
-            jnp.ones((8, lanes), jnp.float32),
-            held_ref[...],
-            (((1,), (1,)), ((), ())),
-            precision=lax.Precision.HIGHEST,
-            preferred_element_type=jnp.float32,
+        over_lanes = lambda a, b, precision: lax.dot_general(
+            a, b, (((1,), (1,)), ((), ())), precision=precision, preferred_element_type=f32
         )
-        now_ref[...] = jnp.zeros_like(now_ref)
+        now = over_lanes(jnp.ones((8, lanes), f32), held_ref[...], lax.Precision.HIGHEST)[:1]
+        shape = (16, lanes)
+        pick = lax.broadcasted_iota(jnp.int32, shape, 0) == lax.broadcasted_iota(jnp.int32, shape, 1)
+        pick = pick.astype(f32).astype(jnp.bfloat16)
+        extra = over_lanes(pick, x_ref[:, 2 * half :], None)
+        ids = (extra[0:1] * 256.0 + extra[1:2]).astype(jnp.int32)
+        local = ((ids & (QUARTER - 1)) - place_ref[16]).astype(f32)
+        index = (place_ref[17] - (ids >> 13)) & 3
+        value = jnp.zeros_like(local)
+        for c in range(4):
+            whole = extra[2 + 3 * c : 3 + 3 * c] + extra[3 + 3 * c : 4 + 3 * c]
+            value += jnp.where(index == c, whole + extra[4 + 3 * c : 5 + 3 * c], 0.0)
         for slot in range(8):
-            now_ref[pl.ds(place_ref[8 + slot], 1), :] = total[:1, slot * rows : (slot + 1) * rows]
-
-
-def encode(block, place, want, bias, w_mine, w_other):
+            for at, source in enumerate((now, local, value)):
+                table_ref[pl.ds(8 * at + place_ref[8 + slot], 1), :] = source[
+                    :, slot * rows : (slot + 1) * rows
+                ]
+
+
+def encode(block, place, bias, w_mine, w_other):
     rows, depth = block[0].shape
     count = 8 * rows
-    span = w_mine.shape[1]
+    half, span = w_mine.shape
     tile = 512
     return pl.pallas_call(
         encode_kernel,
@@ -173,13 +196,12 @@
             grid=(span // tile,),
             in_specs=[pl.BlockSpec(memory_space=pl.ANY)] * 8
             + [
-                pl.BlockSpec((count, 1), lambda i, place: (0, 0)),
                 pl.BlockSpec((1, tile), lambda i, place: (0, i)),
-                pl.BlockSpec((depth // 2, tile), lambda i, place: (0, i)),
-                pl.BlockSpec((depth // 2, tile), lambda i, place: (0, i)),
+                pl.BlockSpec((half, tile), lambda i, place: (0, i)),
+                pl.BlockSpec((half, tile), lambda i, place: (0, i)),
             ],
             out_specs=[pl.BlockSpec((rows, tile), lambda i, place: (0, i))] * 8
-            + [pl.BlockSpec((16, rows), lambda i, place: (0, 0))],
+            + [pl.BlockSpec((24, rows), lambda i, place: (0, 0))],
             scratch_shapes=[
                 pltpu.VMEM((count, depth), jnp.bfloat16),
                 pltpu.VMEM((count, 128), jnp.float32),
@@ -187,14 +209,14 @@
             ],
         ),
         out_shape=[jax.ShapeDtypeStruct((rows, span), jnp.bfloat16)] * 8
-        + [jax.ShapeDtypeStruct((16, rows), jnp.float32)],
+        + [jax.ShapeDtypeStruct((24, rows), jnp.float32)],
         cost_estimate=pl.CostEstimate(
-            flops=2 * count * depth * span,
-            bytes_accessed=2 * (depth * span + count * (depth + span)),
+            flops=4 * count * half * span,
+            bytes_accessed=2 * (2 * half * span + count * (depth + span)),
             transcendentals=0,
         ),
         name="encode",
-    )(place, *block, want, bias, w_mine, w_other)
+    )(place, *block, bias, w_mine, w_other)
 
 
 def per_device(
@@ -216,11 +238,8 @@
     z, plane = grp_rank // 2, grp_rank % 2
     rows, width = resid_in.shape
     span = enc_weight.shape[1]
-    my_quarter, parity = z // 2, z % 2
-
-    ids = lax.all_to_all(
-        jnp.broadcast_to(clamp_ids[:, 0].reshape(1, 1, rows), (16, 1, rows)), "grp", 0, 0, tiled=True
-    ).reshape(16, rows)
+    my_quarter = z // 2
+
     out_other = swap_core(out_weight)
     enc_other = swap_core(enc_weight)
 
@@ -231,20 +250,19 @@
     arrived = lax.all_to_all(part, "tp", 0, 0, axis_index_groups=groups, tiled=True)
     resid_mid = (resid_in.astype(f32) + jnp.sum(arrived.astype(f32), axis=0)).astype(bf16)
 
-    want = ids % QUARTER + my_quarter * QUARTER - grp_rank * span
-    ordered = want.reshape(4, 2, 2, rows).transpose(1, 2, 0, 3)
-    ordered = jnp.where(parity == 1, ordered, ordered[::-1])
-    ordered = jnp.where(plane == 1, ordered, ordered[:, ::-1]).reshape(16 * rows)
-    hits = (ordered[:, None] == jnp.arange(span, dtype=jnp.int32)[None, :]).astype(bf16)
-    found = mm(hits, dec_weight).astype(bf16)
-
     mid_other = swap_core(resid_mid)
-    both = jnp.concatenate([resid_mid, mid_other], axis=1)
+    coarse = lambda value: lax.reduce_precision(value, 8, 7)
+    high = coarse(clamp_values)
+    middle = coarse(clamp_values - high)
+    parts = jnp.stack([high, middle, clamp_values - high - middle], axis=2).reshape(rows, 12)
+    first_id = clamp_ids[:, :1]
+    id_parts = jnp.concatenate([first_id // 256, first_id % 256], axis=1).astype(f32)
+    extra = jnp.concatenate([id_parts, parts, jnp.zeros((rows, 114), f32)], axis=1).astype(bf16)
+    both = jnp.concatenate([resid_mid, mid_other, extra], axis=1)
     cross = [
         (t * 16 + z_ * 2 + t % 2, t * 16 + z_ * 2 + 1 - t % 2) for t in range(16) for z_ in range(8)
     ]
     crossed = lax.ppermute(both, ("tp", "grp"), cross)
-    near = lax.ppermute(found[: 8 * rows], "grp", grp_moves(lambda z_, s: (z_ ^ 1) * 2 + s))
     block = [None] * 8
     block[0] = jnp.where(core == plane, both, crossed)
     for k, source, step in (
@@ -252,25 +270,46 @@
         (3, 2, 1), (5, 6, 7), (4, 2, 2),
     ):
         block[k] = from_z(block[source], step)
-    found = found[8 * rows :] + near
-    near = lax.ppermute(found[: 4 * rows], "grp", grp_moves(lambda z_, s: z_ * 2 + 1 - s))
-    found = (found[4 * rows :] + near).reshape(4, rows, width)
-    dec_rows = [lax.dynamic_index_in_dim(found, my_quarter, 0, keepdims=False)]
-    for k in (1, 2, 3):
-        give = lax.dynamic_index_in_dim(found, (my_quarter + k) % 4, 0, keepdims=False)
-        dec_rows.append(from_z(give, -2 * k))
-
-    target = [chip_at(chip, s // 4, s % 4) for s in range(8)]
     ahead = (jnp.arange(8, dtype=jnp.int32) + z) % 8
     slot = (ahead // 4 + chip // 4) % 2 * 4 + (ahead - chip) % 4
-    mine = lax.dynamic_index_in_dim(want.reshape(8, 2, rows), core, 1, keepdims=False)
-    slots = jnp.concatenate([lax.dynamic_index_in_dim(mine, t, 0, keepdims=False) for t in target])
     bias = jnp.where(chip == 0, enc_bias, 0.0).reshape(1, span)
     each = jnp.arange(8, dtype=jnp.int32)
-    goal = ((chip // 4 + each // 4) % 2 * 4 + (chip + each) % 4) * 2 + core
+    goal = ((chip // 4 + each // 4) % 2 * 4 + (chip + each) % 4 - z) % 8
+    others = jnp.stack([grp_rank % 4 * span, my_quarter])
     outs = encode(
-        block, jnp.concatenate([slot, goal]), slots.reshape(8 * rows, 1), bias, enc_weight, enc_other
-    )
+        block, jnp.concatenate([slot, goal, others]), bias, enc_weight, enc_other
+    )
+
+    table = lax.all_to_all(
+        jnp.broadcast_to(outs[8][None], (16, 24, rows)), "tp", 0, 0, tiled=True
+    ).reshape(8, 2, 24, rows)
+    now = jnp.maximum(table[:, :, :8].sum(axis=0), 0.0)
+    now = lax.reduce_precision(now, 8, 7)
+    want, delta = table[0, :, 8:16], table[0, :, 16:] - now
+
+    def arrange(value):
+        value = jnp.where(plane == 1, value, value[::-1])
+        odd = value[:, 1::2]
+        odd = jnp.where(z % 2 == 0, odd, jnp.concatenate([odd[:, 3:], odd[:, :3]], axis=1))
+        return odd.reshape(8 * rows), value[:, 0::2].reshape(8 * rows)
+
+    def decode(want, delta):
+        column = jnp.arange(span, dtype=jnp.int32)[None, :]
+        hits = jnp.where(column == want.astype(jnp.int32)[:, None], delta[:, None], 0.0)
+        return mm(hits.astype(bf16), dec_weight)
+
+    want_give, want_keep = arrange(want)
+    delta_give, delta_keep = arrange(delta)
+    give = decode(want_give, delta_give).astype(bf16)
+    near = flip_z(give, 1)
+    keep = decode(want_keep, delta_keep).astype(bf16)
+    first, last = slice(0, 4 * rows), slice(4 * rows, 8 * rows)
+    near_2 = flip_plane(keep[first] + near[first])
+    found = keep[last] + near[last] + near_2
+    edit = found[:rows].astype(f32)
+    edits = []
+    for k in (1, 2, 3):
+        edits.append(from_z(found[k * rows : (k + 1) * rows], -2 * k))
 
     relayed = to_chip(outs[6], 0, 3)
     seven = outs[7] + relayed
@@ -280,25 +319,13 @@
     for value, s in ((outs[4], 4), (outs[5], 5), (outs[3], 3), (seven, 7), (one, 1)):
         moved.append(to_chip(value, s // 4, s % 4))
 
-    held = lax.all_to_all(outs[8].reshape(16, 1, rows), "grp", 0, 0, tiled=True)
-    held = held.reshape(4, 4, rows).sum(axis=1)
-    every = lax.all_to_all(
-        jnp.broadcast_to(held[None], (16, 4, rows)), "tp", 0, 0, tiled=True
-    )
     total = outs[0].astype(f32)
     for value in moved:
         total = total + value.astype(f32)
     features = jnp.maximum(total + enc_bias, 0.0).astype(bf16)
 
-    every = every.reshape(16, 4, rows).sum(axis=0)
-    every = jnp.maximum(every, 0.0).astype(bf16).astype(f32)
-    edit = jnp.zeros((rows, width), f32)
-    own_quarter = clamp_ids // QUARTER
-    for k in range(4):
-        q = (my_quarter - k) % 4
-        value = jnp.sum(jnp.where(own_quarter == q, clamp_values, 0.0), axis=1)
-        delta = (value - lax.dynamic_index_in_dim(every, q, 0, keepdims=False)).astype(bf16)
-        edit = edit + delta.astype(f32)[:, None] * dec_rows[k].astype(f32)
+    for value in edits:
+        edit = edit + value.astype(f32)
     resid_out = (resid_mid.astype(f32) + edit).astype(bf16)
     return (resid_out, features)
 

time: 144 us -> 137 us (0.951)
  starting transfers between devices: 63 us -> 51 us
  waiting for transfers between devices: 40.5 us -> 49.4 us
  other arithmetic: 8.63 us -> 5.98 us
    all_to_all x3 -> x1, starting transfers between devices: 21.4 us -> 4.82 us  [per_device(): lax.all_to_all(jnp.broadcast_to(outs[8][None], (16, 24, rows)), 'tp', 0,...]
    ppermute x10, waiting for transfers between devices: 4.81 us -> 12 us  [from_z(): lax.ppermute(value, 'grp', grp_moves(lambda z, plane: (z - ahead) % 8 * 2...]
    ppermute x10, starting transfers between devices: 19 us -> 23.4 us  [from_z(): lax.ppermute(value, 'grp', grp_moves(lambda z, plane: (z - ahead) % 8 * 2...]
    ppermute x2, waiting for transfers between devices: 9.73 us -> 12.4 us  [the longest x1 9.25 us: flip_z(): lax.ppermute(value, 'grp', grp_moves(lambda z, plane: (z ^ k) * 2 + plane))]
    ppermute x1, waiting for transfers between devices: 0.01 us -> 2.59 us  [per_device(): crossed = lax.ppermute(both, ('tp', 'grp'), cross)]
    all_to_all x3 -> x1, waiting for transfers between devices: 6.87 us -> 4.78 us  [per_device(): lax.all_to_all(jnp.broadcast_to(outs[8][None], (16, 24, rows)), 'tp', 0,...]
    ppermute x7, waiting for transfers between devices: 10 us -> 8.1 us  [to_chip(): lax.ppermute(value, 'tp', tp_moves(lambda chip, core: chip_at(chip, dx, d...]
    dot_general x1 -> x2, matrix products: 2.37 us -> 3.37 us  [mm(): return jnp.dot(a, b, preferred_element_type=jnp.float32)]
  transfers between devices with their start and end apart: 28 -> 26, of which waited for: 8 -> 14; matrix products, arithmetic and copies ran while one was open for 15% -> 10% of each run, Pallas kernels for 9% -> 3%
where the time goes in v4:
time: 137 us; the launch traced here: 135 us
  starting transfers between devices  51 us (37%)
  waiting for transfers between devices  49.4 us (36%)
  Pallas kernels  12.8 us (9%)
  matrix products  8.75 us (6%)
  local copies, waits for them, and re-layouts  6.09 us (4%)
  other arithmetic  5.98 us (4%)
    ppermute x10, starting transfers between devices, from_z(): lax.ppermute(value, 'grp', grp_moves(lambda z, plane: (z - ahead) % 8 * 2...  23.4 us
    ppermute x10, waiting for transfers between devices, from_z(): lax.ppermute(value, 'grp', grp_moves(lambda z, plane: (z - ahead) % 8 * 2...  12 us
    ppermute x1, waiting for transfers between devices, flip_z(): lax.ppermute(value, 'grp', grp_moves(lambda z, plane: (z ^ k) * 2 + plane))  9.25 us
    pallas_call x1, Pallas kernels, encode(): pl.pallas_call(encode_kernel, grid_spec=pltpu.PrefetchScalarGridSpec(num_...  8.43 us
    ppermute x7, starting transfers between devices, to_chip(): lax.ppermute(value, 'tp', tp_moves(lambda chip, core: chip_at(chip, dx, d...  8.41 us
    ppermute x7, waiting for transfers between devices, to_chip(): lax.ppermute(value, 'tp', tp_moves(lambda chip, core: chip_at(chip, dx, d...  8.1 us
    all_to_all x1, waiting for transfers between devices, per_device(): lax.all_to_all(part, 'tp', 0, 0, axis_index_groups=groups, tiled=True)  7.68 us
    all_to_all x1, starting transfers between devices, per_device(): lax.all_to_all(part, 'tp', 0, 0, axis_index_groups=groups, tiled=True)  5.97 us
  transfers between devices with their start and end apart: 26, of which 14 were waited for; matrix products, arithmetic and copies ran while one was open for 10% of the time, Pallas kernels for 3%

profile of v4, /device:TPU:8, one launch (start us, length us, event | category | flops | bytes accessed | tf_op | source)
XLA Modules:
  0.0 135.1 jit_solution(2559011814210576728)
XLA Ops:
  3.6 2.9 %select_reduce_fusion = (f32[64,2]{1,0:T(8,128)S(1)}, f32[64,2,128]{2,1,0:T(2,128)S(1)}) fusion(pred[64,128]{1,0:T(8,128)(4,1)S(1)} %iota_compare_fusion.2, bf16[64,2,128]{2,1,0:T(2,128)(2,1)S(1)} %reshape.73, bf16[2,64,1,128,128]{4,3,1,2,0:T(8,128)(2,1)} %bitcast.68), kind=kOutput, calls=%fused_computation.32 | convolution fusion | flops 4243328 | bytes 2204160 | tf_op jit(solution)/shard_map/shd,spd->shp/dot_general | solution.py:61
  6.8 2.3 %fusion.15 = bf16[64,2,128]{2,1,0:T(2,128)(2,1)S(1)} fusion(bf16[2,64,1,128,128]{4,3,1,2,0:T(8,128)(2,1)} %bitcast.69, f32[64,2]{1,0:T(8,128)S(1)} %get-tuple-element.28, f32[64,128]{1,0:T(8,128)S(1)} %bitcast.64, f32[64,2]{1,0:T(8,128)S(1)} %convert_element_type.109, f32[64,2,128]{2,1,0:T(2,128)S(1)} %get-tuple-element.33, ...), kind=kOutput, calls=%fused_computation.21 | convolution fusion | flops 4308992 | bytes 2237952 | tf_op jit(solution)/shard_map/shp,spd->shd/dot_general | solution.py:75
  11.0 4.4 %project.1 = bf16[8,64,512]{2,1,0:T(8,128)(2,1)} custom-call(s32[1]{0:T(128)} %bitcast.core_ref, bf16[64,256]{1,0:T(8,128)(2,1)} %bitcast.59, bf16[64,256]{1,0:T(8,128)(2,1)} %copy-done.7, bf16[256,8192]{1,0:T(8,128)(2,1)} %refs_1_.1, bf16[256,8192]{1,0:T(8,128)(2,1)} %refs_1_.1, bf16[256,8192]{1,0:T(8,128)(2,1)} %collective-permute-done.1.refs_2_.refs_3_, ...), custom_call_target="tpu_custom_call" | custom-call | flops 268435456 | bytes 4194304 | tf_op jit(solution)/shard_map/project/pallas_call | solution.py:105
  15.4 6.0 %all-to-all-start = ((bf16[8,64,512]{2,1,0:T(8,128)(2,1)}), bf16[8,64,512]{2,1,0:T(8,128)(2,1)S(1)}, u32[]{:S(2)}, u32[]{:S(2)}) async-start(bf16[8,64,512]{2,1,0:T(8,128)(2,1)} %project.1), calls=%async_computation | async-start | bytes 1048576 | tf_op jit(solution)/shard_map/all_to_all | solution.py:250
  22.2 7.7 %all-to-all-done = bf16[8,64,512]{2,1,0:T(8,128)(2,1)S(1)} async-done(((bf16[8,64,512]{2,1,0:T(8,128)(2,1)}), bf16[8,64,512]{2,1,0:T(8,128)(2,1)S(1)}, u32[]{:S(2)}, u32[]{:S(2)}) %all-to-all-start) | async-done | bytes 524320 | tf_op jit(solution)/shard_map/all_to_all | solution.py:250
  31.5 4.6 %collective-permute-start.3 = (bf16[64,1152]{1,0:T(8,128)(2,1)S(1)}, bf16[64,1152]{1,0:T(8,128)(2,1)S(1)}, u32[]{:S(2)}, u32[]{:S(2)}) collective-permute-start(bf16[64,1152]{1,0:T(8,128)(2,1)S(1)} %concatenate.20), channel_id=1, source_target_pairs={{0,1},{2,3},{4,5},{6,7},{8,9},{10,11},{12,13},{14,15},{17,16},{19,... | collective-permute-start | bytes 442376 | tf_op jit(solution)/shard_map/ppermute | solution.py:265
  36.2 2.6 %collective-permute-done.3 = bf16[64,1152]{1,0:T(8,128)(2,1)S(1)} collective-permute-done((bf16[64,1152]{1,0:T(8,128)(2,1)S(1)}, bf16[64,1152]{1,0:T(8,128)(2,1)S(1)}, u32[]{:S(2)}, u32[]{:S(2)}) %collective-permute-start.3) | collective-permute-done | bytes 147488 | tf_op jit(solution)/shard_map/ppermute | solution.py:265
  38.8 6.4 %collective-permute-start.5 = (bf16[64,1152]{1,0:T(8,128)(2,1)S(1)}, bf16[64,1152]{1,0:T(8,128)(2,1)S(1)}, u32[]{:S(2)}, u32[]{:S(2)}) collective-permute-start(bf16[64,1152]{1,0:T(8,128)(2,1)S(1)} %broadcast_select_fusion.refs_0_), channel_id=1, source_target_pairs={{0,12},{1,13},{2,14},{3,15},{4,0},{5,1},{6,2},{7,3},{8,4},{9,5},{1... | collective-permute-start | bytes 442376 | tf_op jit(solution)/shard_map/ppermute | solution.py:27
  46.8 2.7 %collective-permute-start.4 = (bf16[64,1152]{1,0:T(8,128)(2,1)S(1)}, bf16[64,1152]{1,0:T(8,128)(2,1)S(1)}, u32[]{:S(2)}, u32[]{:S(2)}) collective-permute-start(bf16[64,1152]{1,0:T(8,128)(2,1)S(1)} %broadcast_select_fusion.refs_0_), channel_id=1, source_target_pairs={{0,14},{1,15},{2,0},{3,1},{4,2},{5,3},{6,4},{7,5},{8,6},{9,7},{10,... | collective-permute-start | bytes 442376 | tf_op jit(solution)/shard_map/ppermute | solution.py:27
  49.5 2.8 %collective-permute-done.5.refs_2_ = bf16[64,1152]{1,0:T(8,128)(2,1)S(1)} collective-permute-done((bf16[64,1152]{1,0:T(8,128)(2,1)S(1)}, bf16[64,1152]{1,0:T(8,128)(2,1)S(1)}, u32[]{:S(2)}, u32[]{:S(2)}) %collective-permute-start.5) | collective-permute-done | bytes 147488 | tf_op jit(solution)/shard_map/ppermute | solution.py:27
  52.3 2.7 %collective-permute-start.6 = (bf16[64,1152]{1,0:T(8,128)(2,1)S(1)}, bf16[64,1152]{1,0:T(8,128)(2,1)S(1)}, u32[]{:S(2)}, u32[]{:S(2)}) collective-permute-start(bf16[64,1152]{1,0:T(8,128)(2,1)S(1)} %collective-permute-done.5.refs_2_), channel_id=1, source_target_pairs={{0,14},{1,15},{2,0},{3,1},{4,2},{5,3},{6,4},{7,5},{8,6},{9,7},{10,... | collective-permute-start | bytes 442376 | tf_op jit(solution)/shard_map/ppermute | solution.py:27
  55.0 2.1 %collective-permute-start.7 = (bf16[64,1152]{1,0:T(8,128)(2,1)S(1)}, bf16[64,1152]{1,0:T(8,128)(2,1)S(1)}, u32[]{:S(2)}, u32[]{:S(2)}) collective-permute-start(bf16[64,1152]{1,0:T(8,128)(2,1)S(1)} %collective-permute-done.5.refs_2_), channel_id=1, source_target_pairs={{0,12},{1,13},{2,14},{3,15},{4,0},{5,1},{6,2},{7,3},{8,4},{9,5},{1... | collective-permute-start | bytes 442376 | tf_op jit(solution)/shard_map/ppermute | solution.py:27
  60.0 4.5 %collective-permute-done.7.refs_4_ = bf16[64,1152]{1,0:T(8,128)(2,1)S(1)} collective-permute-done((bf16[64,1152]{1,0:T(8,128)(2,1)S(1)}, bf16[64,1152]{1,0:T(8,128)(2,1)S(1)}, u32[]{:S(2)}, u32[]{:S(2)}) %collective-permute-start.7) | collective-permute-done | bytes 147488 | tf_op jit(solution)/shard_map/ppermute | solution.py:27
  65.2 8.4 %encode.1 = (bf16[64,2048]{1,0:T(8,128)(2,1)}, bf16[64,2048]{1,0:T(8,128)(2,1)}, bf16[64,2048]{1,0:T(8,128)(2,1)}, bf16[64,2048]{1,0:T(8,128)(2,1)}, bf16[64,204...) custom-call(s32[18]{0:T(128)} %pad_add_fusion.place_ref, ...), custom_call_target="tpu_custom_call" | custom-call | flops 2147483648 | bytes 7471104 | tf_op jit(solution)/shard_map/encode/pallas_call | solution.py:192
  75.2 4.8 %all-to-all-start.1 = ((f32[16,1,1536]{2,1,0:T(1,128)}), f32[16,1,1536]{2,1,0:T(1,128)S(1)}, u32[]{:S(2)}, u32[]{:S(2)}) async-start(f32[16,1,1536]{2,1,0:T(1,128)} %reshape.81), calls=%async_computation.1 | async-start | bytes 196608 | tf_op jit(solution)/shard_map/all_to_all | solution.py:283
  80.0 4.8 %all-to-all-done.1 = f32[16,1,1536]{2,1,0:T(1,128)S(1)} async-done(((f32[16,1,1536]{2,1,0:T(1,128)}), f32[16,1,1536]{2,1,0:T(1,128)S(1)}, u32[]{:S(2)}, u32[]{:S(2)}) %all-to-all-start.1) | async-done | bytes 98336 | tf_op jit(solution)/shard_map/all_to_all | solution.py:283
  86.6 2.1 %fusion.10 = bf16[512,512]{1,0:T(8,128)(2,1)} fusion(bf16[2048,512]{1,0:T(8,128)(2,1)S(1)} %copy-done, bf16[512]{0:T(512)(128)(2,1)S(1)} %broadcast_in_dim.74, s32[512]{0:T(512)S(1)} %convert_element_type.122), kind=kOutput, calls=%fused_computation.16 | convolution fusion | flops 1076101120 | bytes 2624512 | tf_op jit(solution)/shard_map/dot_general | solution.py:90
  93.6 9.3 %collective-permute-done.12 = bf16[512,512]{1,0:T(8,128)(2,1)S(1)} collective-permute-done((bf16[512,512]{1,0:T(8,128)(2,1)}, bf16[512,512]{1,0:T(8,128)(2,1)S(1)}, u32[]{:S(2)}, u32[]{:S(2)}) %collective-permute-start.12) | collective-permute-done | bytes 524320 | tf_op jit(solution)/shard_map/ppermute | solution.py:33
  108.2 2.3 %collective-permute-start.21 = (bf16[64,2048]{1,0:T(8,128)(2,1)S(1)}, bf16[64,2048]{1,0:T(8,128)(2,1)S(1)}, u32[]{:S(2)}, u32[]{:S(2)}) collective-permute-start(bf16[64,2048]{1,0:T(8,128)(2,1)S(1)} %add.177), channel_id=1, source_target_pairs={{0,224},{16,240},{32,128},{48,144},{64,160},{80,176},{96,192},{112... | collective-permute-start | bytes 786440 | tf_op jit(solution)/shard_map/ppermute | solution.py:45
  110.5 3.2 %collective-permute-done.13 = bf16[256,512]{1,0:T(8,128)(2,1)S(1)} collective-permute-done((bf16[256,512]{1,0:T(8,128)(2,1)S(1)}, bf16[256,512]{1,0:T(8,128)(2,1)S(1)}, u32[]{:S(2)}, u32[]{:S(2)}) %collective-permute-start.13) | collective-permute-done | bytes 262176 | tf_op jit(solution)/shard_map/ppermute | solution.py:37
  114.4 3.0 %collective-permute-done.17 = bf16[64,2048]{1,0:T(8,128)(2,1)S(1)} collective-permute-done((bf16[64,2048]{1,0:T(8,128)(2,1)S(1)}, bf16[64,2048]{1,0:T(8,128)(2,1)S(1)}, u32[]{:S(2)}, u32[]{:S(2)}) %collective-permute-start.17) | collective-permute-done | bytes 262176 | tf_op jit(solution)/shard_map/ppermute | solution.py:45
  118.9 5.1 %collective-permute-done.18 = bf16[64,2048]{1,0:T(8,128)(2,1)S(1)} collective-permute-done((bf16[64,2048]{1,0:T(8,128)(2,1)S(1)}, bf16[64,2048]{1,0:T(8,128)(2,1)S(1)}, u32[]{:S(2)}, u32[]{:S(2)}) %collective-permute-start.18) | collective-permute-done | bytes 262176 | tf_op jit(solution)/shard_map/ppermute | solution.py:45
  124.0 4.2 %collective-permute-start.15 = (bf16[64,512]{1,0:T(8,128)(2,1)S(1)}, bf16[64,512]{1,0:T(8,128)(2,1)S(1)}, u32[]{:S(2)}, u32[]{:S(2)}) collective-permute-start(bf16[64,512]{1,0:T(8,128)(2,1)S(1)} %get-tuple-element.24), channel_id=1, source_target_pairs={{0,8},{1,9},{2,10},{3,11},{4,12},{5,13},{6,14},{7,15},{8,0},{9,1},... | collective-permute-start | bytes 196616 | tf_op jit(solution)/shard_map/ppermute | solution.py:27
  130.0 2.5 %collective-permute-done.15 = bf16[64,512]{1,0:T(8,128)(2,1)S(1)} collective-permute-done((bf16[64,512]{1,0:T(8,128)(2,1)S(1)}, bf16[64,512]{1,0:T(8,128)(2,1)S(1)}, u32[]{:S(2)}, u32[]{:S(2)}) %collective-permute-start.15) | collective-permute-done | bytes 65568 | tf_op jit(solution)/shard_map/ppermute | solution.py:27
  (134 shorter events, 32.8 us)
Async XLA Ops:
  0.6 9.8 %collective-permute-start.1 = (bf16[256,8192]{1,0:T(8,128)(2,1)}, bf16[256,8192]{1,0:T(8,128)(2,1)}, u32[]{:S(2)}, u32[]{:S(2)}) collective-permute-start(bf16[256,8192]{1,0:T(8,128)(2,1)} %refs_1_.1), channel_id=1, source_target_pairs={{0,16},{16,0},{32,48},{48,32},{64,80},{80,64},{96,112},{112,96},{1... | collective-permute-start | bytes 12582920 | tf_op jit(solution)/shard_map/ppermute | solution.py:23
  9.6 45.4 %collective-permute-start.11 = (bf16[512,2048]{1,0:T(8,128)(2,1)}, bf16[512,2048]{1,0:T(8,128)(2,1)}, u32[]{:S(2)}, u32[]{:S(2)}) collective-permute-start(bf16[512,2048]{1,0:T(8,128)(2,1)} %refs_9_.1), channel_id=1, source_target_pairs={{0,16},{16,0},{32,48},{48,32},{64,80},{80,64},{96,112},{112,96},{1... | collective-permute-start | bytes 6291464 | tf_op jit(solution)/shard_map/ppermute | solution.py:23
  15.4 14.5 %all-to-all-start = ((bf16[8,64,512]{2,1,0:T(8,128)(2,1)}), bf16[8,64,512]{2,1,0:T(8,128)(2,1)S(1)}, u32[]{:S(2)}, u32[]{:S(2)}) async-start(bf16[8,64,512]{2,1,0:T(8,128)(2,1)} %project.1), calls=%async_computation | async-start | bytes 1048576 | tf_op jit(solution)/shard_map/all_to_all | solution.py:250
  31.5 7.3 %collective-permute-start.3 = (bf16[64,1152]{1,0:T(8,128)(2,1)S(1)}, bf16[64,1152]{1,0:T(8,128)(2,1)S(1)}, u32[]{:S(2)}, u32[]{:S(2)}) collective-permute-start(bf16[64,1152]{1,0:T(8,128)(2,1)S(1)} %concatenate.20), channel_id=1, source_target_pairs={{0,1},{2,3},{4,5},{6,7},{8,9},{10,11},{12,13},{14,15},{17,16},{19,... | collective-permute-start | bytes 442376 | tf_op jit(solution)/shard_map/ppermute | solution.py:265
  38.8 13.5 %collective-permute-start.5 = (bf16[64,1152]{1,0:T(8,128)(2,1)S(1)}, bf16[64,1152]{1,0:T(8,128)(2,1)S(1)}, u32[]{:S(2)}, u32[]{:S(2)}) collective-permute-start(bf16[64,1152]{1,0:T(8,128)(2,1)S(1)} %broadcast_select_fusion.refs_0_), channel_id=1, source_target_pairs={{0,12},{1,13},{2,14},{3,15},{4,0},{5,1},{6,2},{7,3},{8,4},{9,5},{1... | collective-permute-start | bytes 442376 | tf_op jit(solution)/shard_map/ppermute | solution.py:27
  45.2 11.9 %collective-permute-start.8 = (bf16[64,1152]{1,0:T(8,128)(2,1)S(1)}, bf16[64,1152]{1,0:T(8,128)(2,1)S(1)}, u32[]{:S(2)}, u32[]{:S(2)}) collective-permute-start(bf16[64,1152]{1,0:T(8,128)(2,1)S(1)} %broadcast_select_fusion.refs_0_), channel_id=1, source_target_pairs={{0,4},{1,5},{2,6},{3,7},{4,8},{5,9},{6,10},{7,11},{8,12},{9,13},{1... | collective-permute-start | bytes 442376 | tf_op jit(solution)/shard_map/ppermute | solution.py:27
  45.8 14.0 %collective-permute-start.10 = (bf16[64,1152]{1,0:T(8,128)(2,1)S(1)}, bf16[64,1152]{1,0:T(8,128)(2,1)S(1)}, u32[]{:S(2)}, u32[]{:S(2)}) collective-permute-start(bf16[64,1152]{1,0:T(8,128)(2,1)S(1)} %broadcast_select_fusion.refs_0_), channel_id=1, source_target_pairs={{0,2},{1,3},{2,4},{3,5},{4,6},{5,7},{6,8},{7,9},{8,10},{9,11},{10,... | collective-permute-start | bytes 442376 | tf_op jit(solution)/shard_map/ppermute | solution.py:27
  46.8 13.0 %collective-permute-start.4 = (bf16[64,1152]{1,0:T(8,128)(2,1)S(1)}, bf16[64,1152]{1,0:T(8,128)(2,1)S(1)}, u32[]{:S(2)}, u32[]{:S(2)}) collective-permute-start(bf16[64,1152]{1,0:T(8,128)(2,1)S(1)} %broadcast_select_fusion.refs_0_), channel_id=1, source_target_pairs={{0,14},{1,15},{2,0},{3,1},{4,2},{5,3},{6,4},{7,5},{8,6},{9,7},{10,... | collective-permute-start | bytes 442376 | tf_op jit(solution)/shard_map/ppermute | solution.py:27
  52.3 7.7 %collective-permute-start.6 = (bf16[64,1152]{1,0:T(8,128)(2,1)S(1)}, bf16[64,1152]{1,0:T(8,128)(2,1)S(1)}, u32[]{:S(2)}, u32[]{:S(2)}) collective-permute-start(bf16[64,1152]{1,0:T(8,128)(2,1)S(1)} %collective-permute-done.5.refs_2_), channel_id=1, source_target_pairs={{0,14},{1,15},{2,0},{3,1},{4,2},{5,3},{6,4},{7,5},{8,6},{9,7},{10,... | collective-permute-start | bytes 442376 | tf_op jit(solution)/shard_map/ppermute | solution.py:27
  55.0 9.6 %collective-permute-start.7 = (bf16[64,1152]{1,0:T(8,128)(2,1)S(1)}, bf16[64,1152]{1,0:T(8,128)(2,1)S(1)}, u32[]{:S(2)}, u32[]{:S(2)}) collective-permute-start(bf16[64,1152]{1,0:T(8,128)(2,1)S(1)} %collective-permute-done.5.refs_2_), channel_id=1, source_target_pairs={{0,12},{1,13},{2,14},{3,15},{4,0},{5,1},{6,2},{7,3},{8,4},{9,5},{1... | collective-permute-start | bytes 442376 | tf_op jit(solution)/shard_map/ppermute | solution.py:27
  57.1 7.4 %collective-permute-start.9 = (bf16[64,1152]{1,0:T(8,128)(2,1)S(1)}, bf16[64,1152]{1,0:T(8,128)(2,1)S(1)}, u32[]{:S(2)}, u32[]{:S(2)}) collective-permute-start(bf16[64,1152]{1,0:T(8,128)(2,1)S(1)} %collective-permute-done.8.refs_6_), channel_id=1, source_target_pairs={{0,2},{1,3},{2,4},{3,5},{4,6},{5,7},{6,8},{7,9},{8,10},{9,11},{10,... | collective-permute-start | bytes 442376 | tf_op jit(solution)/shard_map/ppermute | solution.py:27
  75.2 9.6 %all-to-all-start.1 = ((f32[16,1,1536]{2,1,0:T(1,128)}), f32[16,1,1536]{2,1,0:T(1,128)S(1)}, u32[]{:S(2)}, u32[]{:S(2)}) async-start(f32[16,1,1536]{2,1,0:T(1,128)} %reshape.81), calls=%async_computation.1 | async-start | bytes 196608 | tf_op jit(solution)/shard_map/all_to_all | solution.py:283
  88.7 14.2 %collective-permute-start.12 = (bf16[512,512]{1,0:T(8,128)(2,1)}, bf16[512,512]{1,0:T(8,128)(2,1)S(1)}, u32[]{:S(2)}, u32[]{:S(2)}) collective-permute-start(bf16[512,512]{1,0:T(8,128)(2,1)} %fusion.10), channel_id=1, source_target_pairs={{0,2},{1,3},{2,0},{3,1},{4,6},{5,7},{6,4},{7,5},{8,10},{9,11},{10,... | collective-permute-start | bytes 1572872 | tf_op jit(solution)/shard_map/ppermute | solution.py:33
  90.0 16.6 %collective-permute-start.20 = (bf16[64,2048]{1,0:T(8,128)(2,1)}, bf16[64,2048]{1,0:T(8,128)(2,1)S(1)}, u32[]{:S(2)}, u32[]{:S(2)}) collective-permute-start(bf16[64,2048]{1,0:T(8,128)(2,1)} %get-tuple-element.17), channel_id=1, source_target_pairs={{0,96},{16,112},{32,0},{48,16},{64,32},{80,48},{96,64},{112,80},{1... | collective-permute-start | bytes 786440 | tf_op jit(solution)/shard_map/ppermute | solution.py:45
  91.7 16.5 %collective-permute-start.22 = (bf16[64,2048]{1,0:T(8,128)(2,1)S(1)}, bf16[64,2048]{1,0:T(8,128)(2,1)S(1)}, u32[]{:S(2)}, u32[]{:S(2)}) collective-permute-start(bf16[64,2048]{1,0:T(8,128)(2,1)S(1)} %copy-done.13), channel_id=1, source_target_pairs={{0,32},{16,48},{32,64},{48,80},{64,96},{80,112},{96,0},{112,16},{1... | collective-permute-start | bytes 786440 | tf_op jit(solution)/shard_map/ppermute | solution.py:45
  102.9 10.8 %collective-permute-start.13 = (bf16[256,512]{1,0:T(8,128)(2,1)S(1)}, bf16[256,512]{1,0:T(8,128)(2,1)S(1)}, u32[]{:S(2)}, u32[]{:S(2)}) collective-permute-start(bf16[256,512]{1,0:T(8,128)(2,1)S(1)} %slice_add_fusion), channel_id=1, source_target_pairs={{0,1},{1,0},{2,3},{3,2},{4,5},{5,4},{6,7},{7,6},{8,9},{9,8},{10,11... | collective-permute-start | bytes 786440 | tf_op jit(solution)/shard_map/ppermute | solution.py:37
  104.6 12.8 %collective-permute-start.17 = (bf16[64,2048]{1,0:T(8,128)(2,1)S(1)}, bf16[64,2048]{1,0:T(8,128)(2,1)S(1)}, u32[]{:S(2)}, u32[]{:S(2)}) collective-permute-start(bf16[64,2048]{1,0:T(8,128)(2,1)S(1)} %copy-done.12), channel_id=1, source_target_pairs={{0,128},{16,144},{32,160},{48,176},{64,192},{80,208},{96,224},{112... | collective-permute-start | bytes 786440 | tf_op jit(solution)/shard_map/ppermute | solution.py:45
  104.6 19.4 %collective-permute-start.18 = (bf16[64,2048]{1,0:T(8,128)(2,1)S(1)}, bf16[64,2048]{1,0:T(8,128)(2,1)S(1)}, u32[]{:S(2)}, u32[]{:S(2)}) collective-permute-start(bf16[64,2048]{1,0:T(8,128)(2,1)S(1)} %copy-done.11), channel_id=1, source_target_pairs={{0,160},{16,176},{32,192},{48,208},{64,224},{80,240},{96,128},{112... | collective-permute-start | bytes 786440 | tf_op jit(solution)/shard_map/ppermute | solution.py:45
  106.7 21.6 %collective-permute-start.19 = (bf16[64,2048]{1,0:T(8,128)(2,1)S(1)}, bf16[64,2048]{1,0:T(8,128)(2,1)S(1)}, u32[]{:S(2)}, u32[]{:S(2)}) collective-permute-start(bf16[64,2048]{1,0:T(8,128)(2,1)S(1)} %copy-done.10), channel_id=1, source_target_pairs={{0,96},{16,112},{32,0},{48,16},{64,32},{80,48},{96,64},{112,80},{1... | collective-permute-start | bytes 786440 | tf_op jit(solution)/shard_map/ppermute | solution.py:45
  108.2 20.9 %collective-permute-start.21 = (bf16[64,2048]{1,0:T(8,128)(2,1)S(1)}, bf16[64,2048]{1,0:T(8,128)(2,1)S(1)}, u32[]{:S(2)}, u32[]{:S(2)}) collective-permute-start(bf16[64,2048]{1,0:T(8,128)(2,1)S(1)} %add.177), channel_id=1, source_target_pairs={{0,224},{16,240},{32,128},{48,144},{64,160},{80,176},{96,192},{112... | collective-permute-start | bytes 786440 | tf_op jit(solution)/shard_map/ppermute | solution.py:45
  113.7 15.4 %collective-permute-start.23 = (bf16[64,2048]{1,0:T(8,128)(2,1)S(1)}, bf16[64,2048]{1,0:T(8,128)(2,1)S(1)}, u32[]{:S(2)}, u32[]{:S(2)}) collective-permute-start(bf16[64,2048]{1,0:T(8,128)(2,1)S(1)} %add.179), channel_id=1, source_target_pairs={{0,32},{16,48},{32,64},{48,80},{64,96},{80,112},{96,0},{112,16},{1... | collective-permute-start | bytes 786440 | tf_op jit(solution)/shard_map/ppermute | solution.py:45
  117.4 12.6 %collective-permute-start.14 = (bf16[64,512]{1,0:T(8,128)(2,1)S(1)}, bf16[64,512]{1,0:T(8,128)(2,1)S(1)}, u32[]{:S(2)}, u32[]{:S(2)}) collective-permute-start(bf16[64,512]{1,0:T(8,128)(2,1)S(1)} %get-tuple-element.22), channel_id=1, source_target_pairs={{0,4},{1,5},{2,6},{3,7},{4,8},{5,9},{6,10},{7,11},{8,12},{9,13},{1... | collective-permute-start | bytes 196616 | tf_op jit(solution)/shard_map/ppermute | solution.py:27
  124.0 8.5 %collective-permute-start.15 = (bf16[64,512]{1,0:T(8,128)(2,1)S(1)}, bf16[64,512]{1,0:T(8,128)(2,1)S(1)}, u32[]{:S(2)}, u32[]{:S(2)}) collective-permute-start(bf16[64,512]{1,0:T(8,128)(2,1)S(1)} %get-tuple-element.24), channel_id=1, source_target_pairs={{0,8},{1,9},{2,10},{3,11},{4,12},{5,13},{6,14},{7,15},{8,0},{9,1},... | collective-permute-start | bytes 196616 | tf_op jit(solution)/shard_map/ppermute | solution.py:27
  128.2 6.2 %collective-permute-start.16 = (bf16[64,512]{1,0:T(8,128)(2,1)S(1)}, bf16[64,512]{1,0:T(8,128)(2,1)S(1)}, u32[]{:S(2)}, u32[]{:S(2)}) collective-permute-start(bf16[64,512]{1,0:T(8,128)(2,1)S(1)} %get-tuple-element.23), channel_id=1, source_target_pairs={{0,12},{1,13},{2,14},{3,15},{4,0},{5,1},{6,2},{7,3},{8,4},{9,5},{1... | collective-permute-start | bytes 196616 | tf_op jit(solution)/shard_map/ppermute | solution.py:27
  (23 other events, 317.0 us)

commit v5 on v4

--- a/solution.py
+++ b/solution.py
@@ -123,7 +123,7 @@
 def encode_kernel(place_ref, *refs):
     block_refs, (bias_ref, w_mine_ref, w_other_ref) = refs[:8], refs[8:11]
     out_refs, table_ref = refs[11:19], refs[19]
-    x_ref, held_ref, sems = refs[20:]
+    x_ref, held_ref, row_ref, sems = refs[20:]
     f32 = jnp.float32
     step = pl.program_id(0)
     half, tile = w_mine_ref.shape
@@ -177,11 +177,14 @@
         for c in range(4):
             whole = extra[2 + 3 * c : 3 + 3 * c] + extra[3 + 3 * c : 4 + 3 * c]
             value += jnp.where(index == c, whole + extra[4 + 3 * c : 5 + 3 * c], 0.0)
+        row_ref[...] = jnp.zeros_like(row_ref)
         for slot in range(8):
             for at, source in enumerate((now, local, value)):
-                table_ref[pl.ds(8 * at + place_ref[8 + slot], 1), :] = source[
+                row_ref[pl.ds(8 * at + place_ref[8 + slot], 1), :rows] = source[
                     :, slot * rows : (slot + 1) * rows
                 ]
+        for i in range(16):
+            table_ref[i] = row_ref[...]
 
 
 def encode(block, place, bias, w_mine, w_other):
@@ -201,15 +204,16 @@
                 pl.BlockSpec((half, tile), lambda i, place: (0, i)),
             ],
             out_specs=[pl.BlockSpec((rows, tile), lambda i, place: (0, i))] * 8
-            + [pl.BlockSpec((24, rows), lambda i, place: (0, 0))],
+            + [pl.BlockSpec((16, 24, 128), lambda i, place: (0, 0, 0))],
             scratch_shapes=[
                 pltpu.VMEM((count, depth), jnp.bfloat16),
                 pltpu.VMEM((count, 128), jnp.float32),
+                pltpu.VMEM((24, 128), jnp.float32),
                 pltpu.SemaphoreType.DMA((8,)),
             ],
         ),
         out_shape=[jax.ShapeDtypeStruct((rows, span), jnp.bfloat16)] * 8
-        + [jax.ShapeDtypeStruct((24, rows), jnp.float32)],
+        + [jax.ShapeDtypeStruct((16, 24, 128), jnp.float32)],
         cost_estimate=pl.CostEstimate(
             flops=4 * count * half * span,
             bytes_accessed=2 * (2 * half * span + count * (depth + span)),
@@ -280,9 +284,8 @@
         block, jnp.concatenate([slot, goal, others]), bias, enc_weight, enc_other
     )
 
-    table = lax.all_to_all(
-        jnp.broadcast_to(outs[8][None], (16, 24, rows)), "tp", 0, 0, tiled=True
-    ).reshape(8, 2, 24, rows)
+    table = lax.all_to_all(outs[8], "tp", 0, 0, tiled=True)
+    table = table[:, :, :rows].reshape(8, 2, 24, rows)
     now = jnp.maximum(table[:, :, :8].sum(axis=0), 0.0)
     now = lax.reduce_precision(now, 8, 7)
     want, delta = table[0, :, 8:16], table[0, :, 16:] - now
@@ -291,21 +294,34 @@
         value = jnp.where(plane == 1, value, value[::-1])
         odd = value[:, 1::2]
         odd = jnp.where(z % 2 == 0, odd, jnp.concatenate([odd[:, 3:], odd[:, :3]], axis=1))
-        return odd.reshape(8 * rows), value[:, 0::2].reshape(8 * rows)
-
-    def decode(want, delta):
+        return odd, value[:, 0::2]
+
+    half = width // 2
+
+    def decode(want, delta, columns):
         column = jnp.arange(span, dtype=jnp.int32)[None, :]
-        hits = jnp.where(column == want.astype(jnp.int32)[:, None], delta[:, None], 0.0)
-        return mm(hits.astype(bf16), dec_weight)
-
-    want_give, want_keep = arrange(want)
-    delta_give, delta_keep = arrange(delta)
-    give = decode(want_give, delta_give).astype(bf16)
-    near = flip_z(give, 1)
-    keep = decode(want_keep, delta_keep).astype(bf16)
+        hits = jnp.where(
+            column == want.reshape(8 * rows).astype(jnp.int32)[:, None],
+            delta.reshape(8 * rows)[:, None],
+            0.0,
+        )
+        return mm(hits.astype(bf16), dec_weight[:, columns]).astype(bf16)
+
+    want, delta = arrange(want), arrange(delta)
+    across = lambda pair, at: jnp.stack([pair[0][at], pair[1][at]])
+    left, right = slice(0, half), slice(half, width)
+    give_z = decode(want[0], delta[0], left)
+    near_z = flip_z(give_z, 1)
+    give_p = decode(across(want, 0), across(delta, 0), right)
+    near_p = flip_plane(give_p)
+    keep_z = decode(want[1], delta[1], left)
+    keep_p = decode(across(want, 1), across(delta, 1), right)
     first, last = slice(0, 4 * rows), slice(4 * rows, 8 * rows)
-    near_2 = flip_plane(keep[first] + near[first])
-    found = keep[last] + near[last] + near_2
+    near_pz = flip_z(keep_p[first] + near_p[first], 1)
+    near_zp = flip_plane(keep_z[first] + near_z[first])
+    found = jnp.concatenate(
+        [keep_z[last] + near_z[last] + near_zp, keep_p[last] + near_p[last] + near_pz], axis=1
+    )
     edit = found[:rows].astype(f32)
     edits = []
     for k in (1, 2, 3):

time: 137 us -> 127 us (0.927)
  waiting for transfers between devices: 49.4 us -> 36.3 us
  starting transfers between devices: 51 us -> 56.6 us
  local copies, waits for them, and re-layouts: 6.09 us -> 4.31 us
    ppermute x7, waiting for transfers between devices: 8.1 us -> 0.02 us  [to_chip(): lax.ppermute(value, 'tp', tp_moves(lambda chip, core: chip_at(chip, dx, d...]
    ppermute x1 -> x2, waiting for transfers between devices: 9.25 us -> 3.63 us  [flip_z(): lax.ppermute(value, 'grp', grp_moves(lambda z, plane: (z ^ k) * 2 + plane))]
    ppermute x1 -> x2, waiting for transfers between devices: 3.18 us -> 7.61 us  [flip_plane(): lax.ppermute(value, 'grp', grp_moves(lambda z, plane: z * 2 + 1 - plane))]
    all_to_all x1, waiting for transfers between devices: 4.78 us -> 1.48 us  [per_device(): table = lax.all_to_all(outs[8], 'tp', 0, 0, tiled=True)]
    ppermute x10, starting transfers between devices: 23.4 us -> 25.2 us  [from_z(): lax.ppermute(value, 'grp', grp_moves(lambda z, plane: (z - ahead) % 8 * 2...]
    ppermute x1 -> x2, starting transfers between devices: 1.66 us -> 3.22 us  [flip_plane(): lax.ppermute(value, 'grp', grp_moves(lambda z, plane: z * 2 + 1 - plane))]
    dot_general x2 -> x4, matrix products: 3.37 us -> 3.02 us  [mm(): return jnp.dot(a, b, preferred_element_type=jnp.float32)]
  transfers between devices with their start and end apart: 26 -> 28, of which waited for: 14 -> 13; matrix products, arithmetic and copies ran while one was open for 10% -> 13% of each run, Pallas kernels for 3% -> 4%
where the time goes in v5:
time: 127 us; the launch traced here: 125 us
  starting transfers between devices  56.6 us (45%)
  waiting for transfers between devices  36.3 us (29%)
  Pallas kernels  13.1 us (10%)
  matrix products  8.54 us (7%)
  other arithmetic  5.08 us (4%)
  local copies, waits for them, and re-layouts  4.31 us (3%)
    ppermute x10, starting transfers between devices, from_z(): lax.ppermute(value, 'grp', grp_moves(lambda z, plane: (z - ahead) % 8 * 2...  25.2 us
    ppermute x10, waiting for transfers between devices, from_z(): lax.ppermute(value, 'grp', grp_moves(lambda z, plane: (z - ahead) % 8 * 2...  11.5 us
    ppermute x7, starting transfers between devices, to_chip(): lax.ppermute(value, 'tp', tp_moves(lambda chip, core: chip_at(chip, dx, d...  9.58 us
    pallas_call x1, Pallas kernels, encode(): pl.pallas_call(encode_kernel, grid_spec=pltpu.PrefetchScalarGridSpec(num_...  8.68 us
    all_to_all x1, waiting for transfers between devices, per_device(): lax.all_to_all(part, 'tp', 0, 0, axis_index_groups=groups, tiled=True)  7.68 us
    ppermute x2, waiting for transfers between devices, flip_plane(): lax.ppermute(value, 'grp', grp_moves(lambda z, plane: z * 2 + 1 - plane))  7.61 us
    all_to_all x1, starting transfers between devices, per_device(): lax.all_to_all(part, 'tp', 0, 0, axis_index_groups=groups, tiled=True)  5.97 us
    all_to_all x1, starting transfers between devices, per_device(): table = lax.all_to_all(outs[8], 'tp', 0, 0, tiled=True)  4.83 us
  transfers between devices with their start and end apart: 28, of which 13 were waited for; matrix products, arithmetic and copies ran while one was open for 13% of the time, Pallas kernels for 4%

profile of v5, /device:TPU:8, one launch (start us, length us, event | category | flops | bytes accessed | tf_op | source)
XLA Modules:
  0.0 125.1 jit_solution(5009136961176184450)
XLA Ops:
  3.5 2.9 %select_reduce_fusion = (f32[64,2]{1,0:T(8,128)S(1)}, f32[64,2,128]{2,1,0:T(2,128)S(1)}) fusion(pred[64,128]{1,0:T(8,128)(4,1)S(1)} %iota_compare_fusion.4, bf16[64,2,128]{2,1,0:T(2,128)(2,1)S(1)} %reshape.88, bf16[2,64,1,128,128]{4,3,1,2,0:T(8,128)(2,1)} %bitcast.67), kind=kOutput, calls=%fused_computation.63 | convolution fusion | flops 4243328 | bytes 2204160 | tf_op jit(solution)/shard_map/shd,spd->shp/dot_general | solution.py:61
  6.6 2.5 %fusion.25 = bf16[64,2,128]{2,1,0:T(2,128)(2,1)S(1)} fusion(bf16[2,64,1,128,128]{4,3,1,2,0:T(8,128)(2,1)} %bitcast.68, f32[64,2]{1,0:T(8,128)S(1)} %get-tuple-element.30, f32[64,128]{1,0:T(8,128)S(1)} %bitcast.63, f32[64,2]{1,0:T(8,128)S(1)} %convert_element_type.141, f32[64,2,128]{2,1,0:T(2,128)S(1)} %get-tuple-element.43, ...), kind=kOutput, calls=%fused_computation.35 | convolution fusion | flops 4308992 | bytes 2237952 | tf_op jit(solution)/shard_map/shp,spd->shd/dot_general | solution.py:75
  11.2 4.4 %project.1 = bf16[8,64,512]{2,1,0:T(8,128)(2,1)} custom-call(s32[1]{0:T(128)} %bitcast.core_ref, bf16[64,256]{1,0:T(8,128)(2,1)} %bitcast.58, bf16[64,256]{1,0:T(8,128)(2,1)} %copy-done.6, bf16[256,8192]{1,0:T(8,128)(2,1)} %refs_1_.1, bf16[256,8192]{1,0:T(8,128)(2,1)} %refs_1_.1, bf16[256,8192]{1,0:T(8,128)(2,1)} %collective-permute-done.1.refs_2_.refs_3_, ...), custom_call_target="tpu_custom_call" | custom-call | flops 268435456 | bytes 4194304 | tf_op jit(solution)/shard_map/project/pallas_call | solution.py:105
  15.6 6.0 %all-to-all-start = ((bf16[8,64,512]{2,1,0:T(8,128)(2,1)}), bf16[8,64,512]{2,1,0:T(8,128)(2,1)S(1)}, u32[]{:S(2)}, u32[]{:S(2)}) async-start(bf16[8,64,512]{2,1,0:T(8,128)(2,1)} %project.1), calls=%async_computation | async-start | bytes 1048576 | tf_op jit(solution)/shard_map/all_to_all | solution.py:254
  22.4 7.7 %all-to-all-done = bf16[8,64,512]{2,1,0:T(8,128)(2,1)S(1)} async-done(((bf16[8,64,512]{2,1,0:T(8,128)(2,1)}), bf16[8,64,512]{2,1,0:T(8,128)(2,1)S(1)}, u32[]{:S(2)}, u32[]{:S(2)}) %all-to-all-start) | async-done | bytes 524320 | tf_op jit(solution)/shard_map/all_to_all | solution.py:254
  31.6 4.6 %collective-permute-start.3 = (bf16[64,1152]{1,0:T(8,128)(2,1)S(1)}, bf16[64,1152]{1,0:T(8,128)(2,1)S(1)}, u32[]{:S(2)}, u32[]{:S(2)}) collective-permute-start(bf16[64,1152]{1,0:T(8,128)(2,1)S(1)} %concatenate.23), channel_id=1, source_target_pairs={{0,1},{2,3},{4,5},{6,7},{8,9},{10,11},{12,13},{14,15},{17,16},{19,... | collective-permute-start | bytes 442376 | tf_op jit(solution)/shard_map/ppermute | solution.py:269
  36.3 2.6 %collective-permute-done.3 = bf16[64,1152]{1,0:T(8,128)(2,1)S(1)} collective-permute-done((bf16[64,1152]{1,0:T(8,128)(2,1)S(1)}, bf16[64,1152]{1,0:T(8,128)(2,1)S(1)}, u32[]{:S(2)}, u32[]{:S(2)}) %collective-permute-start.3) | collective-permute-done | bytes 147488 | tf_op jit(solution)/shard_map/ppermute | solution.py:269
  39.0 6.4 %collective-permute-start.5 = (bf16[64,1152]{1,0:T(8,128)(2,1)S(1)}, bf16[64,1152]{1,0:T(8,128)(2,1)S(1)}, u32[]{:S(2)}, u32[]{:S(2)}) collective-permute-start(bf16[64,1152]{1,0:T(8,128)(2,1)S(1)} %broadcast_select_fusion.refs_0_), channel_id=1, source_target_pairs={{0,12},{1,13},{2,14},{3,15},{4,0},{5,1},{6,2},{7,3},{8,4},{9,5},{1... | collective-permute-start | bytes 442376 | tf_op jit(solution)/shard_map/ppermute | solution.py:27
  47.0 2.7 %collective-permute-start.4 = (bf16[64,1152]{1,0:T(8,128)(2,1)S(1)}, bf16[64,1152]{1,0:T(8,128)(2,1)S(1)}, u32[]{:S(2)}, u32[]{:S(2)}) collective-permute-start(bf16[64,1152]{1,0:T(8,128)(2,1)S(1)} %broadcast_select_fusion.refs_0_), channel_id=1, source_target_pairs={{0,14},{1,15},{2,0},{3,1},{4,2},{5,3},{6,4},{7,5},{8,6},{9,7},{10,... | collective-permute-start | bytes 442376 | tf_op jit(solution)/shard_map/ppermute | solution.py:27
  49.6 2.8 %collective-permute-done.5.refs_2_ = bf16[64,1152]{1,0:T(8,128)(2,1)S(1)} collective-permute-done((bf16[64,1152]{1,0:T(8,128)(2,1)S(1)}, bf16[64,1152]{1,0:T(8,128)(2,1)S(1)}, u32[]{:S(2)}, u32[]{:S(2)}) %collective-permute-start.5) | collective-permute-done | bytes 147488 | tf_op jit(solution)/shard_map/ppermute | solution.py:27
  52.4 2.7 %collective-permute-start.6 = (bf16[64,1152]{1,0:T(8,128)(2,1)S(1)}, bf16[64,1152]{1,0:T(8,128)(2,1)S(1)}, u32[]{:S(2)}, u32[]{:S(2)}) collective-permute-start(bf16[64,1152]{1,0:T(8,128)(2,1)S(1)} %collective-permute-done.5.refs_2_), channel_id=1, source_target_pairs={{0,14},{1,15},{2,0},{3,1},{4,2},{5,3},{6,4},{7,5},{8,6},{9,7},{10,... | collective-permute-start | bytes 442376 | tf_op jit(solution)/shard_map/ppermute | solution.py:27
  55.1 2.1 %collective-permute-start.7 = (bf16[64,1152]{1,0:T(8,128)(2,1)S(1)}, bf16[64,1152]{1,0:T(8,128)(2,1)S(1)}, u32[]{:S(2)}, u32[]{:S(2)}) collective-permute-start(bf16[64,1152]{1,0:T(8,128)(2,1)S(1)} %collective-permute-done.5.refs_2_), channel_id=1, source_target_pairs={{0,12},{1,13},{2,14},{3,15},{4,0},{5,1},{6,2},{7,3},{8,4},{9,5},{1... | collective-permute-start | bytes 442376 | tf_op jit(solution)/shard_map/ppermute | solution.py:27
  57.3 1.9 %collective-permute-start.9 = (bf16[64,1152]{1,0:T(8,128)(2,1)S(1)}, bf16[64,1152]{1,0:T(8,128)(2,1)S(1)}, u32[]{:S(2)}, u32[]{:S(2)}) collective-permute-start(bf16[64,1152]{1,0:T(8,128)(2,1)S(1)} %collective-permute-done.8.refs_6_), channel_id=1, source_target_pairs={{0,2},{1,3},{2,4},{3,5},{4,6},{5,7},{6,8},{7,9},{8,10},{9,11},{10,... | collective-permute-start | bytes 442376 | tf_op jit(solution)/shard_map/ppermute | solution.py:27
  60.2 4.5 %collective-permute-done.7.refs_4_ = bf16[64,1152]{1,0:T(8,128)(2,1)S(1)} collective-permute-done((bf16[64,1152]{1,0:T(8,128)(2,1)S(1)}, bf16[64,1152]{1,0:T(8,128)(2,1)S(1)}, u32[]{:S(2)}, u32[]{:S(2)}) %collective-permute-start.7) | collective-permute-done | bytes 147488 | tf_op jit(solution)/shard_map/ppermute | solution.py:27
  65.4 8.7 %encode.1 = (bf16[64,2048]{1,0:T(8,128)(2,1)}, bf16[64,2048]{1,0:T(8,128)(2,1)}, bf16[64,2048]{1,0:T(8,128)(2,1)}, bf16[64,2048]{1,0:T(8,128)(2,1)}, bf16[64,204...) custom-call(s32[18]{0:T(128)} %pad_add_fusion.place_ref, ...), custom_call_target="tpu_custom_call" | custom-call | flops 2147483648 | bytes 7471104 | tf_op jit(solution)/shard_map/encode/pallas_call | solution.py:195
  74.1 4.8 %all-to-all-start.1 = ((f32[16,24,128]{2,1,0:T(8,128)}), f32[16,24,128]{2,1,0:T(8,128)S(1)}, u32[]{:S(2)}, u32[]{:S(2)}) async-start(f32[16,24,128]{2,1,0:T(8,128)} %get-tuple-element.11), calls=%async_computation.1 | async-start | bytes 393216 | tf_op jit(solution)/shard_map/all_to_all | solution.py:287
  91.4 1.9 %collective-permute-start.21 = (bf16[64,2048]{1,0:T(8,128)(2,1)S(1)}, bf16[64,2048]{1,0:T(8,128)(2,1)S(1)}, u32[]{:S(2)}, u32[]{:S(2)}) collective-permute-start(bf16[64,2048]{1,0:T(8,128)(2,1)S(1)} %copy-done.11), channel_id=1, source_target_pairs={{0,96},{16,112},{32,0},{48,16},{64,32},{80,48},{96,64},{112,80},{1... | collective-permute-start | bytes 786440 | tf_op jit(solution)/shard_map/ppermute | solution.py:45
  93.5 2.7 %collective-permute-done.14 = bf16[512,256]{1,0:T(8,128)(2,1)S(1)} collective-permute-done((bf16[512,256]{1,0:T(8,128)(2,1)S(1)}, bf16[512,256]{1,0:T(8,128)(2,1)S(1)}, u32[]{:S(2)}, u32[]{:S(2)}) %collective-permute-start.14) | collective-permute-done | bytes 262176 | tf_op jit(solution)/shard_map/ppermute | solution.py:37
  96.2 2.6 %collective-permute-start.23 = (bf16[64,2048]{1,0:T(8,128)(2,1)S(1)}, bf16[64,2048]{1,0:T(8,128)(2,1)S(1)}, u32[]{:S(2)}, u32[]{:S(2)}) collective-permute-start(bf16[64,2048]{1,0:T(8,128)(2,1)S(1)} %add.189), channel_id=1, source_target_pairs={{0,224},{16,240},{32,128},{48,144},{64,160},{80,176},{96,192},{112... | collective-permute-start | bytes 786440 | tf_op jit(solution)/shard_map/ppermute | solution.py:45
  100.2 3.6 %collective-permute-done.15 = bf16[256,256]{1,0:T(8,128)(2,1)S(1)} collective-permute-done((bf16[256,256]{1,0:T(8,128)(2,1)S(1)}, bf16[256,256]{1,0:T(8,128)(2,1)S(1)}, u32[]{:S(2)}, u32[]{:S(2)}) %collective-permute-start.15) | collective-permute-done | bytes 131104 | tf_op jit(solution)/shard_map/ppermute | solution.py:33
  105.4 4.9 %collective-permute-done.13 = bf16[256,256]{1,0:T(8,128)(2,1)S(1)} collective-permute-done((bf16[256,256]{1,0:T(8,128)(2,1)S(1)}, bf16[256,256]{1,0:T(8,128)(2,1)S(1)}, u32[]{:S(2)}, u32[]{:S(2)}) %collective-permute-start.13) | collective-permute-done | bytes 131104 | tf_op jit(solution)/shard_map/ppermute | solution.py:37
  111.1 2.4 %collective-permute-start.16 = (bf16[64,512]{1,0:T(8,128)(2,1)S(1)}, bf16[64,512]{1,0:T(8,128)(2,1)S(1)}, u32[]{:S(2)}, u32[]{:S(2)}) collective-permute-start(bf16[64,512]{1,0:T(8,128)(2,1)S(1)} %get-tuple-element.24), channel_id=1, source_target_pairs={{0,4},{1,5},{2,6},{3,7},{4,8},{5,9},{6,10},{7,11},{8,12},{9,13},{1... | collective-permute-start | bytes 196616 | tf_op jit(solution)/shard_map/ppermute | solution.py:27
  113.6 4.3 %collective-permute-start.17 = (bf16[64,512]{1,0:T(8,128)(2,1)S(1)}, bf16[64,512]{1,0:T(8,128)(2,1)S(1)}, u32[]{:S(2)}, u32[]{:S(2)}) collective-permute-start(bf16[64,512]{1,0:T(8,128)(2,1)S(1)} %get-tuple-element.26), channel_id=1, source_target_pairs={{0,8},{1,9},{2,10},{3,11},{4,12},{5,13},{6,14},{7,15},{8,0},{9,1},... | collective-permute-start | bytes 196616 | tf_op jit(solution)/shard_map/ppermute | solution.py:27
  120.5 2.1 %collective-permute-done.17 = bf16[64,512]{1,0:T(8,128)(2,1)S(1)} collective-permute-done((bf16[64,512]{1,0:T(8,128)(2,1)S(1)}, bf16[64,512]{1,0:T(8,128)(2,1)S(1)}, u32[]{:S(2)}, u32[]{:S(2)}) %collective-permute-start.17) | collective-permute-done | bytes 65568 | tf_op jit(solution)/shard_map/ppermute | solution.py:27
  (147 shorter events, 32.2 us)
Async XLA Ops:
  0.6 9.9 %collective-permute-start.1 = (bf16[256,8192]{1,0:T(8,128)(2,1)}, bf16[256,8192]{1,0:T(8,128)(2,1)}, u32[]{:S(2)}, u32[]{:S(2)}) collective-permute-start(bf16[256,8192]{1,0:T(8,128)(2,1)} %refs_1_.1), channel_id=1, source_target_pairs={{0,16},{16,0},{32,48},{48,32},{64,80},{80,64},{96,112},{112,96},{1... | collective-permute-start | bytes 12582920 | tf_op jit(solution)/shard_map/ppermute | solution.py:23
  9.7 45.4 %collective-permute-start.11 = (bf16[512,2048]{1,0:T(8,128)(2,1)S(1)}, bf16[512,2048]{1,0:T(8,128)(2,1)}, u32[]{:S(2)}, u32[]{:S(2)}) collective-permute-start(bf16[512,2048]{1,0:T(8,128)(2,1)S(1)} %copy-done.9), channel_id=1, source_target_pairs={{0,16},{16,0},{32,48},{48,32},{64,80},{80,64},{96,112},{112,96},{1... | collective-permute-start | bytes 6291464 | tf_op jit(solution)/shard_map/ppermute | solution.py:23
  15.6 14.5 %all-to-all-start = ((bf16[8,64,512]{2,1,0:T(8,128)(2,1)}), bf16[8,64,512]{2,1,0:T(8,128)(2,1)S(1)}, u32[]{:S(2)}, u32[]{:S(2)}) async-start(bf16[8,64,512]{2,1,0:T(8,128)(2,1)} %project.1), calls=%async_computation | async-start | bytes 1048576 | tf_op jit(solution)/shard_map/all_to_all | solution.py:254
  31.6 7.3 %collective-permute-start.3 = (bf16[64,1152]{1,0:T(8,128)(2,1)S(1)}, bf16[64,1152]{1,0:T(8,128)(2,1)S(1)}, u32[]{:S(2)}, u32[]{:S(2)}) collective-permute-start(bf16[64,1152]{1,0:T(8,128)(2,1)S(1)} %concatenate.23), channel_id=1, source_target_pairs={{0,1},{2,3},{4,5},{6,7},{8,9},{10,11},{12,13},{14,15},{17,16},{19,... | collective-permute-start | bytes 442376 | tf_op jit(solution)/shard_map/ppermute | solution.py:269
  39.0 13.5 %collective-permute-start.5 = (bf16[64,1152]{1,0:T(8,128)(2,1)S(1)}, bf16[64,1152]{1,0:T(8,128)(2,1)S(1)}, u32[]{:S(2)}, u32[]{:S(2)}) collective-permute-start(bf16[64,1152]{1,0:T(8,128)(2,1)S(1)} %broadcast_select_fusion.refs_0_), channel_id=1, source_target_pairs={{0,12},{1,13},{2,14},{3,15},{4,0},{5,1},{6,2},{7,3},{8,4},{9,5},{1... | collective-permute-start | bytes 442376 | tf_op jit(solution)/shard_map/ppermute | solution.py:27
  45.3 11.9 %collective-permute-start.8 = (bf16[64,1152]{1,0:T(8,128)(2,1)S(1)}, bf16[64,1152]{1,0:T(8,128)(2,1)S(1)}, u32[]{:S(2)}, u32[]{:S(2)}) collective-permute-start(bf16[64,1152]{1,0:T(8,128)(2,1)S(1)} %broadcast_select_fusion.refs_0_), channel_id=1, source_target_pairs={{0,4},{1,5},{2,6},{3,7},{4,8},{5,9},{6,10},{7,11},{8,12},{9,13},{1... | collective-permute-start | bytes 442376 | tf_op jit(solution)/shard_map/ppermute | solution.py:27
  46.0 13.9 %collective-permute-start.10 = (bf16[64,1152]{1,0:T(8,128)(2,1)S(1)}, bf16[64,1152]{1,0:T(8,128)(2,1)S(1)}, u32[]{:S(2)}, u32[]{:S(2)}) collective-permute-start(bf16[64,1152]{1,0:T(8,128)(2,1)S(1)} %broadcast_select_fusion.refs_0_), channel_id=1, source_target_pairs={{0,2},{1,3},{2,4},{3,5},{4,6},{5,7},{6,8},{7,9},{8,10},{9,11},{10,... | collective-permute-start | bytes 442376 | tf_op jit(solution)/shard_map/ppermute | solution.py:27
  47.0 12.9 %collective-permute-start.4 = (bf16[64,1152]{1,0:T(8,128)(2,1)S(1)}, bf16[64,1152]{1,0:T(8,128)(2,1)S(1)}, u32[]{:S(2)}, u32[]{:S(2)}) collective-permute-start(bf16[64,1152]{1,0:T(8,128)(2,1)S(1)} %broadcast_select_fusion.refs_0_), channel_id=1, source_target_pairs={{0,14},{1,15},{2,0},{3,1},{4,2},{5,3},{6,4},{7,5},{8,6},{9,7},{10,... | collective-permute-start | bytes 442376 | tf_op jit(solution)/shard_map/ppermute | solution.py:27
  52.4 7.7 %collective-permute-start.6 = (bf16[64,1152]{1,0:T(8,128)(2,1)S(1)}, bf16[64,1152]{1,0:T(8,128)(2,1)S(1)}, u32[]{:S(2)}, u32[]{:S(2)}) collective-permute-start(bf16[64,1152]{1,0:T(8,128)(2,1)S(1)} %collective-permute-done.5.refs_2_), channel_id=1, source_target_pairs={{0,14},{1,15},{2,0},{3,1},{4,2},{5,3},{6,4},{7,5},{8,6},{9,7},{10,... | collective-permute-start | bytes 442376 | tf_op jit(solution)/shard_map/ppermute | solution.py:27
  55.1 9.6 %collective-permute-start.7 = (bf16[64,1152]{1,0:T(8,128)(2,1)S(1)}, bf16[64,1152]{1,0:T(8,128)(2,1)S(1)}, u32[]{:S(2)}, u32[]{:S(2)}) collective-permute-start(bf16[64,1152]{1,0:T(8,128)(2,1)S(1)} %collective-permute-done.5.refs_2_), channel_id=1, source_target_pairs={{0,12},{1,13},{2,14},{3,15},{4,0},{5,1},{6,2},{7,3},{8,4},{9,5},{1... | collective-permute-start | bytes 442376 | tf_op jit(solution)/shard_map/ppermute | solution.py:27
  57.3 7.4 %collective-permute-start.9 = (bf16[64,1152]{1,0:T(8,128)(2,1)S(1)}, bf16[64,1152]{1,0:T(8,128)(2,1)S(1)}, u32[]{:S(2)}, u32[]{:S(2)}) collective-permute-start(bf16[64,1152]{1,0:T(8,128)(2,1)S(1)} %collective-permute-done.8.refs_6_), channel_id=1, source_target_pairs={{0,2},{1,3},{2,4},{3,5},{4,6},{5,7},{6,8},{7,9},{8,10},{9,11},{10,... | collective-permute-start | bytes 442376 | tf_op jit(solution)/shard_map/ppermute | solution.py:27
  74.1 9.8 %all-to-all-start.1 = ((f32[16,24,128]{2,1,0:T(8,128)}), f32[16,24,128]{2,1,0:T(8,128)S(1)}, u32[]{:S(2)}, u32[]{:S(2)}) async-start(f32[16,24,128]{2,1,0:T(8,128)} %get-tuple-element.11), calls=%async_computation.1 | async-start | bytes 393216 | tf_op jit(solution)/shard_map/all_to_all | solution.py:287
  78.9 11.5 %collective-permute-start.22 = (bf16[64,2048]{1,0:T(8,128)(2,1)}, bf16[64,2048]{1,0:T(8,128)(2,1)S(1)}, u32[]{:S(2)}, u32[]{:S(2)}) collective-permute-start(bf16[64,2048]{1,0:T(8,128)(2,1)} %get-tuple-element.17), channel_id=1, source_target_pairs={{0,96},{16,112},{32,0},{48,16},{64,32},{80,48},{96,64},{112,80},{1... | collective-permute-start | bytes 786440 | tf_op jit(solution)/shard_map/ppermute | solution.py:45
  79.3 12.1 %collective-permute-start.24 = (bf16[64,2048]{1,0:T(8,128)(2,1)}, bf16[64,2048]{1,0:T(8,128)(2,1)S(1)}, u32[]{:S(2)}, u32[]{:S(2)}) collective-permute-start(bf16[64,2048]{1,0:T(8,128)(2,1)} %get-tuple-element.19), channel_id=1, source_target_pairs={{0,32},{16,48},{32,64},{48,80},{64,96},{80,112},{96,0},{112,16},{1... | collective-permute-start | bytes 786440 | tf_op jit(solution)/shard_map/ppermute | solution.py:45
  81.0 30.2 %collective-permute-start.19 = (bf16[64,2048]{1,0:T(8,128)(2,1)}, bf16[64,2048]{1,0:T(8,128)(2,1)S(1)}, u32[]{:S(2)}, u32[]{:S(2)}) collective-permute-start(bf16[64,2048]{1,0:T(8,128)(2,1)} %get-tuple-element.13), channel_id=1, source_target_pairs={{0,128},{16,144},{32,160},{48,176},{64,192},{80,208},{96,224},{112... | collective-permute-start | bytes 786440 | tf_op jit(solution)/shard_map/ppermute | solution.py:45
  85.4 10.7 %collective-permute-start.14 = (bf16[512,256]{1,0:T(8,128)(2,1)S(1)}, bf16[512,256]{1,0:T(8,128)(2,1)S(1)}, u32[]{:S(2)}, u32[]{:S(2)}) collective-permute-start(bf16[512,256]{1,0:T(8,128)(2,1)S(1)} %fusion.18), channel_id=1, source_target_pairs={{0,1},{1,0},{2,3},{3,2},{4,5},{5,4},{6,7},{7,6},{8,9},{9,8},{10,11... | collective-permute-start | bytes 786440 | tf_op jit(solution)/shard_map/ppermute | solution.py:37
  88.0 10.7 %collective-permute-start.12 = (bf16[512,256]{1,0:T(8,128)(2,1)S(1)}, bf16[512,256]{1,0:T(8,128)(2,1)S(1)}, u32[]{:S(2)}, u32[]{:S(2)}) collective-permute-start(bf16[512,256]{1,0:T(8,128)(2,1)S(1)} %fusion.20), channel_id=1, source_target_pairs={{0,2},{1,3},{2,0},{3,1},{4,6},{5,7},{6,4},{7,5},{8,10},{9,11},{10,... | collective-permute-start | bytes 786440 | tf_op jit(solution)/shard_map/ppermute | solution.py:33
  90.6 23.0 %collective-permute-start.20 = (bf16[64,2048]{1,0:T(8,128)(2,1)S(1)}, bf16[64,2048]{1,0:T(8,128)(2,1)S(1)}, u32[]{:S(2)}, u32[]{:S(2)}) collective-permute-start(bf16[64,2048]{1,0:T(8,128)(2,1)S(1)} %copy-done.12), channel_id=1, source_target_pairs={{0,160},{16,176},{32,192},{48,208},{64,224},{80,240},{96,128},{112... | collective-permute-start | bytes 786440 | tf_op jit(solution)/shard_map/ppermute | solution.py:45
  91.4 26.4 %collective-permute-start.21 = (bf16[64,2048]{1,0:T(8,128)(2,1)S(1)}, bf16[64,2048]{1,0:T(8,128)(2,1)S(1)}, u32[]{:S(2)}, u32[]{:S(2)}) collective-permute-start(bf16[64,2048]{1,0:T(8,128)(2,1)S(1)} %copy-done.11), channel_id=1, source_target_pairs={{0,96},{16,112},{32,0},{48,16},{64,32},{80,48},{96,64},{112,80},{1... | collective-permute-start | bytes 786440 | tf_op jit(solution)/shard_map/ppermute | solution.py:45
  96.2 23.4 %collective-permute-start.23 = (bf16[64,2048]{1,0:T(8,128)(2,1)S(1)}, bf16[64,2048]{1,0:T(8,128)(2,1)S(1)}, u32[]{:S(2)}, u32[]{:S(2)}) collective-permute-start(bf16[64,2048]{1,0:T(8,128)(2,1)S(1)} %add.189), channel_id=1, source_target_pairs={{0,224},{16,240},{32,128},{48,144},{64,160},{80,176},{96,192},{112... | collective-permute-start | bytes 786440 | tf_op jit(solution)/shard_map/ppermute | solution.py:45
  110.3 9.3 %collective-permute-start.25 = (bf16[64,2048]{1,0:T(8,128)(2,1)S(1)}, bf16[64,2048]{1,0:T(8,128)(2,1)S(1)}, u32[]{:S(2)}, u32[]{:S(2)}) collective-permute-start(bf16[64,2048]{1,0:T(8,128)(2,1)S(1)} %add.191), channel_id=1, source_target_pairs={{0,32},{16,48},{32,64},{48,80},{64,96},{80,112},{96,0},{112,16},{1... | collective-permute-start | bytes 786440 | tf_op jit(solution)/shard_map/ppermute | solution.py:45
  111.1 9.4 %collective-permute-start.16 = (bf16[64,512]{1,0:T(8,128)(2,1)S(1)}, bf16[64,512]{1,0:T(8,128)(2,1)S(1)}, u32[]{:S(2)}, u32[]{:S(2)}) collective-permute-start(bf16[64,512]{1,0:T(8,128)(2,1)S(1)} %get-tuple-element.24), channel_id=1, source_target_pairs={{0,4},{1,5},{2,6},{3,7},{4,8},{5,9},{6,10},{7,11},{8,12},{9,13},{1... | collective-permute-start | bytes 196616 | tf_op jit(solution)/shard_map/ppermute | solution.py:27
  113.6 9.0 %collective-permute-start.17 = (bf16[64,512]{1,0:T(8,128)(2,1)S(1)}, bf16[64,512]{1,0:T(8,128)(2,1)S(1)}, u32[]{:S(2)}, u32[]{:S(2)}) collective-permute-start(bf16[64,512]{1,0:T(8,128)(2,1)S(1)} %get-tuple-element.26), channel_id=1, source_target_pairs={{0,8},{1,9},{2,10},{3,11},{4,12},{5,13},{6,14},{7,15},{8,0},{9,1},... | collective-permute-start | bytes 196616 | tf_op jit(solution)/shard_map/ppermute | solution.py:27
  117.8 6.6 %collective-permute-start.18 = (bf16[64,512]{1,0:T(8,128)(2,1)S(1)}, bf16[64,512]{1,0:T(8,128)(2,1)S(1)}, u32[]{:S(2)}, u32[]{:S(2)}) collective-permute-start(bf16[64,512]{1,0:T(8,128)(2,1)S(1)} %get-tuple-element.25), channel_id=1, source_target_pairs={{0,12},{1,13},{2,14},{3,15},{4,0},{5,1},{6,2},{7,3},{8,4},{9,5},{1... | collective-permute-start | bytes 196616 | tf_op jit(solution)/shard_map/ppermute | solution.py:27
  (24 other events, 189.6 us)

commit v6 on v4

--- a/solution.py
+++ b/solution.py
@@ -123,7 +123,7 @@
 def encode_kernel(place_ref, *refs):
     block_refs, (bias_ref, w_mine_ref, w_other_ref) = refs[:8], refs[8:11]
     out_refs, table_ref = refs[11:19], refs[19]
-    x_ref, held_ref, sems = refs[20:]
+    x_ref, held_ref, row_ref, sems = refs[20:]
     f32 = jnp.float32
     step = pl.program_id(0)
     half, tile = w_mine_ref.shape
@@ -177,11 +177,14 @@
         for c in range(4):
             whole = extra[2 + 3 * c : 3 + 3 * c] + extra[3 + 3 * c : 4 + 3 * c]
             value += jnp.where(index == c, whole + extra[4 + 3 * c : 5 + 3 * c], 0.0)
+        row_ref[...] = jnp.zeros_like(row_ref)
         for slot in range(8):
             for at, source in enumerate((now, local, value)):
-                table_ref[pl.ds(8 * at + place_ref[8 + slot], 1), :] = source[
+                row_ref[pl.ds(8 * at + place_ref[8 + slot], 1), :rows] = source[
                     :, slot * rows : (slot + 1) * rows
                 ]
+        for i in range(16):
+            table_ref[i] = row_ref[...]
 
 
 def encode(block, place, bias, w_mine, w_other):
@@ -201,15 +204,16 @@
                 pl.BlockSpec((half, tile), lambda i, place: (0, i)),
             ],
             out_specs=[pl.BlockSpec((rows, tile), lambda i, place: (0, i))] * 8
-            + [pl.BlockSpec((24, rows), lambda i, place: (0, 0))],
+            + [pl.BlockSpec((16, 24, 128), lambda i, place: (0, 0, 0))],
             scratch_shapes=[
                 pltpu.VMEM((count, depth), jnp.bfloat16),
                 pltpu.VMEM((count, 128), jnp.float32),
+                pltpu.VMEM((24, 128), jnp.float32),
                 pltpu.SemaphoreType.DMA((8,)),
             ],
         ),
         out_shape=[jax.ShapeDtypeStruct((rows, span), jnp.bfloat16)] * 8
-        + [jax.ShapeDtypeStruct((24, rows), jnp.float32)],
+        + [jax.ShapeDtypeStruct((16, 24, 128), jnp.float32)],
         cost_estimate=pl.CostEstimate(
             flops=4 * count * half * span,
             bytes_accessed=2 * (2 * half * span + count * (depth + span)),
@@ -280,9 +284,8 @@
         block, jnp.concatenate([slot, goal, others]), bias, enc_weight, enc_other
     )
 
-    table = lax.all_to_all(
-        jnp.broadcast_to(outs[8][None], (16, 24, rows)), "tp", 0, 0, tiled=True
-    ).reshape(8, 2, 24, rows)
+    table = lax.all_to_all(outs[8], "tp", 0, 0, tiled=True)
+    table = table[:, :, :rows].reshape(8, 2, 24, rows)
     now = jnp.maximum(table[:, :, :8].sum(axis=0), 0.0)
     now = lax.reduce_precision(now, 8, 7)
     want, delta = table[0, :, 8:16], table[0, :, 16:] - now

time: 137 us -> 136 us (level)
  local copies, waits for them, and re-layouts: 6.09 us -> 4 us
where the time goes in v6:
time: 136 us; the launch traced here: 133 us
  starting transfers between devices  51.8 us (38%)
  waiting for transfers between devices  49.6 us (36%)
  Pallas kernels  12.9 us (9%)
  matrix products  8.77 us (6%)
  other arithmetic  5.11 us (4%)
  local copies, waits for them, and re-layouts  4 us (3%)
    ppermute x10, starting transfers between devices, from_z(): lax.ppermute(value, 'grp', grp_moves(lambda z, plane: (z - ahead) % 8 * 2...  23.5 us
    ppermute x10, waiting for transfers between devices, from_z(): lax.ppermute(value, 'grp', grp_moves(lambda z, plane: (z - ahead) % 8 * 2...  12 us
    ppermute x1, waiting for transfers between devices, flip_z(): lax.ppermute(value, 'grp', grp_moves(lambda z, plane: (z ^ k) * 2 + plane))  9.39 us
    ppermute x7, starting transfers between devices, to_chip(): lax.ppermute(value, 'tp', tp_moves(lambda chip, core: chip_at(chip, dx, d...  9.14 us
    pallas_call x1, Pallas kernels, encode(): pl.pallas_call(encode_kernel, grid_spec=pltpu.PrefetchScalarGridSpec(num_...  8.53 us
    ppermute x7, waiting for transfers between devices, to_chip(): lax.ppermute(value, 'tp', tp_moves(lambda chip, core: chip_at(chip, dx, d...  8.24 us
    all_to_all x1, waiting for transfers between devices, per_device(): lax.all_to_all(part, 'tp', 0, 0, axis_index_groups=groups, tiled=True)  7.68 us
    all_to_all x1, starting transfers between devices, per_device(): lax.all_to_all(part, 'tp', 0, 0, axis_index_groups=groups, tiled=True)  5.97 us
  transfers between devices with their start and end apart: 26, of which 14 were waited for; matrix products, arithmetic and copies ran while one was open for 10% of the time, Pallas kernels for 3%

profile of v6, /device:TPU:8, one launch (start us, length us, event | category | flops | bytes accessed | tf_op | source)
XLA Modules:
  0.0 133.3 jit_solution(17412042470866919132)
XLA Ops:
  3.6 2.9 %select_reduce_fusion = (f32[64,2]{1,0:T(8,128)S(1)}, f32[64,2,128]{2,1,0:T(2,128)S(1)}) fusion(pred[64,128]{1,0:T(8,128)(4,1)S(1)} %iota_compare_fusion.2, bf16[64,2,128]{2,1,0:T(2,128)(2,1)S(1)} %reshape.72, bf16[2,64,1,128,128]{4,3,1,2,0:T(8,128)(2,1)} %bitcast.69), kind=kOutput, calls=%fused_computation.32 | convolution fusion | flops 4243328 | bytes 2204160 | tf_op jit(solution)/shard_map/shd,spd->shp/dot_general | solution.py:61
  6.8 2.3 %fusion.15 = bf16[64,2,128]{2,1,0:T(2,128)(2,1)S(1)} fusion(bf16[2,64,1,128,128]{4,3,1,2,0:T(8,128)(2,1)} %bitcast.70, f32[64,2]{1,0:T(8,128)S(1)} %get-tuple-element.28, f32[64,128]{1,0:T(8,128)S(1)} %bitcast.65, f32[64,2]{1,0:T(8,128)S(1)} %convert_element_type.109, f32[64,2,128]{2,1,0:T(2,128)S(1)} %get-tuple-element.33, ...), kind=kOutput, calls=%fused_computation.21 | convolution fusion | flops 4308992 | bytes 2237952 | tf_op jit(solution)/shard_map/shp,spd->shd/dot_general | solution.py:75
  11.0 4.4 %project.1 = bf16[8,64,512]{2,1,0:T(8,128)(2,1)} custom-call(s32[1]{0:T(128)} %bitcast.core_ref, bf16[64,256]{1,0:T(8,128)(2,1)} %bitcast.60, bf16[64,256]{1,0:T(8,128)(2,1)} %copy-done.7, bf16[256,8192]{1,0:T(8,128)(2,1)} %refs_1_.1, bf16[256,8192]{1,0:T(8,128)(2,1)} %refs_1_.1, bf16[256,8192]{1,0:T(8,128)(2,1)} %collective-permute-done.1.refs_2_.refs_3_, ...), custom_call_target="tpu_custom_call" | custom-call | flops 268435456 | bytes 4194304 | tf_op jit(solution)/shard_map/project/pallas_call | solution.py:105
  15.4 6.0 %all-to-all-start = ((bf16[8,64,512]{2,1,0:T(8,128)(2,1)}), bf16[8,64,512]{2,1,0:T(8,128)(2,1)S(1)}, u32[]{:S(2)}, u32[]{:S(2)}) async-start(bf16[8,64,512]{2,1,0:T(8,128)(2,1)} %project.1), calls=%async_computation | async-start | bytes 1048576 | tf_op jit(solution)/shard_map/all_to_all | solution.py:254
  22.2 7.7 %all-to-all-done = bf16[8,64,512]{2,1,0:T(8,128)(2,1)S(1)} async-done(((bf16[8,64,512]{2,1,0:T(8,128)(2,1)}), bf16[8,64,512]{2,1,0:T(8,128)(2,1)S(1)}, u32[]{:S(2)}, u32[]{:S(2)}) %all-to-all-start) | async-done | bytes 524320 | tf_op jit(solution)/shard_map/all_to_all | solution.py:254
  31.5 4.6 %collective-permute-start.3 = (bf16[64,1152]{1,0:T(8,128)(2,1)S(1)}, bf16[64,1152]{1,0:T(8,128)(2,1)S(1)}, u32[]{:S(2)}, u32[]{:S(2)}) collective-permute-start(bf16[64,1152]{1,0:T(8,128)(2,1)S(1)} %concatenate.20), channel_id=1, source_target_pairs={{0,1},{2,3},{4,5},{6,7},{8,9},{10,11},{12,13},{14,15},{17,16},{19,... | collective-permute-start | bytes 442376 | tf_op jit(solution)/shard_map/ppermute | solution.py:269
  36.2 2.6 %collective-permute-done.3 = bf16[64,1152]{1,0:T(8,128)(2,1)S(1)} collective-permute-done((bf16[64,1152]{1,0:T(8,128)(2,1)S(1)}, bf16[64,1152]{1,0:T(8,128)(2,1)S(1)}, u32[]{:S(2)}, u32[]{:S(2)}) %collective-permute-start.3) | collective-permute-done | bytes 147488 | tf_op jit(solution)/shard_map/ppermute | solution.py:269
  38.8 6.4 %collective-permute-start.5 = (bf16[64,1152]{1,0:T(8,128)(2,1)S(1)}, bf16[64,1152]{1,0:T(8,128)(2,1)S(1)}, u32[]{:S(2)}, u32[]{:S(2)}) collective-permute-start(bf16[64,1152]{1,0:T(8,128)(2,1)S(1)} %broadcast_select_fusion.refs_0_), channel_id=1, source_target_pairs={{0,12},{1,13},{2,14},{3,15},{4,0},{5,1},{6,2},{7,3},{8,4},{9,5},{1... | collective-permute-start | bytes 442376 | tf_op jit(solution)/shard_map/ppermute | solution.py:27
  46.8 2.7 %collective-permute-start.4 = (bf16[64,1152]{1,0:T(8,128)(2,1)S(1)}, bf16[64,1152]{1,0:T(8,128)(2,1)S(1)}, u32[]{:S(2)}, u32[]{:S(2)}) collective-permute-start(bf16[64,1152]{1,0:T(8,128)(2,1)S(1)} %broadcast_select_fusion.refs_0_), channel_id=1, source_target_pairs={{0,14},{1,15},{2,0},{3,1},{4,2},{5,3},{6,4},{7,5},{8,6},{9,7},{10,... | collective-permute-start | bytes 442376 | tf_op jit(solution)/shard_map/ppermute | solution.py:27
  49.5 2.8 %collective-permute-done.5.refs_2_ = bf16[64,1152]{1,0:T(8,128)(2,1)S(1)} collective-permute-done((bf16[64,1152]{1,0:T(8,128)(2,1)S(1)}, bf16[64,1152]{1,0:T(8,128)(2,1)S(1)}, u32[]{:S(2)}, u32[]{:S(2)}) %collective-permute-start.5) | collective-permute-done | bytes 147488 | tf_op jit(solution)/shard_map/ppermute | solution.py:27
  52.3 2.7 %collective-permute-start.6 = (bf16[64,1152]{1,0:T(8,128)(2,1)S(1)}, bf16[64,1152]{1,0:T(8,128)(2,1)S(1)}, u32[]{:S(2)}, u32[]{:S(2)}) collective-permute-start(bf16[64,1152]{1,0:T(8,128)(2,1)S(1)} %collective-permute-done.5.refs_2_), channel_id=1, source_target_pairs={{0,14},{1,15},{2,0},{3,1},{4,2},{5,3},{6,4},{7,5},{8,6},{9,7},{10,... | collective-permute-start | bytes 442376 | tf_op jit(solution)/shard_map/ppermute | solution.py:27
  60.0 4.5 %collective-permute-done.7.refs_4_ = bf16[64,1152]{1,0:T(8,128)(2,1)S(1)} collective-permute-done((bf16[64,1152]{1,0:T(8,128)(2,1)S(1)}, bf16[64,1152]{1,0:T(8,128)(2,1)S(1)}, u32[]{:S(2)}, u32[]{:S(2)}) %collective-permute-start.7) | collective-permute-done | bytes 147488 | tf_op jit(solution)/shard_map/ppermute | solution.py:27
  65.3 8.5 %encode.1 = (bf16[64,2048]{1,0:T(8,128)(2,1)}, bf16[64,2048]{1,0:T(8,128)(2,1)}, bf16[64,2048]{1,0:T(8,128)(2,1)}, bf16[64,2048]{1,0:T(8,128)(2,1)}, bf16[64,204...) custom-call(s32[18]{0:T(128)} %pad_add_fusion.place_ref, ...), custom_call_target="tpu_custom_call" | custom-call | flops 2147483648 | bytes 7471104 | tf_op jit(solution)/shard_map/encode/pallas_call | solution.py:195
  73.8 4.8 %all-to-all-start.1 = ((f32[16,24,128]{2,1,0:T(8,128)}), f32[16,24,128]{2,1,0:T(8,128)S(1)}, u32[]{:S(2)}, u32[]{:S(2)}) async-start(f32[16,24,128]{2,1,0:T(8,128)} %get-tuple-element.11), calls=%async_computation.1 | async-start | bytes 393216 | tf_op jit(solution)/shard_map/all_to_all | solution.py:287
  78.6 5.0 %all-to-all-done.1 = f32[16,24,128]{2,1,0:T(8,128)S(1)} async-done(((f32[16,24,128]{2,1,0:T(8,128)}), f32[16,24,128]{2,1,0:T(8,128)S(1)}, u32[]{:S(2)}, u32[]{:S(2)}) %all-to-all-start.1) | async-done | bytes 196640 | tf_op jit(solution)/shard_map/all_to_all | solution.py:287
  87.4 2.5 %collective-permute-start.20 = (bf16[64,2048]{1,0:T(8,128)(2,1)}, bf16[64,2048]{1,0:T(8,128)(2,1)S(1)}, u32[]{:S(2)}, u32[]{:S(2)}) collective-permute-start(bf16[64,2048]{1,0:T(8,128)(2,1)} %get-tuple-element.17), channel_id=1, source_target_pairs={{0,96},{16,112},{32,0},{48,16},{64,32},{80,48},{96,64},{112,80},{1... | collective-permute-start | bytes 786440 | tf_op jit(solution)/shard_map/ppermute | solution.py:45
  91.4 9.4 %collective-permute-done.12 = bf16[512,512]{1,0:T(8,128)(2,1)S(1)} collective-permute-done((bf16[512,512]{1,0:T(8,128)(2,1)}, bf16[512,512]{1,0:T(8,128)(2,1)S(1)}, u32[]{:S(2)}, u32[]{:S(2)}) %collective-permute-start.12) | collective-permute-done | bytes 524320 | tf_op jit(solution)/shard_map/ppermute | solution.py:33
  106.1 2.5 %collective-permute-start.21 = (bf16[64,2048]{1,0:T(8,128)(2,1)S(1)}, bf16[64,2048]{1,0:T(8,128)(2,1)S(1)}, u32[]{:S(2)}, u32[]{:S(2)}) collective-permute-start(bf16[64,2048]{1,0:T(8,128)(2,1)S(1)} %add.177), channel_id=1, source_target_pairs={{0,224},{16,240},{32,128},{48,144},{64,160},{80,176},{96,192},{112... | collective-permute-start | bytes 786440 | tf_op jit(solution)/shard_map/ppermute | solution.py:45
  108.6 3.0 %collective-permute-done.13 = bf16[256,512]{1,0:T(8,128)(2,1)S(1)} collective-permute-done((bf16[256,512]{1,0:T(8,128)(2,1)S(1)}, bf16[256,512]{1,0:T(8,128)(2,1)S(1)}, u32[]{:S(2)}, u32[]{:S(2)}) %collective-permute-start.13) | collective-permute-done | bytes 262176 | tf_op jit(solution)/shard_map/ppermute | solution.py:37
  112.4 3.1 %collective-permute-done.17 = bf16[64,2048]{1,0:T(8,128)(2,1)S(1)} collective-permute-done((bf16[64,2048]{1,0:T(8,128)(2,1)S(1)}, bf16[64,2048]{1,0:T(8,128)(2,1)S(1)}, u32[]{:S(2)}, u32[]{:S(2)}) %collective-permute-start.17) | collective-permute-done | bytes 262176 | tf_op jit(solution)/shard_map/ppermute | solution.py:45
  117.0 5.2 %collective-permute-done.18 = bf16[64,2048]{1,0:T(8,128)(2,1)S(1)} collective-permute-done((bf16[64,2048]{1,0:T(8,128)(2,1)S(1)}, bf16[64,2048]{1,0:T(8,128)(2,1)S(1)}, u32[]{:S(2)}, u32[]{:S(2)}) %collective-permute-start.18) | collective-permute-done | bytes 262176 | tf_op jit(solution)/shard_map/ppermute | solution.py:45
  122.1 4.2 %collective-permute-start.15 = (bf16[64,512]{1,0:T(8,128)(2,1)S(1)}, bf16[64,512]{1,0:T(8,128)(2,1)S(1)}, u32[]{:S(2)}, u32[]{:S(2)}) collective-permute-start(bf16[64,512]{1,0:T(8,128)(2,1)S(1)} %get-tuple-element.24), channel_id=1, source_target_pairs={{0,8},{1,9},{2,10},{3,11},{4,12},{5,13},{6,14},{7,15},{8,0},{9,1},... | collective-permute-start | bytes 196616 | tf_op jit(solution)/shard_map/ppermute | solution.py:27
  128.2 2.2 %collective-permute-done.15 = bf16[64,512]{1,0:T(8,128)(2,1)S(1)} collective-permute-done((bf16[64,512]{1,0:T(8,128)(2,1)S(1)}, bf16[64,512]{1,0:T(8,128)(2,1)S(1)}, u32[]{:S(2)}, u32[]{:S(2)}) %collective-permute-start.15) | collective-permute-done | bytes 65568 | tf_op jit(solution)/shard_map/ppermute | solution.py:27
  130.4 2.2 %collective-permute-done.16 = bf16[64,512]{1,0:T(8,128)(2,1)S(1)} collective-permute-done((bf16[64,512]{1,0:T(8,128)(2,1)S(1)}, bf16[64,512]{1,0:T(8,128)(2,1)S(1)}, u32[]{:S(2)}, u32[]{:S(2)}) %collective-permute-start.16) | collective-permute-done | bytes 65568 | tf_op jit(solution)/shard_map/ppermute | solution.py:27
  (129 shorter events, 30.2 us)
Async XLA Ops:
  0.6 9.8 %collective-permute-start.1 = (bf16[256,8192]{1,0:T(8,128)(2,1)}, bf16[256,8192]{1,0:T(8,128)(2,1)}, u32[]{:S(2)}, u32[]{:S(2)}) collective-permute-start(bf16[256,8192]{1,0:T(8,128)(2,1)} %refs_1_.1), channel_id=1, source_target_pairs={{0,16},{16,0},{32,48},{48,32},{64,80},{80,64},{96,112},{112,96},{1... | collective-permute-start | bytes 12582920 | tf_op jit(solution)/shard_map/ppermute | solution.py:23
  9.6 45.4 %collective-permute-start.11 = (bf16[512,2048]{1,0:T(8,128)(2,1)}, bf16[512,2048]{1,0:T(8,128)(2,1)}, u32[]{:S(2)}, u32[]{:S(2)}) collective-permute-start(bf16[512,2048]{1,0:T(8,128)(2,1)} %refs_9_.1), channel_id=1, source_target_pairs={{0,16},{16,0},{32,48},{48,32},{64,80},{80,64},{96,112},{112,96},{1... | collective-permute-start | bytes 6291464 | tf_op jit(solution)/shard_map/ppermute | solution.py:23
  15.4 14.5 %all-to-all-start = ((bf16[8,64,512]{2,1,0:T(8,128)(2,1)}), bf16[8,64,512]{2,1,0:T(8,128)(2,1)S(1)}, u32[]{:S(2)}, u32[]{:S(2)}) async-start(bf16[8,64,512]{2,1,0:T(8,128)(2,1)} %project.1), calls=%async_computation | async-start | bytes 1048576 | tf_op jit(solution)/shard_map/all_to_all | solution.py:254
  31.5 7.3 %collective-permute-start.3 = (bf16[64,1152]{1,0:T(8,128)(2,1)S(1)}, bf16[64,1152]{1,0:T(8,128)(2,1)S(1)}, u32[]{:S(2)}, u32[]{:S(2)}) collective-permute-start(bf16[64,1152]{1,0:T(8,128)(2,1)S(1)} %concatenate.20), channel_id=1, source_target_pairs={{0,1},{2,3},{4,5},{6,7},{8,9},{10,11},{12,13},{14,15},{17,16},{19,... | collective-permute-start | bytes 442376 | tf_op jit(solution)/shard_map/ppermute | solution.py:269
  38.8 13.5 %collective-permute-start.5 = (bf16[64,1152]{1,0:T(8,128)(2,1)S(1)}, bf16[64,1152]{1,0:T(8,128)(2,1)S(1)}, u32[]{:S(2)}, u32[]{:S(2)}) collective-permute-start(bf16[64,1152]{1,0:T(8,128)(2,1)S(1)} %broadcast_select_fusion.refs_0_), channel_id=1, source_target_pairs={{0,12},{1,13},{2,14},{3,15},{4,0},{5,1},{6,2},{7,3},{8,4},{9,5},{1... | collective-permute-start | bytes 442376 | tf_op jit(solution)/shard_map/ppermute | solution.py:27
  45.2 11.9 %collective-permute-start.8 = (bf16[64,1152]{1,0:T(8,128)(2,1)S(1)}, bf16[64,1152]{1,0:T(8,128)(2,1)S(1)}, u32[]{:S(2)}, u32[]{:S(2)}) collective-permute-start(bf16[64,1152]{1,0:T(8,128)(2,1)S(1)} %broadcast_select_fusion.refs_0_), channel_id=1, source_target_pairs={{0,4},{1,5},{2,6},{3,7},{4,8},{5,9},{6,10},{7,11},{8,12},{9,13},{1... | collective-permute-start | bytes 442376 | tf_op jit(solution)/shard_map/ppermute | solution.py:27
  45.8 14.0 %collective-permute-start.10 = (bf16[64,1152]{1,0:T(8,128)(2,1)S(1)}, bf16[64,1152]{1,0:T(8,128)(2,1)S(1)}, u32[]{:S(2)}, u32[]{:S(2)}) collective-permute-start(bf16[64,1152]{1,0:T(8,128)(2,1)S(1)} %broadcast_select_fusion.refs_0_), channel_id=1, source_target_pairs={{0,2},{1,3},{2,4},{3,5},{4,6},{5,7},{6,8},{7,9},{8,10},{9,11},{10,... | collective-permute-start | bytes 442376 | tf_op jit(solution)/shard_map/ppermute | solution.py:27
  46.8 13.0 %collective-permute-start.4 = (bf16[64,1152]{1,0:T(8,128)(2,1)S(1)}, bf16[64,1152]{1,0:T(8,128)(2,1)S(1)}, u32[]{:S(2)}, u32[]{:S(2)}) collective-permute-start(bf16[64,1152]{1,0:T(8,128)(2,1)S(1)} %broadcast_select_fusion.refs_0_), channel_id=1, source_target_pairs={{0,14},{1,15},{2,0},{3,1},{4,2},{5,3},{6,4},{7,5},{8,6},{9,7},{10,... | collective-permute-start | bytes 442376 | tf_op jit(solution)/shard_map/ppermute | solution.py:27
  52.3 7.7 %collective-permute-start.6 = (bf16[64,1152]{1,0:T(8,128)(2,1)S(1)}, bf16[64,1152]{1,0:T(8,128)(2,1)S(1)}, u32[]{:S(2)}, u32[]{:S(2)}) collective-permute-start(bf16[64,1152]{1,0:T(8,128)(2,1)S(1)} %collective-permute-done.5.refs_2_), channel_id=1, source_target_pairs={{0,14},{1,15},{2,0},{3,1},{4,2},{5,3},{6,4},{7,5},{8,6},{9,7},{10,... | collective-permute-start | bytes 442376 | tf_op jit(solution)/shard_map/ppermute | solution.py:27
  55.0 9.6 %collective-permute-start.7 = (bf16[64,1152]{1,0:T(8,128)(2,1)S(1)}, bf16[64,1152]{1,0:T(8,128)(2,1)S(1)}, u32[]{:S(2)}, u32[]{:S(2)}) collective-permute-start(bf16[64,1152]{1,0:T(8,128)(2,1)S(1)} %collective-permute-done.5.refs_2_), channel_id=1, source_target_pairs={{0,12},{1,13},{2,14},{3,15},{4,0},{5,1},{6,2},{7,3},{8,4},{9,5},{1... | collective-permute-start | bytes 442376 | tf_op jit(solution)/shard_map/ppermute | solution.py:27
  57.1 7.4 %collective-permute-start.9 = (bf16[64,1152]{1,0:T(8,128)(2,1)S(1)}, bf16[64,1152]{1,0:T(8,128)(2,1)S(1)}, u32[]{:S(2)}, u32[]{:S(2)}) collective-permute-start(bf16[64,1152]{1,0:T(8,128)(2,1)S(1)} %collective-permute-done.8.refs_6_), channel_id=1, source_target_pairs={{0,2},{1,3},{2,4},{3,5},{4,6},{5,7},{6,8},{7,9},{8,10},{9,11},{10,... | collective-permute-start | bytes 442376 | tf_op jit(solution)/shard_map/ppermute | solution.py:27
  73.8 9.8 %all-to-all-start.1 = ((f32[16,24,128]{2,1,0:T(8,128)}), f32[16,24,128]{2,1,0:T(8,128)S(1)}, u32[]{:S(2)}, u32[]{:S(2)}) async-start(f32[16,24,128]{2,1,0:T(8,128)} %get-tuple-element.11), calls=%async_computation.1 | async-start | bytes 393216 | tf_op jit(solution)/shard_map/all_to_all | solution.py:287
  86.0 14.7 %collective-permute-start.12 = (bf16[512,512]{1,0:T(8,128)(2,1)}, bf16[512,512]{1,0:T(8,128)(2,1)S(1)}, u32[]{:S(2)}, u32[]{:S(2)}) collective-permute-start(bf16[512,512]{1,0:T(8,128)(2,1)} %fusion.10), channel_id=1, source_target_pairs={{0,2},{1,3},{2,0},{3,1},{4,6},{5,7},{6,4},{7,5},{8,10},{9,11},{10,... | collective-permute-start | bytes 1572872 | tf_op jit(solution)/shard_map/ppermute | solution.py:33
  87.4 17.3 %collective-permute-start.20 = (bf16[64,2048]{1,0:T(8,128)(2,1)}, bf16[64,2048]{1,0:T(8,128)(2,1)S(1)}, u32[]{:S(2)}, u32[]{:S(2)}) collective-permute-start(bf16[64,2048]{1,0:T(8,128)(2,1)} %get-tuple-element.17), channel_id=1, source_target_pairs={{0,96},{16,112},{32,0},{48,16},{64,32},{80,48},{96,64},{112,80},{1... | collective-permute-start | bytes 786440 | tf_op jit(solution)/shard_map/ppermute | solution.py:45
  89.8 16.2 %collective-permute-start.22 = (bf16[64,2048]{1,0:T(8,128)(2,1)S(1)}, bf16[64,2048]{1,0:T(8,128)(2,1)S(1)}, u32[]{:S(2)}, u32[]{:S(2)}) collective-permute-start(bf16[64,2048]{1,0:T(8,128)(2,1)S(1)} %copy-done.13), channel_id=1, source_target_pairs={{0,32},{16,48},{32,64},{48,80},{64,96},{80,112},{96,0},{112,16},{1... | collective-permute-start | bytes 786440 | tf_op jit(solution)/shard_map/ppermute | solution.py:45
  100.8 10.8 %collective-permute-start.13 = (bf16[256,512]{1,0:T(8,128)(2,1)S(1)}, bf16[256,512]{1,0:T(8,128)(2,1)S(1)}, u32[]{:S(2)}, u32[]{:S(2)}) collective-permute-start(bf16[256,512]{1,0:T(8,128)(2,1)S(1)} %slice_add_fusion), channel_id=1, source_target_pairs={{0,1},{1,0},{2,3},{3,2},{4,5},{5,4},{6,7},{7,6},{8,9},{9,8},{10,11... | collective-permute-start | bytes 786440 | tf_op jit(solution)/shard_map/ppermute | solution.py:37
  102.5 12.9 %collective-permute-start.17 = (bf16[64,2048]{1,0:T(8,128)(2,1)S(1)}, bf16[64,2048]{1,0:T(8,128)(2,1)S(1)}, u32[]{:S(2)}, u32[]{:S(2)}) collective-permute-start(bf16[64,2048]{1,0:T(8,128)(2,1)S(1)} %copy-done.12), channel_id=1, source_target_pairs={{0,128},{16,144},{32,160},{48,176},{64,192},{80,208},{96,224},{112... | collective-permute-start | bytes 786440 | tf_op jit(solution)/shard_map/ppermute | solution.py:45
  102.7 19.5 %collective-permute-start.18 = (bf16[64,2048]{1,0:T(8,128)(2,1)S(1)}, bf16[64,2048]{1,0:T(8,128)(2,1)S(1)}, u32[]{:S(2)}, u32[]{:S(2)}) collective-permute-start(bf16[64,2048]{1,0:T(8,128)(2,1)S(1)} %copy-done.11), channel_id=1, source_target_pairs={{0,160},{16,176},{32,192},{48,208},{64,224},{80,240},{96,128},{112... | collective-permute-start | bytes 786440 | tf_op jit(solution)/shard_map/ppermute | solution.py:45
  104.7 21.7 %collective-permute-start.19 = (bf16[64,2048]{1,0:T(8,128)(2,1)S(1)}, bf16[64,2048]{1,0:T(8,128)(2,1)S(1)}, u32[]{:S(2)}, u32[]{:S(2)}) collective-permute-start(bf16[64,2048]{1,0:T(8,128)(2,1)S(1)} %copy-done.10), channel_id=1, source_target_pairs={{0,96},{16,112},{32,0},{48,16},{64,32},{80,48},{96,64},{112,80},{1... | collective-permute-start | bytes 786440 | tf_op jit(solution)/shard_map/ppermute | solution.py:45
  106.1 21.2 %collective-permute-start.21 = (bf16[64,2048]{1,0:T(8,128)(2,1)S(1)}, bf16[64,2048]{1,0:T(8,128)(2,1)S(1)}, u32[]{:S(2)}, u32[]{:S(2)}) collective-permute-start(bf16[64,2048]{1,0:T(8,128)(2,1)S(1)} %add.177), channel_id=1, source_target_pairs={{0,224},{16,240},{32,128},{48,144},{64,160},{80,176},{96,192},{112... | collective-permute-start | bytes 786440 | tf_op jit(solution)/shard_map/ppermute | solution.py:45
  111.6 15.6 %collective-permute-start.23 = (bf16[64,2048]{1,0:T(8,128)(2,1)S(1)}, bf16[64,2048]{1,0:T(8,128)(2,1)S(1)}, u32[]{:S(2)}, u32[]{:S(2)}) collective-permute-start(bf16[64,2048]{1,0:T(8,128)(2,1)S(1)} %add.179), channel_id=1, source_target_pairs={{0,32},{16,48},{32,64},{48,80},{64,96},{80,112},{96,0},{112,16},{1... | collective-permute-start | bytes 786440 | tf_op jit(solution)/shard_map/ppermute | solution.py:45
  115.4 12.8 %collective-permute-start.14 = (bf16[64,512]{1,0:T(8,128)(2,1)S(1)}, bf16[64,512]{1,0:T(8,128)(2,1)S(1)}, u32[]{:S(2)}, u32[]{:S(2)}) collective-permute-start(bf16[64,512]{1,0:T(8,128)(2,1)S(1)} %get-tuple-element.22), channel_id=1, source_target_pairs={{0,4},{1,5},{2,6},{3,7},{4,8},{5,9},{6,10},{7,11},{8,12},{9,13},{1... | collective-permute-start | bytes 196616 | tf_op jit(solution)/shard_map/ppermute | solution.py:27
  122.1 8.2 %collective-permute-start.15 = (bf16[64,512]{1,0:T(8,128)(2,1)S(1)}, bf16[64,512]{1,0:T(8,128)(2,1)S(1)}, u32[]{:S(2)}, u32[]{:S(2)}) collective-permute-start(bf16[64,512]{1,0:T(8,128)(2,1)S(1)} %get-tuple-element.24), channel_id=1, source_target_pairs={{0,8},{1,9},{2,10},{3,11},{4,12},{5,13},{6,14},{7,15},{8,0},{9,1},... | collective-permute-start | bytes 196616 | tf_op jit(solution)/shard_map/ppermute | solution.py:27
  126.4 6.2 %collective-permute-start.16 = (bf16[64,512]{1,0:T(8,128)(2,1)S(1)}, bf16[64,512]{1,0:T(8,128)(2,1)S(1)}, u32[]{:S(2)}, u32[]{:S(2)}) collective-permute-start(bf16[64,512]{1,0:T(8,128)(2,1)S(1)} %get-tuple-element.23), channel_id=1, source_target_pairs={{0,12},{1,13},{2,14},{3,15},{4,0},{5,1},{6,2},{7,3},{8,4},{9,5},{1... | collective-permute-start | bytes 196616 | tf_op jit(solution)/shard_map/ppermute | solution.py:27
  (23 other events, 316.7 us)

commit v7 on v6

--- a/solution.py
+++ b/solution.py
@@ -290,23 +290,31 @@
     now = lax.reduce_precision(now, 8, 7)
     want, delta = table[0, :, 8:16], table[0, :, 16:] - now
 
+    even_z = z % 2 == 0
+    half = width // 2
+
     def arrange(value):
         value = jnp.where(plane == 1, value, value[::-1])
         odd = value[:, 1::2]
-        odd = jnp.where(z % 2 == 0, odd, jnp.concatenate([odd[:, 3:], odd[:, :3]], axis=1))
-        return odd.reshape(8 * rows), value[:, 0::2].reshape(8 * rows)
-
-    def decode(want, delta):
+        turned = jnp.concatenate([odd[:, 3:], odd[:, :3]], axis=1)
+        parts = jnp.where(even_z, odd, turned), jnp.where(even_z, turned, odd), value[:, 0::2]
+        return [part.reshape(8 * rows) for part in parts]
+
+    def decode(want, delta, weight):
         column = jnp.arange(span, dtype=jnp.int32)[None, :]
         hits = jnp.where(column == want.astype(jnp.int32)[:, None], delta[:, None], 0.0)
-        return mm(hits.astype(bf16), dec_weight)
-
-    want_give, want_keep = arrange(want)
-    delta_give, delta_keep = arrange(delta)
-    give = decode(want_give, delta_give).astype(bf16)
-    near = flip_z(give, 1)
-    keep = decode(want_keep, delta_keep).astype(bf16)
+        return mm(hits.astype(bf16), weight).astype(bf16)
+
+    wants, deltas = arrange(want), arrange(delta)
+    give = decode(wants[0], deltas[0], dec_weight[:, :half])
+    near_left = flip_z(give, 1)
+    give = decode(wants[1], deltas[1], dec_weight[:, half:])
+    near_right = lax.ppermute(
+        give, "grp", grp_moves(lambda z_, s: (z_ + (7 if z_ % 2 == 0 else 1)) % 8 * 2 + s)
+    )
+    keep = decode(wants[2], deltas[2], dec_weight)
     first, last = slice(0, 4 * rows), slice(4 * rows, 8 * rows)
+    near = jnp.concatenate([near_left, near_right], axis=1)
     near_2 = flip_plane(keep[first] + near[first])
     found = keep[last] + near[last] + near_2
     edit = found[:rows].astype(f32)

time: 136 us -> 131 us (0.963)
  waiting for transfers between devices: 49.6 us -> 45.4 us
    ppermute x0 -> x1, starting transfers between devices: none -> 2.75 us  [per_device(): lax.ppermute(give, 'grp', grp_moves(lambda z_, s: (z_ + (7 if z_ % 2 == 0...]
    ppermute x1, waiting for transfers between devices: 9.39 us -> 7.37 us  [flip_z(): lax.ppermute(value, 'grp', grp_moves(lambda z, plane: (z ^ k) * 2 + plane))]
    all_to_all x1, waiting for transfers between devices: 4.97 us -> 2.95 us  [per_device(): table = lax.all_to_all(outs[8], 'tp', 0, 0, tiled=True)]
    dot_general x2 -> x3, matrix products: 3.39 us -> 2.8 us  [mm(): return jnp.dot(a, b, preferred_element_type=jnp.float32)]
  transfers between devices with their start and end apart: 26 -> 27, of which waited for: 14 -> 14; matrix products, arithmetic and copies ran while one was open for 10% -> 12% of each run, Pallas kernels for 3% -> 3%
where the time goes in v7:
time: 131 us; the launch traced here: 129 us
  starting transfers between devices  51.8 us (40%)
  waiting for transfers between devices  45.4 us (35%)
  Pallas kernels  13 us (10%)
  matrix products  8.32 us (6%)
  other arithmetic  5.09 us (4%)
  local copies, waits for them, and re-layouts  4.07 us (3%)
    ppermute x10, starting transfers between devices, from_z(): lax.ppermute(value, 'grp', grp_moves(lambda z, plane: (z - ahead) % 8 * 2...  22.4 us
    ppermute x10, waiting for transfers between devices, from_z(): lax.ppermute(value, 'grp', grp_moves(lambda z, plane: (z - ahead) % 8 * 2...  11.2 us
    pallas_call x1, Pallas kernels, encode(): pl.pallas_call(encode_kernel, grid_spec=pltpu.PrefetchScalarGridSpec(num_...  8.66 us
    ppermute x7, waiting for transfers between devices, to_chip(): lax.ppermute(value, 'tp', tp_moves(lambda chip, core: chip_at(chip, dx, d...  8.62 us
    ppermute x7, starting transfers between devices, to_chip(): lax.ppermute(value, 'tp', tp_moves(lambda chip, core: chip_at(chip, dx, d...  8.59 us
    all_to_all x1, waiting for transfers between devices, per_device(): lax.all_to_all(part, 'tp', 0, 0, axis_index_groups=groups, tiled=True)  7.69 us
    ppermute x1, waiting for transfers between devices, flip_z(): lax.ppermute(value, 'grp', grp_moves(lambda z, plane: (z ^ k) * 2 + plane))  7.37 us
    all_to_all x1, starting transfers between devices, per_device(): lax.all_to_all(part, 'tp', 0, 0, axis_index_groups=groups, tiled=True)  5.97 us
  transfers between devices with their start and end apart: 27, of which 14 were waited for; matrix products, arithmetic and copies ran while one was open for 12% of the time, Pallas kernels for 3%

profile of v7, /device:TPU:8, one launch (start us, length us, event | category | flops | bytes accessed | tf_op | source)
XLA Modules:
  0.0 128.9 jit_solution(9057597748732667778)
XLA Ops:
  3.5 2.9 %select_reduce_fusion = (f32[64,2]{1,0:T(8,128)S(1)}, f32[64,2,128]{2,1,0:T(2,128)S(1)}) fusion(pred[64,128]{1,0:T(8,128)(4,1)S(1)} %iota_compare_fusion.3, bf16[64,2,128]{2,1,0:T(2,128)(2,1)S(1)} %reshape.80, bf16[2,64,1,128,128]{4,3,1,2,0:T(8,128)(2,1)} %bitcast.68), kind=kOutput, calls=%fused_computation.41 | convolution fusion | flops 4243328 | bytes 2204160 | tf_op jit(solution)/shard_map/shd,spd->shp/dot_general | solution.py:61
  6.6 2.5 %fusion.20 = bf16[64,2,128]{2,1,0:T(2,128)(2,1)S(1)} fusion(bf16[2,64,1,128,128]{4,3,1,2,0:T(8,128)(2,1)} %bitcast.69, f32[64,2]{1,0:T(8,128)S(1)} %get-tuple-element.28, f32[64,128]{1,0:T(8,128)S(1)} %bitcast.64, f32[64,2]{1,0:T(8,128)S(1)} %convert_element_type.125, f32[64,2,128]{2,1,0:T(2,128)S(1)} %get-tuple-element.37, ...), kind=kOutput, calls=%fused_computation.28 | convolution fusion | flops 4308992 | bytes 2237952 | tf_op jit(solution)/shard_map/shp,spd->shd/dot_general | solution.py:75
  11.2 4.4 %project.1 = bf16[8,64,512]{2,1,0:T(8,128)(2,1)} custom-call(s32[1]{0:T(128)} %bitcast.core_ref, bf16[64,256]{1,0:T(8,128)(2,1)} %bitcast.59, bf16[64,256]{1,0:T(8,128)(2,1)} %copy-done.6, bf16[256,8192]{1,0:T(8,128)(2,1)} %refs_1_.1, bf16[256,8192]{1,0:T(8,128)(2,1)} %refs_1_.1, bf16[256,8192]{1,0:T(8,128)(2,1)} %collective-permute-done.1.refs_2_.refs_3_, ...), custom_call_target="tpu_custom_call" | custom-call | flops 268435456 | bytes 4194304 | tf_op jit(solution)/shard_map/project/pallas_call | solution.py:105
  15.6 6.0 %all-to-all-start = ((bf16[8,64,512]{2,1,0:T(8,128)(2,1)}), bf16[8,64,512]{2,1,0:T(8,128)(2,1)S(1)}, u32[]{:S(2)}, u32[]{:S(2)}) async-start(bf16[8,64,512]{2,1,0:T(8,128)(2,1)} %project.1), calls=%async_computation | async-start | bytes 1048576 | tf_op jit(solution)/shard_map/all_to_all | solution.py:254
  22.4 7.7 %all-to-all-done = bf16[8,64,512]{2,1,0:T(8,128)(2,1)S(1)} async-done(((bf16[8,64,512]{2,1,0:T(8,128)(2,1)}), bf16[8,64,512]{2,1,0:T(8,128)(2,1)S(1)}, u32[]{:S(2)}, u32[]{:S(2)}) %all-to-all-start) | async-done | bytes 524320 | tf_op jit(solution)/shard_map/all_to_all | solution.py:254
  31.6 4.6 %collective-permute-start.3 = (bf16[64,1152]{1,0:T(8,128)(2,1)S(1)}, bf16[64,1152]{1,0:T(8,128)(2,1)S(1)}, u32[]{:S(2)}, u32[]{:S(2)}) collective-permute-start(bf16[64,1152]{1,0:T(8,128)(2,1)S(1)} %concatenate.23), channel_id=1, source_target_pairs={{0,1},{2,3},{4,5},{6,7},{8,9},{10,11},{12,13},{14,15},{17,16},{19,... | collective-permute-start | bytes 442376 | tf_op jit(solution)/shard_map/ppermute | solution.py:269
  36.3 2.6 %collective-permute-done.3 = bf16[64,1152]{1,0:T(8,128)(2,1)S(1)} collective-permute-done((bf16[64,1152]{1,0:T(8,128)(2,1)S(1)}, bf16[64,1152]{1,0:T(8,128)(2,1)S(1)}, u32[]{:S(2)}, u32[]{:S(2)}) %collective-permute-start.3) | collective-permute-done | bytes 147488 | tf_op jit(solution)/shard_map/ppermute | solution.py:269
  39.0 6.4 %collective-permute-start.5 = (bf16[64,1152]{1,0:T(8,128)(2,1)S(1)}, bf16[64,1152]{1,0:T(8,128)(2,1)S(1)}, u32[]{:S(2)}, u32[]{:S(2)}) collective-permute-start(bf16[64,1152]{1,0:T(8,128)(2,1)S(1)} %broadcast_select_fusion.refs_0_), channel_id=1, source_target_pairs={{0,12},{1,13},{2,14},{3,15},{4,0},{5,1},{6,2},{7,3},{8,4},{9,5},{1... | collective-permute-start | bytes 442376 | tf_op jit(solution)/shard_map/ppermute | solution.py:27
  47.0 2.7 %collective-permute-start.4 = (bf16[64,1152]{1,0:T(8,128)(2,1)S(1)}, bf16[64,1152]{1,0:T(8,128)(2,1)S(1)}, u32[]{:S(2)}, u32[]{:S(2)}) collective-permute-start(bf16[64,1152]{1,0:T(8,128)(2,1)S(1)} %broadcast_select_fusion.refs_0_), channel_id=1, source_target_pairs={{0,14},{1,15},{2,0},{3,1},{4,2},{5,3},{6,4},{7,5},{8,6},{9,7},{10,... | collective-permute-start | bytes 442376 | tf_op jit(solution)/shard_map/ppermute | solution.py:27
  49.6 2.8 %collective-permute-done.5.refs_2_ = bf16[64,1152]{1,0:T(8,128)(2,1)S(1)} collective-permute-done((bf16[64,1152]{1,0:T(8,128)(2,1)S(1)}, bf16[64,1152]{1,0:T(8,128)(2,1)S(1)}, u32[]{:S(2)}, u32[]{:S(2)}) %collective-permute-start.5) | collective-permute-done | bytes 147488 | tf_op jit(solution)/shard_map/ppermute | solution.py:27
  52.4 2.7 %collective-permute-start.6 = (bf16[64,1152]{1,0:T(8,128)(2,1)S(1)}, bf16[64,1152]{1,0:T(8,128)(2,1)S(1)}, u32[]{:S(2)}, u32[]{:S(2)}) collective-permute-start(bf16[64,1152]{1,0:T(8,128)(2,1)S(1)} %collective-permute-done.5.refs_2_), channel_id=1, source_target_pairs={{0,14},{1,15},{2,0},{3,1},{4,2},{5,3},{6,4},{7,5},{8,6},{9,7},{10,... | collective-permute-start | bytes 442376 | tf_op jit(solution)/shard_map/ppermute | solution.py:27
  55.1 2.1 %collective-permute-start.7 = (bf16[64,1152]{1,0:T(8,128)(2,1)S(1)}, bf16[64,1152]{1,0:T(8,128)(2,1)S(1)}, u32[]{:S(2)}, u32[]{:S(2)}) collective-permute-start(bf16[64,1152]{1,0:T(8,128)(2,1)S(1)} %collective-permute-done.5.refs_2_), channel_id=1, source_target_pairs={{0,12},{1,13},{2,14},{3,15},{4,0},{5,1},{6,2},{7,3},{8,4},{9,5},{1... | collective-permute-start | bytes 442376 | tf_op jit(solution)/shard_map/ppermute | solution.py:27
  60.2 4.5 %collective-permute-done.7.refs_4_ = bf16[64,1152]{1,0:T(8,128)(2,1)S(1)} collective-permute-done((bf16[64,1152]{1,0:T(8,128)(2,1)S(1)}, bf16[64,1152]{1,0:T(8,128)(2,1)S(1)}, u32[]{:S(2)}, u32[]{:S(2)}) %collective-permute-start.7) | collective-permute-done | bytes 147488 | tf_op jit(solution)/shard_map/ppermute | solution.py:27
  65.4 8.7 %encode.1 = (bf16[64,2048]{1,0:T(8,128)(2,1)}, bf16[64,2048]{1,0:T(8,128)(2,1)}, bf16[64,2048]{1,0:T(8,128)(2,1)}, bf16[64,2048]{1,0:T(8,128)(2,1)}, bf16[64,204...) custom-call(s32[18]{0:T(128)} %pad_add_fusion.place_ref, ...), custom_call_target="tpu_custom_call" | custom-call | flops 2147483648 | bytes 7471104 | tf_op jit(solution)/shard_map/encode/pallas_call | solution.py:195
  74.1 4.8 %all-to-all-start.1 = ((f32[16,24,128]{2,1,0:T(8,128)}), f32[16,24,128]{2,1,0:T(8,128)S(1)}, u32[]{:S(2)}, u32[]{:S(2)}) async-start(f32[16,24,128]{2,1,0:T(8,128)} %get-tuple-element.11), calls=%async_computation.1 | async-start | bytes 393216 | tf_op jit(solution)/shard_map/all_to_all | solution.py:287
  80.9 3.0 %all-to-all-done.1 = f32[16,24,128]{2,1,0:T(8,128)S(1)} async-done(((f32[16,24,128]{2,1,0:T(8,128)}), f32[16,24,128]{2,1,0:T(8,128)S(1)}, u32[]{:S(2)}, u32[]{:S(2)}) %all-to-all-start.1) | async-done | bytes 196640 | tf_op jit(solution)/shard_map/all_to_all | solution.py:287
  85.2 2.7 %collective-permute-start.13 = (bf16[512,256]{1,0:T(8,128)(2,1)S(1)}, bf16[512,256]{1,0:T(8,128)(2,1)S(1)}, u32[]{:S(2)}, u32[]{:S(2)}) collective-permute-start(bf16[512,256]{1,0:T(8,128)(2,1)S(1)} %fusion.15), channel_id=1, source_target_pairs={{0,14},{1,15},{2,4},{3,5},{4,2},{5,3},{6,8},{7,9},{8,6},{9,7},{10,... | collective-permute-start | bytes 786440 | tf_op jit(solution)/shard_map/ppermute | solution.py:312
  90.3 7.4 %collective-permute-done.12 = bf16[512,256]{1,0:T(8,128)(2,1)S(1)} collective-permute-done((bf16[512,256]{1,0:T(8,128)(2,1)S(1)}, bf16[512,256]{1,0:T(8,128)(2,1)S(1)}, u32[]{:S(2)}, u32[]{:S(2)}) %collective-permute-start.12) | collective-permute-done | bytes 262176 | tf_op jit(solution)/shard_map/ppermute | solution.py:33
  103.0 2.4 %collective-permute-start.22 = (bf16[64,2048]{1,0:T(8,128)(2,1)S(1)}, bf16[64,2048]{1,0:T(8,128)(2,1)S(1)}, u32[]{:S(2)}, u32[]{:S(2)}) collective-permute-start(bf16[64,2048]{1,0:T(8,128)(2,1)S(1)} %add.176), channel_id=1, source_target_pairs={{0,224},{16,240},{32,128},{48,144},{64,160},{80,176},{96,192},{112... | collective-permute-start | bytes 786440 | tf_op jit(solution)/shard_map/ppermute | solution.py:45
  105.5 3.1 %collective-permute-done.14 = bf16[256,512]{1,0:T(8,128)(2,1)S(1)} collective-permute-done((bf16[256,512]{1,0:T(8,128)(2,1)S(1)}, bf16[256,512]{1,0:T(8,128)(2,1)S(1)}, u32[]{:S(2)}, u32[]{:S(2)}) %collective-permute-start.14) | collective-permute-done | bytes 262176 | tf_op jit(solution)/shard_map/ppermute | solution.py:37
  109.4 3.1 %collective-permute-done.18 = bf16[64,2048]{1,0:T(8,128)(2,1)S(1)} collective-permute-done((bf16[64,2048]{1,0:T(8,128)(2,1)S(1)}, bf16[64,2048]{1,0:T(8,128)(2,1)S(1)}, u32[]{:S(2)}, u32[]{:S(2)}) %collective-permute-start.18) | collective-permute-done | bytes 262176 | tf_op jit(solution)/shard_map/ppermute | solution.py:45
  113.5 5.5 %collective-permute-done.19 = bf16[64,2048]{1,0:T(8,128)(2,1)S(1)} collective-permute-done((bf16[64,2048]{1,0:T(8,128)(2,1)S(1)}, bf16[64,2048]{1,0:T(8,128)(2,1)S(1)}, u32[]{:S(2)}, u32[]{:S(2)}) %collective-permute-start.19) | collective-permute-done | bytes 262176 | tf_op jit(solution)/shard_map/ppermute | solution.py:45
  119.0 2.7 %collective-permute-start.16 = (bf16[64,512]{1,0:T(8,128)(2,1)S(1)}, bf16[64,512]{1,0:T(8,128)(2,1)S(1)}, u32[]{:S(2)}, u32[]{:S(2)}) collective-permute-start(bf16[64,512]{1,0:T(8,128)(2,1)S(1)} %get-tuple-element.24), channel_id=1, source_target_pairs={{0,8},{1,9},{2,10},{3,11},{4,12},{5,13},{6,14},{7,15},{8,0},{9,1},... | collective-permute-start | bytes 196616 | tf_op jit(solution)/shard_map/ppermute | solution.py:27
  124.5 2.6 %collective-permute-done.16 = bf16[64,512]{1,0:T(8,128)(2,1)S(1)} collective-permute-done((bf16[64,512]{1,0:T(8,128)(2,1)S(1)}, bf16[64,512]{1,0:T(8,128)(2,1)S(1)}, u32[]{:S(2)}, u32[]{:S(2)}) %collective-permute-start.16) | collective-permute-done | bytes 65568 | tf_op jit(solution)/shard_map/ppermute | solution.py:27
  (136 shorter events, 30.0 us)
Async XLA Ops:
  0.6 9.9 %collective-permute-start.1 = (bf16[256,8192]{1,0:T(8,128)(2,1)}, bf16[256,8192]{1,0:T(8,128)(2,1)}, u32[]{:S(2)}, u32[]{:S(2)}) collective-permute-start(bf16[256,8192]{1,0:T(8,128)(2,1)} %refs_1_.1), channel_id=1, source_target_pairs={{0,16},{16,0},{32,48},{48,32},{64,80},{80,64},{96,112},{112,96},{1... | collective-permute-start | bytes 12582920 | tf_op jit(solution)/shard_map/ppermute | solution.py:23
  9.7 45.4 %collective-permute-start.11 = (bf16[512,2048]{1,0:T(8,128)(2,1)S(1)}, bf16[512,2048]{1,0:T(8,128)(2,1)}, u32[]{:S(2)}, u32[]{:S(2)}) collective-permute-start(bf16[512,2048]{1,0:T(8,128)(2,1)S(1)} %copy-done.9), channel_id=1, source_target_pairs={{0,16},{16,0},{32,48},{48,32},{64,80},{80,64},{96,112},{112,96},{1... | collective-permute-start | bytes 6291464 | tf_op jit(solution)/shard_map/ppermute | solution.py:23
  15.6 14.5 %all-to-all-start = ((bf16[8,64,512]{2,1,0:T(8,128)(2,1)}), bf16[8,64,512]{2,1,0:T(8,128)(2,1)S(1)}, u32[]{:S(2)}, u32[]{:S(2)}) async-start(bf16[8,64,512]{2,1,0:T(8,128)(2,1)} %project.1), calls=%async_computation | async-start | bytes 1048576 | tf_op jit(solution)/shard_map/all_to_all | solution.py:254
  31.6 7.3 %collective-permute-start.3 = (bf16[64,1152]{1,0:T(8,128)(2,1)S(1)}, bf16[64,1152]{1,0:T(8,128)(2,1)S(1)}, u32[]{:S(2)}, u32[]{:S(2)}) collective-permute-start(bf16[64,1152]{1,0:T(8,128)(2,1)S(1)} %concatenate.23), channel_id=1, source_target_pairs={{0,1},{2,3},{4,5},{6,7},{8,9},{10,11},{12,13},{14,15},{17,16},{19,... | collective-permute-start | bytes 442376 | tf_op jit(solution)/shard_map/ppermute | solution.py:269
  39.0 13.5 %collective-permute-start.5 = (bf16[64,1152]{1,0:T(8,128)(2,1)S(1)}, bf16[64,1152]{1,0:T(8,128)(2,1)S(1)}, u32[]{:S(2)}, u32[]{:S(2)}) collective-permute-start(bf16[64,1152]{1,0:T(8,128)(2,1)S(1)} %broadcast_select_fusion.refs_0_), channel_id=1, source_target_pairs={{0,12},{1,13},{2,14},{3,15},{4,0},{5,1},{6,2},{7,3},{8,4},{9,5},{1... | collective-permute-start | bytes 442376 | tf_op jit(solution)/shard_map/ppermute | solution.py:27
  45.3 11.9 %collective-permute-start.8 = (bf16[64,1152]{1,0:T(8,128)(2,1)S(1)}, bf16[64,1152]{1,0:T(8,128)(2,1)S(1)}, u32[]{:S(2)}, u32[]{:S(2)}) collective-permute-start(bf16[64,1152]{1,0:T(8,128)(2,1)S(1)} %broadcast_select_fusion.refs_0_), channel_id=1, source_target_pairs={{0,4},{1,5},{2,6},{3,7},{4,8},{5,9},{6,10},{7,11},{8,12},{9,13},{1... | collective-permute-start | bytes 442376 | tf_op jit(solution)/shard_map/ppermute | solution.py:27
  45.9 14.0 %collective-permute-start.10 = (bf16[64,1152]{1,0:T(8,128)(2,1)S(1)}, bf16[64,1152]{1,0:T(8,128)(2,1)S(1)}, u32[]{:S(2)}, u32[]{:S(2)}) collective-permute-start(bf16[64,1152]{1,0:T(8,128)(2,1)S(1)} %broadcast_select_fusion.refs_0_), channel_id=1, source_target_pairs={{0,2},{1,3},{2,4},{3,5},{4,6},{5,7},{6,8},{7,9},{8,10},{9,11},{10,... | collective-permute-start | bytes 442376 | tf_op jit(solution)/shard_map/ppermute | solution.py:27
  47.0 13.0 %collective-permute-start.4 = (bf16[64,1152]{1,0:T(8,128)(2,1)S(1)}, bf16[64,1152]{1,0:T(8,128)(2,1)S(1)}, u32[]{:S(2)}, u32[]{:S(2)}) collective-permute-start(bf16[64,1152]{1,0:T(8,128)(2,1)S(1)} %broadcast_select_fusion.refs_0_), channel_id=1, source_target_pairs={{0,14},{1,15},{2,0},{3,1},{4,2},{5,3},{6,4},{7,5},{8,6},{9,7},{10,... | collective-permute-start | bytes 442376 | tf_op jit(solution)/shard_map/ppermute | solution.py:27
  52.4 7.7 %collective-permute-start.6 = (bf16[64,1152]{1,0:T(8,128)(2,1)S(1)}, bf16[64,1152]{1,0:T(8,128)(2,1)S(1)}, u32[]{:S(2)}, u32[]{:S(2)}) collective-permute-start(bf16[64,1152]{1,0:T(8,128)(2,1)S(1)} %collective-permute-done.5.refs_2_), channel_id=1, source_target_pairs={{0,14},{1,15},{2,0},{3,1},{4,2},{5,3},{6,4},{7,5},{8,6},{9,7},{10,... | collective-permute-start | bytes 442376 | tf_op jit(solution)/shard_map/ppermute | solution.py:27
  55.1 9.6 %collective-permute-start.7 = (bf16[64,1152]{1,0:T(8,128)(2,1)S(1)}, bf16[64,1152]{1,0:T(8,128)(2,1)S(1)}, u32[]{:S(2)}, u32[]{:S(2)}) collective-permute-start(bf16[64,1152]{1,0:T(8,128)(2,1)S(1)} %collective-permute-done.5.refs_2_), channel_id=1, source_target_pairs={{0,12},{1,13},{2,14},{3,15},{4,0},{5,1},{6,2},{7,3},{8,4},{9,5},{1... | collective-permute-start | bytes 442376 | tf_op jit(solution)/shard_map/ppermute | solution.py:27
  57.2 7.4 %collective-permute-start.9 = (bf16[64,1152]{1,0:T(8,128)(2,1)S(1)}, bf16[64,1152]{1,0:T(8,128)(2,1)S(1)}, u32[]{:S(2)}, u32[]{:S(2)}) collective-permute-start(bf16[64,1152]{1,0:T(8,128)(2,1)S(1)} %collective-permute-done.8.refs_6_), channel_id=1, source_target_pairs={{0,2},{1,3},{2,4},{3,5},{4,6},{5,7},{6,8},{7,9},{8,10},{9,11},{10,... | collective-permute-start | bytes 442376 | tf_op jit(solution)/shard_map/ppermute | solution.py:27
  74.1 9.8 %all-to-all-start.1 = ((f32[16,24,128]{2,1,0:T(8,128)}), f32[16,24,128]{2,1,0:T(8,128)S(1)}, u32[]{:S(2)}, u32[]{:S(2)}) async-start(f32[16,24,128]{2,1,0:T(8,128)} %get-tuple-element.11), calls=%async_computation.1 | async-start | bytes 393216 | tf_op jit(solution)/shard_map/all_to_all | solution.py:287
  78.9 22.7 %collective-permute-start.21 = (bf16[64,2048]{1,0:T(8,128)(2,1)}, bf16[64,2048]{1,0:T(8,128)(2,1)S(1)}, u32[]{:S(2)}, u32[]{:S(2)}) collective-permute-start(bf16[64,2048]{1,0:T(8,128)(2,1)} %get-tuple-element.17), channel_id=1, source_target_pairs={{0,96},{16,112},{32,0},{48,16},{64,32},{80,48},{96,64},{112,80},{1... | collective-permute-start | bytes 786440 | tf_op jit(solution)/shard_map/ppermute | solution.py:45
  79.3 23.7 %collective-permute-start.23 = (bf16[64,2048]{1,0:T(8,128)(2,1)}, bf16[64,2048]{1,0:T(8,128)(2,1)S(1)}, u32[]{:S(2)}, u32[]{:S(2)}) collective-permute-start(bf16[64,2048]{1,0:T(8,128)(2,1)} %get-tuple-element.19), channel_id=1, source_target_pairs={{0,32},{16,48},{32,64},{48,80},{64,96},{80,112},{96,0},{112,16},{1... | collective-permute-start | bytes 786440 | tf_op jit(solution)/shard_map/ppermute | solution.py:45
  85.2 12.6 %collective-permute-start.13 = (bf16[512,256]{1,0:T(8,128)(2,1)S(1)}, bf16[512,256]{1,0:T(8,128)(2,1)S(1)}, u32[]{:S(2)}, u32[]{:S(2)}) collective-permute-start(bf16[512,256]{1,0:T(8,128)(2,1)S(1)} %fusion.15), channel_id=1, source_target_pairs={{0,14},{1,15},{2,4},{3,5},{4,2},{5,3},{6,8},{7,9},{8,6},{9,7},{10,... | collective-permute-start | bytes 786440 | tf_op jit(solution)/shard_map/ppermute | solution.py:312
  88.9 8.8 %collective-permute-start.12 = (bf16[512,256]{1,0:T(8,128)(2,1)S(1)}, bf16[512,256]{1,0:T(8,128)(2,1)S(1)}, u32[]{:S(2)}, u32[]{:S(2)}) collective-permute-start(bf16[512,256]{1,0:T(8,128)(2,1)S(1)} %fusion.16), channel_id=1, source_target_pairs={{0,2},{1,3},{2,0},{3,1},{4,6},{5,7},{6,4},{7,5},{8,10},{9,11},{10,... | collective-permute-start | bytes 786440 | tf_op jit(solution)/shard_map/ppermute | solution.py:33
  97.8 10.8 %collective-permute-start.14 = (bf16[256,512]{1,0:T(8,128)(2,1)S(1)}, bf16[256,512]{1,0:T(8,128)(2,1)S(1)}, u32[]{:S(2)}, u32[]{:S(2)}) collective-permute-start(bf16[256,512]{1,0:T(8,128)(2,1)S(1)} %slice_add_fusion), channel_id=1, source_target_pairs={{0,1},{1,0},{2,3},{3,2},{4,5},{5,4},{6,7},{7,6},{8,9},{9,8},{10,11... | collective-permute-start | bytes 786440 | tf_op jit(solution)/shard_map/ppermute | solution.py:37
  99.4 13.0 %collective-permute-start.18 = (bf16[64,2048]{1,0:T(8,128)(2,1)S(1)}, bf16[64,2048]{1,0:T(8,128)(2,1)S(1)}, u32[]{:S(2)}, u32[]{:S(2)}) collective-permute-start(bf16[64,2048]{1,0:T(8,128)(2,1)S(1)} %copy-done.13), channel_id=1, source_target_pairs={{0,128},{16,144},{32,160},{48,176},{64,192},{80,208},{96,224},{112... | collective-permute-start | bytes 786440 | tf_op jit(solution)/shard_map/ppermute | solution.py:45
  99.7 19.2 %collective-permute-start.19 = (bf16[64,2048]{1,0:T(8,128)(2,1)S(1)}, bf16[64,2048]{1,0:T(8,128)(2,1)S(1)}, u32[]{:S(2)}, u32[]{:S(2)}) collective-permute-start(bf16[64,2048]{1,0:T(8,128)(2,1)S(1)} %copy-done.12), channel_id=1, source_target_pairs={{0,160},{16,176},{32,192},{48,208},{64,224},{80,240},{96,128},{112... | collective-permute-start | bytes 786440 | tf_op jit(solution)/shard_map/ppermute | solution.py:45
  101.6 20.0 %collective-permute-start.20 = (bf16[64,2048]{1,0:T(8,128)(2,1)S(1)}, bf16[64,2048]{1,0:T(8,128)(2,1)S(1)}, u32[]{:S(2)}, u32[]{:S(2)}) collective-permute-start(bf16[64,2048]{1,0:T(8,128)(2,1)S(1)} %copy-done.11), channel_id=1, source_target_pairs={{0,96},{16,112},{32,0},{48,16},{64,32},{80,48},{96,64},{112,80},{1... | collective-permute-start | bytes 786440 | tf_op jit(solution)/shard_map/ppermute | solution.py:45
  103.0 20.5 %collective-permute-start.22 = (bf16[64,2048]{1,0:T(8,128)(2,1)S(1)}, bf16[64,2048]{1,0:T(8,128)(2,1)S(1)}, u32[]{:S(2)}, u32[]{:S(2)}) collective-permute-start(bf16[64,2048]{1,0:T(8,128)(2,1)S(1)} %add.176), channel_id=1, source_target_pairs={{0,224},{16,240},{32,128},{48,144},{64,160},{80,176},{96,192},{112... | collective-permute-start | bytes 786440 | tf_op jit(solution)/shard_map/ppermute | solution.py:45
  108.6 15.0 %collective-permute-start.24 = (bf16[64,2048]{1,0:T(8,128)(2,1)S(1)}, bf16[64,2048]{1,0:T(8,128)(2,1)S(1)}, u32[]{:S(2)}, u32[]{:S(2)}) collective-permute-start(bf16[64,2048]{1,0:T(8,128)(2,1)S(1)} %add.178), channel_id=1, source_target_pairs={{0,32},{16,48},{32,64},{48,80},{64,96},{80,112},{96,0},{112,16},{1... | collective-permute-start | bytes 786440 | tf_op jit(solution)/shard_map/ppermute | solution.py:45
  112.5 12.0 %collective-permute-start.15 = (bf16[64,512]{1,0:T(8,128)(2,1)S(1)}, bf16[64,512]{1,0:T(8,128)(2,1)S(1)}, u32[]{:S(2)}, u32[]{:S(2)}) collective-permute-start(bf16[64,512]{1,0:T(8,128)(2,1)S(1)} %get-tuple-element.22), channel_id=1, source_target_pairs={{0,4},{1,5},{2,6},{3,7},{4,8},{5,9},{6,10},{7,11},{8,12},{9,13},{1... | collective-permute-start | bytes 196616 | tf_op jit(solution)/shard_map/ppermute | solution.py:27
  119.0 8.2 %collective-permute-start.16 = (bf16[64,512]{1,0:T(8,128)(2,1)S(1)}, bf16[64,512]{1,0:T(8,128)(2,1)S(1)}, u32[]{:S(2)}, u32[]{:S(2)}) collective-permute-start(bf16[64,512]{1,0:T(8,128)(2,1)S(1)} %get-tuple-element.24), channel_id=1, source_target_pairs={{0,8},{1,9},{2,10},{3,11},{4,12},{5,13},{6,14},{7,15},{8,0},{9,1},... | collective-permute-start | bytes 196616 | tf_op jit(solution)/shard_map/ppermute | solution.py:27
  (24 other events, 236.1 us)

commit v8 on v7

--- a/solution.py
+++ b/solution.py
@@ -55,8 +55,8 @@
     query_heads = queries.reshape(row_count, own_heads, HEAD_DIM)
     cache_keys = kv_cache[0, :, 0]
     cache_values = kv_cache[1, :, 0]
-    new_key = lax.dynamic_index_in_dim(new_kv[0], kv_index, 1, keepdims=False)
-    new_value = lax.dynamic_index_in_dim(new_kv[1], kv_index, 1, keepdims=False)
+    chosen = lax.dynamic_index_in_dim(new_kv, kv_index, 2, keepdims=False)
+    new_key, new_value = chosen[0], chosen[1]
     scores = (
         jnp.einsum("shd,spd->shp", query_heads, cache_keys, preferred_element_type=jnp.float32)
         * score_scale
@@ -191,7 +191,7 @@
     rows, depth = block[0].shape
     count = 8 * rows
     half, span = w_mine.shape
-    tile = 512
+    tile = 1024
     return pl.pallas_call(
         encode_kernel,
         grid_spec=pltpu.PrefetchScalarGridSpec(
@@ -326,9 +326,13 @@
     seven = outs[7] + relayed
     relayed = to_chip(outs[2], 0, 1)
     one = outs[1] + relayed
-    moved = []
-    for value, s in ((outs[4], 4), (outs[5], 5), (outs[3], 3), (seven, 7), (one, 1)):
-        moved.append(to_chip(value, s // 4, s % 4))
+    five = to_chip(outs[5], 0, 1)
+    seven = to_chip(seven, 0, 3)
+    three = to_chip(outs[3], 0, 3)
+    one = to_chip(one, 0, 1)
+    four = (outs[4].astype(f32) + five.astype(f32) + seven.astype(f32)).astype(bf16)
+    four = to_chip(four, 1, 0)
+    moved = [one, three, four]
 
     total = outs[0].astype(f32)
     for value in moved:

time: 131 us -> 124 us (0.947)
  waiting for transfers between devices: 45.4 us -> 38.2 us
    ppermute x7, waiting for transfers between devices: 8.62 us -> 2.03 us  [to_chip(): lax.ppermute(value, 'tp', tp_moves(lambda chip, core: chip_at(chip, dx, d...]
  transfers between devices with their start and end apart: 27 -> 27, of which waited for: 14 -> 14; matrix products, arithmetic and copies ran while one was open for 12% -> 13% of each run, Pallas kernels for 3% -> 4%
where the time goes in v8:
time: 124 us; the launch traced here: 122 us
  starting transfers between devices  52.5 us (42%)
  waiting for transfers between devices  38.2 us (31%)
  Pallas kernels  12.6 us (10%)
  matrix products  8.33 us (7%)
  other arithmetic  5.03 us (4%)
  local copies, waits for them, and re-layouts  4.12 us (3%)
    ppermute x10, starting transfers between devices, from_z(): lax.ppermute(value, 'grp', grp_moves(lambda z, plane: (z - ahead) % 8 * 2...  23.7 us
    ppermute x10, waiting for transfers between devices, from_z(): lax.ppermute(value, 'grp', grp_moves(lambda z, plane: (z - ahead) % 8 * 2...  11 us
    pallas_call x1, Pallas kernels, encode(): pl.pallas_call(encode_kernel, grid_spec=pltpu.PrefetchScalarGridSpec(num_...  8.21 us
    ppermute x7, starting transfers between devices, to_chip(): lax.ppermute(value, 'tp', tp_moves(lambda chip, core: chip_at(chip, dx, d...  7.99 us
    all_to_all x1, waiting for transfers between devices, per_device(): lax.all_to_all(part, 'tp', 0, 0, axis_index_groups=groups, tiled=True)  7.69 us
    ppermute x1, waiting for transfers between devices, flip_z(): lax.ppermute(value, 'grp', grp_moves(lambda z, plane: (z ^ k) * 2 + plane))  7.37 us
    all_to_all x1, starting transfers between devices, per_device(): lax.all_to_all(part, 'tp', 0, 0, axis_index_groups=groups, tiled=True)  5.97 us
    all_to_all x1, starting transfers between devices, per_device(): table = lax.all_to_all(outs[8], 'tp', 0, 0, tiled=True)  4.83 us
  transfers between devices with their start and end apart: 27, of which 14 were waited for; matrix products, arithmetic and copies ran while one was open for 13% of the time, Pallas kernels for 4%

profile of v8, /device:TPU:8, one launch (start us, length us, event | category | flops | bytes accessed | tf_op | source)
XLA Modules:
  0.0 121.9 jit_solution(2662417217776409565)
XLA Ops:
  3.4 2.9 %select_reduce_fusion = (f32[64,2]{1,0:T(8,128)S(1)}, f32[64,2,128]{2,1,0:T(2,128)S(1)}) fusion(pred[64,128]{1,0:T(8,128)(4,1)S(1)} %iota_compare_fusion.3, bf16[64,2,128]{2,1,0:T(2,128)(2,1)S(1)} %reshape.80, bf16[2,64,1,128,128]{4,3,1,2,0:T(8,128)(2,1)} %bitcast.71), kind=kOutput, calls=%fused_computation.42 | convolution fusion | flops 4243328 | bytes 2204160 | tf_op jit(solution)/shard_map/shd,spd->shp/dot_general | solution.py:61
  6.6 2.5 %fusion.20 = bf16[64,2,128]{2,1,0:T(2,128)(2,1)S(1)} fusion(bf16[2,64,1,128,128]{4,3,1,2,0:T(8,128)(2,1)} %bitcast.72, f32[64,2]{1,0:T(8,128)S(1)} %get-tuple-element.28, f32[64,128]{1,0:T(8,128)S(1)} %fusion.27, f32[64,2]{1,0:T(8,128)S(1)} %convert_element_type.131, f32[64,2,128]{2,1,0:T(2,128)S(1)} %get-tuple-element.37, ...), kind=kOutput, calls=%fused_computation.28 | convolution fusion | flops 4308992 | bytes 2237952 | tf_op jit(solution)/shard_map/shp,spd->shd/dot_general | solution.py:75
  11.2 4.4 %project.1 = bf16[8,64,512]{2,1,0:T(8,128)(2,1)} custom-call(s32[1]{0:T(128)} %bitcast.core_ref, bf16[64,256]{1,0:T(8,128)(2,1)} %bitcast.63, bf16[64,256]{1,0:T(8,128)(2,1)} %copy-done.7, bf16[256,8192]{1,0:T(8,128)(2,1)} %refs_1_.1, bf16[256,8192]{1,0:T(8,128)(2,1)} %refs_1_.1, bf16[256,8192]{1,0:T(8,128)(2,1)} %collective-permute-done.1.refs_2_.refs_3_, ...), custom_call_target="tpu_custom_call" | custom-call | flops 268435456 | bytes 4194304 | tf_op jit(solution)/shard_map/project/pallas_call | solution.py:105
  15.6 6.0 %all-to-all-start = ((bf16[8,64,512]{2,1,0:T(8,128)(2,1)}), bf16[8,64,512]{2,1,0:T(8,128)(2,1)S(1)}, u32[]{:S(2)}, u32[]{:S(2)}) async-start(bf16[8,64,512]{2,1,0:T(8,128)(2,1)} %project.1), calls=%async_computation | async-start | bytes 1048576 | tf_op jit(solution)/shard_map/all_to_all | solution.py:254
  22.4 7.7 %all-to-all-done = bf16[8,64,512]{2,1,0:T(8,128)(2,1)S(1)} async-done(((bf16[8,64,512]{2,1,0:T(8,128)(2,1)}), bf16[8,64,512]{2,1,0:T(8,128)(2,1)S(1)}, u32[]{:S(2)}, u32[]{:S(2)}) %all-to-all-start) | async-done | bytes 524320 | tf_op jit(solution)/shard_map/all_to_all | solution.py:254
  31.6 4.6 %collective-permute-start.3 = (bf16[64,1152]{1,0:T(8,128)(2,1)S(1)}, bf16[64,1152]{1,0:T(8,128)(2,1)S(1)}, u32[]{:S(2)}, u32[]{:S(2)}) collective-permute-start(bf16[64,1152]{1,0:T(8,128)(2,1)S(1)} %concatenate.23), channel_id=1, source_target_pairs={{0,1},{2,3},{4,5},{6,7},{8,9},{10,11},{12,13},{14,15},{17,16},{19,... | collective-permute-start | bytes 442376 | tf_op jit(solution)/shard_map/ppermute | solution.py:269
  36.3 2.6 %collective-permute-done.3 = bf16[64,1152]{1,0:T(8,128)(2,1)S(1)} collective-permute-done((bf16[64,1152]{1,0:T(8,128)(2,1)S(1)}, bf16[64,1152]{1,0:T(8,128)(2,1)S(1)}, u32[]{:S(2)}, u32[]{:S(2)}) %collective-permute-start.3) | collective-permute-done | bytes 147488 | tf_op jit(solution)/shard_map/ppermute | solution.py:269
  39.0 6.4 %collective-permute-start.5 = (bf16[64,1152]{1,0:T(8,128)(2,1)S(1)}, bf16[64,1152]{1,0:T(8,128)(2,1)S(1)}, u32[]{:S(2)}, u32[]{:S(2)}) collective-permute-start(bf16[64,1152]{1,0:T(8,128)(2,1)S(1)} %broadcast_select_fusion.refs_0_), channel_id=1, source_target_pairs={{0,12},{1,13},{2,14},{3,15},{4,0},{5,1},{6,2},{7,3},{8,4},{9,5},{1... | collective-permute-start | bytes 442376 | tf_op jit(solution)/shard_map/ppermute | solution.py:27
  47.0 2.7 %collective-permute-start.4 = (bf16[64,1152]{1,0:T(8,128)(2,1)S(1)}, bf16[64,1152]{1,0:T(8,128)(2,1)S(1)}, u32[]{:S(2)}, u32[]{:S(2)}) collective-permute-start(bf16[64,1152]{1,0:T(8,128)(2,1)S(1)} %broadcast_select_fusion.refs_0_), channel_id=1, source_target_pairs={{0,14},{1,15},{2,0},{3,1},{4,2},{5,3},{6,4},{7,5},{8,6},{9,7},{10,... | collective-permute-start | bytes 442376 | tf_op jit(solution)/shard_map/ppermute | solution.py:27
  49.6 2.8 %collective-permute-done.5.refs_2_ = bf16[64,1152]{1,0:T(8,128)(2,1)S(1)} collective-permute-done((bf16[64,1152]{1,0:T(8,128)(2,1)S(1)}, bf16[64,1152]{1,0:T(8,128)(2,1)S(1)}, u32[]{:S(2)}, u32[]{:S(2)}) %collective-permute-start.5) | collective-permute-done | bytes 147488 | tf_op jit(solution)/shard_map/ppermute | solution.py:27
  52.4 2.7 %collective-permute-start.6 = (bf16[64,1152]{1,0:T(8,128)(2,1)S(1)}, bf16[64,1152]{1,0:T(8,128)(2,1)S(1)}, u32[]{:S(2)}, u32[]{:S(2)}) collective-permute-start(bf16[64,1152]{1,0:T(8,128)(2,1)S(1)} %collective-permute-done.5.refs_2_), channel_id=1, source_target_pairs={{0,14},{1,15},{2,0},{3,1},{4,2},{5,3},{6,4},{7,5},{8,6},{9,7},{10,... | collective-permute-start | bytes 442376 | tf_op jit(solution)/shard_map/ppermute | solution.py:27
  55.1 2.1 %collective-permute-start.7 = (bf16[64,1152]{1,0:T(8,128)(2,1)S(1)}, bf16[64,1152]{1,0:T(8,128)(2,1)S(1)}, u32[]{:S(2)}, u32[]{:S(2)}) collective-permute-start(bf16[64,1152]{1,0:T(8,128)(2,1)S(1)} %collective-permute-done.5.refs_2_), channel_id=1, source_target_pairs={{0,12},{1,13},{2,14},{3,15},{4,0},{5,1},{6,2},{7,3},{8,4},{9,5},{1... | collective-permute-start | bytes 442376 | tf_op jit(solution)/shard_map/ppermute | solution.py:27
  57.3 1.9 %collective-permute-start.9 = (bf16[64,1152]{1,0:T(8,128)(2,1)S(1)}, bf16[64,1152]{1,0:T(8,128)(2,1)S(1)}, u32[]{:S(2)}, u32[]{:S(2)}) collective-permute-start(bf16[64,1152]{1,0:T(8,128)(2,1)S(1)} %collective-permute-done.8.refs_6_), channel_id=1, source_target_pairs={{0,2},{1,3},{2,4},{3,5},{4,6},{5,7},{6,8},{7,9},{8,10},{9,11},{10,... | collective-permute-start | bytes 442376 | tf_op jit(solution)/shard_map/ppermute | solution.py:27
  60.2 4.5 %collective-permute-done.7.refs_4_ = bf16[64,1152]{1,0:T(8,128)(2,1)S(1)} collective-permute-done((bf16[64,1152]{1,0:T(8,128)(2,1)S(1)}, bf16[64,1152]{1,0:T(8,128)(2,1)S(1)}, u32[]{:S(2)}, u32[]{:S(2)}) %collective-permute-start.7) | collective-permute-done | bytes 147488 | tf_op jit(solution)/shard_map/ppermute | solution.py:27
  65.4 8.2 %encode.1 = (bf16[64,2048]{1,0:T(8,128)(2,1)}, bf16[64,2048]{1,0:T(8,128)(2,1)}, bf16[64,2048]{1,0:T(8,128)(2,1)}, bf16[64,2048]{1,0:T(8,128)(2,1)}, bf16[64,204...) custom-call(s32[18]{0:T(128)} %pad_add_fusion.place_ref, ...), custom_call_target="tpu_custom_call" | custom-call | flops 2147483648 | bytes 7471104 | tf_op jit(solution)/shard_map/encode/pallas_call | solution.py:195
  73.6 4.8 %all-to-all-start.1 = ((f32[16,24,128]{2,1,0:T(8,128)}), f32[16,24,128]{2,1,0:T(8,128)S(1)}, u32[]{:S(2)}, u32[]{:S(2)}) async-start(f32[16,24,128]{2,1,0:T(8,128)} %get-tuple-element.11), calls=%async_computation.1 | async-start | bytes 393216 | tf_op jit(solution)/shard_map/all_to_all | solution.py:287
  80.5 2.9 %all-to-all-done.1 = f32[16,24,128]{2,1,0:T(8,128)S(1)} async-done(((f32[16,24,128]{2,1,0:T(8,128)}), f32[16,24,128]{2,1,0:T(8,128)S(1)}, u32[]{:S(2)}, u32[]{:S(2)}) %all-to-all-start.1) | async-done | bytes 196640 | tf_op jit(solution)/shard_map/all_to_all | solution.py:287
  84.7 2.7 %collective-permute-start.13 = (bf16[512,256]{1,0:T(8,128)(2,1)S(1)}, bf16[512,256]{1,0:T(8,128)(2,1)S(1)}, u32[]{:S(2)}, u32[]{:S(2)}) collective-permute-start(bf16[512,256]{1,0:T(8,128)(2,1)S(1)} %fusion.15), channel_id=1, source_target_pairs={{0,14},{1,15},{2,4},{3,5},{4,2},{5,3},{6,8},{7,9},{8,6},{9,7},{10,... | collective-permute-start | bytes 786440 | tf_op jit(solution)/shard_map/ppermute | solution.py:312
  89.9 7.4 %collective-permute-done.12 = bf16[512,256]{1,0:T(8,128)(2,1)S(1)} collective-permute-done((bf16[512,256]{1,0:T(8,128)(2,1)S(1)}, bf16[512,256]{1,0:T(8,128)(2,1)S(1)}, u32[]{:S(2)}, u32[]{:S(2)}) %collective-permute-start.12) | collective-permute-done | bytes 262176 | tf_op jit(solution)/shard_map/ppermute | solution.py:33
  101.9 2.1 %collective-permute-start.23 = (bf16[64,2048]{1,0:T(8,128)(2,1)S(1)}, bf16[64,2048]{1,0:T(8,128)(2,1)S(1)}, u32[]{:S(2)}, u32[]{:S(2)}) collective-permute-start(bf16[64,2048]{1,0:T(8,128)(2,1)S(1)} %add.176), channel_id=1, source_target_pairs={{0,96},{16,112},{32,0},{48,16},{64,32},{80,48},{96,64},{112,80},{1... | collective-permute-start | bytes 786440 | tf_op jit(solution)/shard_map/ppermute | solution.py:45
  104.1 2.8 %collective-permute-done.14 = bf16[256,512]{1,0:T(8,128)(2,1)S(1)} collective-permute-done((bf16[256,512]{1,0:T(8,128)(2,1)S(1)}, bf16[256,512]{1,0:T(8,128)(2,1)S(1)}, u32[]{:S(2)}, u32[]{:S(2)}) %collective-permute-start.14) | collective-permute-done | bytes 262176 | tf_op jit(solution)/shard_map/ppermute | solution.py:37
  108.2 3.6 %collective-permute-start.16 = (bf16[64,512]{1,0:T(8,128)(2,1)S(1)}, bf16[64,512]{1,0:T(8,128)(2,1)S(1)}, u32[]{:S(2)}, u32[]{:S(2)}) collective-permute-start(bf16[64,512]{1,0:T(8,128)(2,1)S(1)} %get-tuple-element.24), channel_id=1, source_target_pairs={{0,8},{1,9},{2,10},{3,11},{4,12},{5,13},{6,14},{7,15},{8,0},{9,1},... | collective-permute-start | bytes 196616 | tf_op jit(solution)/shard_map/ppermute | solution.py:27
  112.5 2.0 %collective-permute-start.17 = (bf16[64,512]{1,0:T(8,128)(2,1)S(1)}, bf16[64,512]{1,0:T(8,128)(2,1)S(1)}, u32[]{:S(2)}, u32[]{:S(2)}) collective-permute-start(bf16[64,512]{1,0:T(8,128)(2,1)S(1)} %get-tuple-element.23), channel_id=1, source_target_pairs={{0,12},{1,13},{2,14},{3,15},{4,0},{5,1},{6,2},{7,3},{8,4},{9,5},{1... | collective-permute-start | bytes 196616 | tf_op jit(solution)/shard_map/ppermute | solution.py:27
  117.2 1.8 %collective-permute-done.17 = bf16[64,512]{1,0:T(8,128)(2,1)S(1)} collective-permute-done((bf16[64,512]{1,0:T(8,128)(2,1)S(1)}, bf16[64,512]{1,0:T(8,128)(2,1)S(1)}, u32[]{:S(2)}, u32[]{:S(2)}) %collective-permute-start.17) | collective-permute-done | bytes 65568 | tf_op jit(solution)/shard_map/ppermute | solution.py:27
  (137 shorter events, 28.6 us)
Async XLA Ops:
  0.6 9.9 %collective-permute-start.1 = (bf16[256,8192]{1,0:T(8,128)(2,1)}, bf16[256,8192]{1,0:T(8,128)(2,1)}, u32[]{:S(2)}, u32[]{:S(2)}) collective-permute-start(bf16[256,8192]{1,0:T(8,128)(2,1)} %refs_1_.1), channel_id=1, source_target_pairs={{0,16},{16,0},{32,48},{48,32},{64,80},{80,64},{96,112},{112,96},{1... | collective-permute-start | bytes 12582920 | tf_op jit(solution)/shard_map/ppermute | solution.py:23
  9.7 45.5 %collective-permute-start.11 = (bf16[512,2048]{1,0:T(8,128)(2,1)S(1)}, bf16[512,2048]{1,0:T(8,128)(2,1)}, u32[]{:S(2)}, u32[]{:S(2)}) collective-permute-start(bf16[512,2048]{1,0:T(8,128)(2,1)S(1)} %copy-done.10), channel_id=1, source_target_pairs={{0,16},{16,0},{32,48},{48,32},{64,80},{80,64},{96,112},{112,96},{1... | collective-permute-start | bytes 6291464 | tf_op jit(solution)/shard_map/ppermute | solution.py:23
  15.6 14.5 %all-to-all-start = ((bf16[8,64,512]{2,1,0:T(8,128)(2,1)}), bf16[8,64,512]{2,1,0:T(8,128)(2,1)S(1)}, u32[]{:S(2)}, u32[]{:S(2)}) async-start(bf16[8,64,512]{2,1,0:T(8,128)(2,1)} %project.1), calls=%async_computation | async-start | bytes 1048576 | tf_op jit(solution)/shard_map/all_to_all | solution.py:254
  31.6 7.3 %collective-permute-start.3 = (bf16[64,1152]{1,0:T(8,128)(2,1)S(1)}, bf16[64,1152]{1,0:T(8,128)(2,1)S(1)}, u32[]{:S(2)}, u32[]{:S(2)}) collective-permute-start(bf16[64,1152]{1,0:T(8,128)(2,1)S(1)} %concatenate.23), channel_id=1, source_target_pairs={{0,1},{2,3},{4,5},{6,7},{8,9},{10,11},{12,13},{14,15},{17,16},{19,... | collective-permute-start | bytes 442376 | tf_op jit(solution)/shard_map/ppermute | solution.py:269
  39.0 13.5 %collective-permute-start.5 = (bf16[64,1152]{1,0:T(8,128)(2,1)S(1)}, bf16[64,1152]{1,0:T(8,128)(2,1)S(1)}, u32[]{:S(2)}, u32[]{:S(2)}) collective-permute-start(bf16[64,1152]{1,0:T(8,128)(2,1)S(1)} %broadcast_select_fusion.refs_0_), channel_id=1, source_target_pairs={{0,12},{1,13},{2,14},{3,15},{4,0},{5,1},{6,2},{7,3},{8,4},{9,5},{1... | collective-permute-start | bytes 442376 | tf_op jit(solution)/shard_map/ppermute | solution.py:27
  45.3 11.9 %collective-permute-start.8 = (bf16[64,1152]{1,0:T(8,128)(2,1)S(1)}, bf16[64,1152]{1,0:T(8,128)(2,1)S(1)}, u32[]{:S(2)}, u32[]{:S(2)}) collective-permute-start(bf16[64,1152]{1,0:T(8,128)(2,1)S(1)} %broadcast_select_fusion.refs_0_), channel_id=1, source_target_pairs={{0,4},{1,5},{2,6},{3,7},{4,8},{5,9},{6,10},{7,11},{8,12},{9,13},{1... | collective-permute-start | bytes 442376 | tf_op jit(solution)/shard_map/ppermute | solution.py:27
  45.9 14.0 %collective-permute-start.10 = (bf16[64,1152]{1,0:T(8,128)(2,1)S(1)}, bf16[64,1152]{1,0:T(8,128)(2,1)S(1)}, u32[]{:S(2)}, u32[]{:S(2)}) collective-permute-start(bf16[64,1152]{1,0:T(8,128)(2,1)S(1)} %broadcast_select_fusion.refs_0_), channel_id=1, source_target_pairs={{0,2},{1,3},{2,4},{3,5},{4,6},{5,7},{6,8},{7,9},{8,10},{9,11},{10,... | collective-permute-start | bytes 442376 | tf_op jit(solution)/shard_map/ppermute | solution.py:27
  47.0 13.0 %collective-permute-start.4 = (bf16[64,1152]{1,0:T(8,128)(2,1)S(1)}, bf16[64,1152]{1,0:T(8,128)(2,1)S(1)}, u32[]{:S(2)}, u32[]{:S(2)}) collective-permute-start(bf16[64,1152]{1,0:T(8,128)(2,1)S(1)} %broadcast_select_fusion.refs_0_), channel_id=1, source_target_pairs={{0,14},{1,15},{2,0},{3,1},{4,2},{5,3},{6,4},{7,5},{8,6},{9,7},{10,... | collective-permute-start | bytes 442376 | tf_op jit(solution)/shard_map/ppermute | solution.py:27
  52.4 7.7 %collective-permute-start.6 = (bf16[64,1152]{1,0:T(8,128)(2,1)S(1)}, bf16[64,1152]{1,0:T(8,128)(2,1)S(1)}, u32[]{:S(2)}, u32[]{:S(2)}) collective-permute-start(bf16[64,1152]{1,0:T(8,128)(2,1)S(1)} %collective-permute-done.5.refs_2_), channel_id=1, source_target_pairs={{0,14},{1,15},{2,0},{3,1},{4,2},{5,3},{6,4},{7,5},{8,6},{9,7},{10,... | collective-permute-start | bytes 442376 | tf_op jit(solution)/shard_map/ppermute | solution.py:27
  55.1 9.6 %collective-permute-start.7 = (bf16[64,1152]{1,0:T(8,128)(2,1)S(1)}, bf16[64,1152]{1,0:T(8,128)(2,1)S(1)}, u32[]{:S(2)}, u32[]{:S(2)}) collective-permute-start(bf16[64,1152]{1,0:T(8,128)(2,1)S(1)} %collective-permute-done.5.refs_2_), channel_id=1, source_target_pairs={{0,12},{1,13},{2,14},{3,15},{4,0},{5,1},{6,2},{7,3},{8,4},{9,5},{1... | collective-permute-start | bytes 442376 | tf_op jit(solution)/shard_map/ppermute | solution.py:27
  57.3 7.4 %collective-permute-start.9 = (bf16[64,1152]{1,0:T(8,128)(2,1)S(1)}, bf16[64,1152]{1,0:T(8,128)(2,1)S(1)}, u32[]{:S(2)}, u32[]{:S(2)}) collective-permute-start(bf16[64,1152]{1,0:T(8,128)(2,1)S(1)} %collective-permute-done.8.refs_6_), channel_id=1, source_target_pairs={{0,2},{1,3},{2,4},{3,5},{4,6},{5,7},{6,8},{7,9},{8,10},{9,11},{10,... | collective-permute-start | bytes 442376 | tf_op jit(solution)/shard_map/ppermute | solution.py:27
  73.6 9.8 %all-to-all-start.1 = ((f32[16,24,128]{2,1,0:T(8,128)}), f32[16,24,128]{2,1,0:T(8,128)S(1)}, u32[]{:S(2)}, u32[]{:S(2)}) async-start(f32[16,24,128]{2,1,0:T(8,128)} %get-tuple-element.11), calls=%async_computation.1 | async-start | bytes 393216 | tf_op jit(solution)/shard_map/all_to_all | solution.py:287
  78.5 22.5 %collective-permute-start.18 = (bf16[64,2048]{1,0:T(8,128)(2,1)}, bf16[64,2048]{1,0:T(8,128)(2,1)S(1)}, u32[]{:S(2)}, u32[]{:S(2)}) collective-permute-start(bf16[64,2048]{1,0:T(8,128)(2,1)} %get-tuple-element.14), channel_id=1, source_target_pairs={{0,32},{16,48},{32,64},{48,80},{64,96},{80,112},{96,0},{112,16},{1... | collective-permute-start | bytes 786440 | tf_op jit(solution)/shard_map/ppermute | solution.py:45
  79.9 21.9 %collective-permute-start.22 = (bf16[64,2048]{1,0:T(8,128)(2,1)}, bf16[64,2048]{1,0:T(8,128)(2,1)S(1)}, u32[]{:S(2)}, u32[]{:S(2)}) collective-permute-start(bf16[64,2048]{1,0:T(8,128)(2,1)} %get-tuple-element.19), channel_id=1, source_target_pairs={{0,96},{16,112},{32,0},{48,16},{64,32},{80,48},{96,64},{112,80},{1... | collective-permute-start | bytes 786440 | tf_op jit(solution)/shard_map/ppermute | solution.py:45
  84.7 12.6 %collective-permute-start.13 = (bf16[512,256]{1,0:T(8,128)(2,1)S(1)}, bf16[512,256]{1,0:T(8,128)(2,1)S(1)}, u32[]{:S(2)}, u32[]{:S(2)}) collective-permute-start(bf16[512,256]{1,0:T(8,128)(2,1)S(1)} %fusion.15), channel_id=1, source_target_pairs={{0,14},{1,15},{2,4},{3,5},{4,2},{5,3},{6,8},{7,9},{8,6},{9,7},{10,... | collective-permute-start | bytes 786440 | tf_op jit(solution)/shard_map/ppermute | solution.py:312
  88.5 8.8 %collective-permute-start.12 = (bf16[512,256]{1,0:T(8,128)(2,1)S(1)}, bf16[512,256]{1,0:T(8,128)(2,1)S(1)}, u32[]{:S(2)}, u32[]{:S(2)}) collective-permute-start(bf16[512,256]{1,0:T(8,128)(2,1)S(1)} %fusion.16), channel_id=1, source_target_pairs={{0,2},{1,3},{2,0},{3,1},{4,6},{5,7},{6,4},{7,5},{8,10},{9,11},{10,... | collective-permute-start | bytes 786440 | tf_op jit(solution)/shard_map/ppermute | solution.py:33
  97.4 9.5 %collective-permute-start.14 = (bf16[256,512]{1,0:T(8,128)(2,1)S(1)}, bf16[256,512]{1,0:T(8,128)(2,1)S(1)}, u32[]{:S(2)}, u32[]{:S(2)}) collective-permute-start(bf16[256,512]{1,0:T(8,128)(2,1)S(1)} %slice_add_fusion), channel_id=1, source_target_pairs={{0,1},{1,0},{2,3},{3,2},{4,5},{5,4},{6,7},{7,6},{8,9},{9,8},{10,11... | collective-permute-start | bytes 786440 | tf_op jit(solution)/shard_map/ppermute | solution.py:37
  99.0 9.2 %collective-permute-start.21 = (bf16[64,2048]{1,0:T(8,128)(2,1)S(1)}, bf16[64,2048]{1,0:T(8,128)(2,1)S(1)}, u32[]{:S(2)}, u32[]{:S(2)}) collective-permute-start(bf16[64,2048]{1,0:T(8,128)(2,1)S(1)} %copy-done.13), channel_id=1, source_target_pairs={{0,32},{16,48},{32,64},{48,80},{64,96},{80,112},{96,0},{112,16},{1... | collective-permute-start | bytes 786440 | tf_op jit(solution)/shard_map/ppermute | solution.py:45
  99.7 20.0 %collective-permute-start.20 = (bf16[64,2048]{1,0:T(8,128)(2,1)S(1)}, bf16[64,2048]{1,0:T(8,128)(2,1)S(1)}, u32[]{:S(2)}, u32[]{:S(2)}) collective-permute-start(bf16[64,2048]{1,0:T(8,128)(2,1)S(1)} %copy-done.12), channel_id=1, source_target_pairs={{0,96},{16,112},{32,0},{48,16},{64,32},{80,48},{96,64},{112,80},{1... | collective-permute-start | bytes 786440 | tf_op jit(solution)/shard_map/ppermute | solution.py:45
  101.1 18.6 %collective-permute-start.19 = (bf16[64,2048]{1,0:T(8,128)(2,1)S(1)}, bf16[64,2048]{1,0:T(8,128)(2,1)S(1)}, u32[]{:S(2)}, u32[]{:S(2)}) collective-permute-start(bf16[64,2048]{1,0:T(8,128)(2,1)S(1)} %add.172), channel_id=1, source_target_pairs={{0,32},{16,48},{32,64},{48,80},{64,96},{80,112},{96,0},{112,16},{1... | collective-permute-start | bytes 786440 | tf_op jit(solution)/shard_map/ppermute | solution.py:45
  101.9 10.5 %collective-permute-start.23 = (bf16[64,2048]{1,0:T(8,128)(2,1)S(1)}, bf16[64,2048]{1,0:T(8,128)(2,1)S(1)}, u32[]{:S(2)}, u32[]{:S(2)}) collective-permute-start(bf16[64,2048]{1,0:T(8,128)(2,1)S(1)} %add.176), channel_id=1, source_target_pairs={{0,96},{16,112},{32,0},{48,16},{64,32},{80,48},{96,64},{112,80},{1... | collective-permute-start | bytes 786440 | tf_op jit(solution)/shard_map/ppermute | solution.py:45
  106.9 7.7 %collective-permute-start.15 = (bf16[64,512]{1,0:T(8,128)(2,1)S(1)}, bf16[64,512]{1,0:T(8,128)(2,1)S(1)}, u32[]{:S(2)}, u32[]{:S(2)}) collective-permute-start(bf16[64,512]{1,0:T(8,128)(2,1)S(1)} %get-tuple-element.22), channel_id=1, source_target_pairs={{0,4},{1,5},{2,6},{3,7},{4,8},{5,9},{6,10},{7,11},{8,12},{9,13},{1... | collective-permute-start | bytes 196616 | tf_op jit(solution)/shard_map/ppermute | solution.py:27
  108.2 9.0 %collective-permute-start.16 = (bf16[64,512]{1,0:T(8,128)(2,1)S(1)}, bf16[64,512]{1,0:T(8,128)(2,1)S(1)}, u32[]{:S(2)}, u32[]{:S(2)}) collective-permute-start(bf16[64,512]{1,0:T(8,128)(2,1)S(1)} %get-tuple-element.24), channel_id=1, source_target_pairs={{0,8},{1,9},{2,10},{3,11},{4,12},{5,13},{6,14},{7,15},{8,0},{9,1},... | collective-permute-start | bytes 196616 | tf_op jit(solution)/shard_map/ppermute | solution.py:27
  112.5 6.5 %collective-permute-start.17 = (bf16[64,512]{1,0:T(8,128)(2,1)S(1)}, bf16[64,512]{1,0:T(8,128)(2,1)S(1)}, u32[]{:S(2)}, u32[]{:S(2)}) collective-permute-start(bf16[64,512]{1,0:T(8,128)(2,1)S(1)} %get-tuple-element.23), channel_id=1, source_target_pairs={{0,12},{1,13},{2,14},{3,15},{4,0},{5,1},{6,2},{7,3},{8,4},{9,5},{1... | collective-permute-start | bytes 196616 | tf_op jit(solution)/shard_map/ppermute | solution.py:27
  (24 other events, 230.1 us)
